TPU v7x, 32 devices: a whole 2x2x4 slice. The times are simulated.
32 devices in a mesh: seq: 4 (over z), fsdp: 8 (over y, x, core).
Axes of the slice: x: 2, y: 2, z: 4, core: 2. Of those that a mesh axis runs over, the one named last changes fastest.
Arguments:
- inputs: bfloat16 [8, 1024, 2048], P('fsdp', 'seq'), may hold values from -6 to 6
- norm1_gain: bfloat16 [2048], P(('seq', 'fsdp')), may hold values from 0.5 to 1.5
- w_query: bfloat16 [2048, 2048], P(('seq', 'fsdp')), may hold values from -0.125 to 0.125
- w_key: bfloat16 [2048, 2048], P(('seq', 'fsdp')), may hold values from -0.125 to 0.125
- w_value: bfloat16 [2048, 2048], P(('seq', 'fsdp')), may hold values from -0.125 to 0.125
- w_output: bfloat16 [2048, 2048], P(('seq', 'fsdp')), may hold values from -0.5 to 0.5
- norm2_gain: bfloat16 [2048], P(('seq', 'fsdp')), may hold values from 0.5 to 1.5
- w_gate: bfloat16 [2048, 8192], P(('seq', 'fsdp')), may hold values from -0.125 to 0.125
- w_up: bfloat16 [2048, 8192], P(('seq', 'fsdp')), may hold values from -0.125 to 0.125
- w_down: bfloat16 [8192, 2048], P(('seq', 'fsdp')), may hold values from -0.0625 to 0.0625
- out_grad: bfloat16 [8, 1024, 2048], P('fsdp', 'seq'), may hold values from -6 to 6
Outputs:
- output: bfloat16 [8, 1024, 2048], P('fsdp', 'seq')
- input_grad: float32 [8, 1024, 2048], P('fsdp', 'seq')
- norm1_gain_grad: float32 [2048], P(('seq', 'fsdp'))
- w_query_grad: float32 [2048, 2048], P(('seq', 'fsdp'))
- w_key_grad: float32 [2048, 2048], P(('seq', 'fsdp'))
- w_value_grad: float32 [2048, 2048], P(('seq', 'fsdp'))
- w_output_grad: float32 [2048, 2048], P(('seq', 'fsdp'))
- norm2_gain_grad: float32 [2048], P(('seq', 'fsdp'))
- w_gate_grad: float32 [2048, 8192], P(('seq', 'fsdp'))
- w_up_grad: float32 [2048, 8192], P(('seq', 'fsdp'))
- w_down_grad: float32 [8192, 2048], P(('seq', 'fsdp'))
All inputs are finite; a program needn't handle non-finite values.
Results may differ from a plain program's by a relative error of at most 0.014.
Values may be sent and summed in bfloat16 or wider, within the bound.
No kernel may reach another device: no remote copies, remote signals or barrier semaphores. Data moves between devices by JAX's collectives and lax.ppermute only.
A program may use at most 576 MiB of HBM per device.

v0:
```python
import math

import jax
import jax.numpy as jnp
from jax import lax
from jax.sharding import PartitionSpec as P

HEAD_DIM = 64
QBLK = 512


EPS = 1e-05
ROPE_BASE = 130000.0
NEG_FILL = -1e30


def tables(positions):
    half_dim = HEAD_DIM // 2
    freqs = jnp.exp(
        jnp.arange(half_dim, dtype=jnp.float32) * (-2.0 * math.log(ROPE_BASE) / HEAD_DIM)
    )
    angle = positions.astype(jnp.float32)[:, None] * freqs[None, :]
    angle = jnp.concatenate([angle, angle], axis=1)
    return (jnp.cos(angle), jnp.sin(angle))


def rotate_half(values):
    half_dim = values.shape[-1] // 2
    return jnp.concatenate([-values[..., half_dim:], values[..., :half_dim]], axis=-1)


def rotary(values, cosine, sine):
    seq_count, local_len, model_width = values.shape
    shaped = values.reshape(seq_count, local_len, model_width // HEAD_DIM, HEAD_DIM)
    turned = shaped * cosine[None, :, None, :] + rotate_half(shaped) * sine[None, :, None, :]
    return turned.reshape(seq_count, local_len, model_width)


def rotary_back(grads, cosine, sine):
    seq_count, local_len, model_width = grads.shape
    shaped = grads.reshape(seq_count, local_len, model_width // HEAD_DIM, HEAD_DIM)
    turned = shaped * cosine[None, :, None, :] - rotate_half(shaped * sine[None, :, None, :])
    return turned.reshape(seq_count, local_len, model_width)


def matmul(left, right):
    return jnp.dot(left, right, preferred_element_type=jnp.float32)


def outer_sum(left, right):
    return lax.dot_general(
        left, right, (((0,), (0,)), ((), ())), preferred_element_type=jnp.float32
    )


def times_transposed(left, right):
    return lax.dot_general(
        left, right, (((1,), (1,)), ((), ())), preferred_element_type=jnp.float32
    )


def normalize(values, gain):
    inverse = lax.rsqrt(jnp.mean(values * values, axis=1, keepdims=True) + EPS)
    return ((values * inverse * gain).astype(jnp.bfloat16), inverse)


def norm_back(grad_normed, values, inverse, gain):
    scaled = grad_normed * gain
    gain_term = jnp.sum(grad_normed * values * inverse, axis=0)
    value_grad = inverse * (
        scaled - values * inverse * inverse * jnp.mean(scaled * values, axis=1, keepdims=True)
    )
    return (gain_term, value_grad)


def causal_block(query_block, key_heads, block_start):
    score_scale = HEAD_DIM ** (-0.5)
    scores = (
        jnp.einsum("sqhd,skhd->shqk", query_block, key_heads, preferred_element_type=jnp.float32)
        * score_scale
    )
    query_pos = block_start + jnp.arange(query_block.shape[1])
    allowed = jnp.arange(key_heads.shape[1])[None, :] <= query_pos[:, None]
    return jnp.where(allowed, scores, NEG_FILL)


def local(
    inputs,
    norm1_gain,
    w_query,
    w_key,
    w_value,
    w_output,
    norm2_gain,
    w_gate,
    w_up,
    w_down,
    out_grad,
):
    seq_count, local_len, model_width = inputs.shape
    row_count = seq_count * local_len
    score_scale = HEAD_DIM ** (-0.5)
    residual_in = inputs.reshape(row_count, model_width).astype(jnp.float32)
    attn_set = (
        lax.all_gather(norm1_gain, ("seq", "fsdp"), axis=0, tiled=True),
        lax.all_gather(w_query, ("seq", "fsdp"), axis=0, tiled=True),
        lax.all_gather(w_key, ("seq", "fsdp"), axis=0, tiled=True),
        lax.all_gather(w_value, ("seq", "fsdp"), axis=0, tiled=True),
        lax.all_gather(w_output, ("seq", "fsdp"), axis=0, tiled=True),
    )
    gain_one, query_w, key_w, value_w, output_w = attn_set
    normed_one, inverse_one = normalize(residual_in, gain_one.astype(jnp.float32))
    positions = lax.axis_index("seq") * local_len + jnp.arange(local_len, dtype=jnp.int32)
    cosine, sine = tables(positions)
    query_rot = rotary(
        matmul(normed_one, query_w).reshape(seq_count, local_len, model_width), cosine, sine
    ).astype(jnp.bfloat16)
    key_rot = rotary(
        matmul(normed_one, key_w).reshape(seq_count, local_len, model_width), cosine, sine
    ).astype(jnp.bfloat16)
    value_tok = (
        matmul(normed_one, value_w).astype(jnp.bfloat16).reshape(seq_count, local_len, model_width)
    )
    query_h, key_h, value_h = (
        lax.all_to_all(query_rot, "seq", split_axis=2, concat_axis=1, tiled=True),
        lax.all_to_all(key_rot, "seq", split_axis=2, concat_axis=1, tiled=True),
        lax.all_to_all(value_tok, "seq", split_axis=2, concat_axis=1, tiled=True),
    )
    full_len = query_h.shape[1]
    head_width = query_h.shape[2]
    heads_here = head_width // HEAD_DIM
    query_heads = query_h.reshape(seq_count, full_len, heads_here, HEAD_DIM)
    key_heads = key_h.reshape(seq_count, full_len, heads_here, HEAD_DIM)
    value_heads = value_h.reshape(seq_count, full_len, heads_here, HEAD_DIM)
    block_outs = []
    block_lse = []
    for block_start in range(0, full_len, QBLK):
        block_end = block_start + QBLK
        query_block = query_heads[:, block_start:block_end]
        scores = causal_block(query_block, key_heads[:, :block_end], block_start)
        row_max = jnp.max(scores, axis=-1, keepdims=True)
        shifted = jnp.exp(scores - row_max)
        row_sum = jnp.sum(shifted, axis=-1, keepdims=True)
        attn_prob = (shifted / row_sum).astype(jnp.bfloat16)
        block_outs.append(
            jnp.einsum(
                "shqk,skhd->sqhd",
                attn_prob,
                value_heads[:, :block_end],
                preferred_element_type=jnp.float32,
            )
        )
        block_lse.append(row_max + jnp.log(row_sum))
    attended = (
        jnp.concatenate(block_outs, axis=1)
        .astype(jnp.bfloat16)
        .reshape(seq_count, full_len, head_width)
    )
    attended_tok = lax.all_to_all(attended, "seq", split_axis=1, concat_axis=2, tiled=True).reshape(
        row_count, model_width
    )
    mid_stream = residual_in + matmul(attended_tok, output_w)
    gain_two, gate_w, up_w, down_w = (
        lax.all_gather(norm2_gain, ("seq", "fsdp"), axis=0, tiled=True),
        lax.all_gather(w_gate, ("seq", "fsdp"), axis=0, tiled=True),
        lax.all_gather(w_up, ("seq", "fsdp"), axis=0, tiled=True),
        lax.all_gather(w_down, ("seq", "fsdp"), axis=0, tiled=True),
    )
    normed_two, inverse_two = normalize(mid_stream, gain_two.astype(jnp.float32))
    gate_pre = matmul(normed_two, gate_w)
    up_pre = matmul(normed_two, up_w)
    gate_sig = jax.nn.sigmoid(gate_pre)
    hidden = (gate_pre * gate_sig * up_pre).astype(jnp.bfloat16)
    output = (
        (mid_stream + matmul(hidden, down_w))
        .astype(jnp.bfloat16)
        .reshape(seq_count, local_len, model_width)
    )
    grad_out = out_grad.reshape(row_count, model_width).astype(jnp.float32)
    grad_outb = grad_out.astype(jnp.bfloat16)
    down_grad = lax.psum_scatter(
        outer_sum(hidden, grad_outb), ("seq", "fsdp"), scatter_dimension=0, tiled=True
    )
    gain_two, gate_w, up_w, down_w = (
        lax.all_gather(norm2_gain, ("seq", "fsdp"), axis=0, tiled=True),
        lax.all_gather(w_gate, ("seq", "fsdp"), axis=0, tiled=True),
        lax.all_gather(w_up, ("seq", "fsdp"), axis=0, tiled=True),
        lax.all_gather(w_down, ("seq", "fsdp"), axis=0, tiled=True),
    )
    grad_hidden = times_transposed(grad_outb, down_w)
    grad_gate = (grad_hidden * up_pre * gate_sig * (1.0 + gate_pre * (1.0 - gate_sig))).astype(
        jnp.bfloat16
    )
    grad_up = (grad_hidden * gate_pre * gate_sig).astype(jnp.bfloat16)
    grad_normed_two = times_transposed(grad_gate, gate_w) + times_transposed(grad_up, up_w)
    gain_two_term, grad_mid = norm_back(
        grad_normed_two, mid_stream, inverse_two, gain_two.astype(jnp.float32)
    )
    grad_mid = grad_out + grad_mid
    gate_grad, gain_two_grad = (
        lax.psum_scatter(
            outer_sum(normed_two, grad_gate), ("seq", "fsdp"), scatter_dimension=0, tiled=True
        ),
        lax.psum_scatter(gain_two_term, ("seq", "fsdp"), scatter_dimension=0, tiled=True),
    )
    up_grad = lax.psum_scatter(
        outer_sum(normed_two, grad_up), ("seq", "fsdp"), scatter_dimension=0, tiled=True
    )
    gain_one, query_w, key_w, value_w, output_w = (
        lax.all_gather(norm1_gain, ("seq", "fsdp"), axis=0, tiled=True),
        lax.all_gather(w_query, ("seq", "fsdp"), axis=0, tiled=True),
        lax.all_gather(w_key, ("seq", "fsdp"), axis=0, tiled=True),
        lax.all_gather(w_value, ("seq", "fsdp"), axis=0, tiled=True),
        lax.all_gather(w_output, ("seq", "fsdp"), axis=0, tiled=True),
    )
    grad_proj = grad_mid.astype(jnp.bfloat16)
    output_term = outer_sum(attended_tok, grad_proj)
    grad_att = (
        times_transposed(grad_proj, output_w)
        .astype(jnp.bfloat16)
        .reshape(seq_count, local_len, model_width)
    )
    grad_att_h = lax.all_to_all(grad_att, "seq", split_axis=2, concat_axis=1, tiled=True)
    grad_heads = grad_att_h.reshape(seq_count, full_len, heads_here, HEAD_DIM)
    grad_key_sum = jnp.zeros(key_heads.shape, jnp.float32)
    grad_value_sum = jnp.zeros(value_heads.shape, jnp.float32)
    query_parts = []
    for block_index, block_start in enumerate(range(0, full_len, QBLK)):
        block_end = block_start + QBLK
        query_block = query_heads[:, block_start:block_end]
        grad_block = grad_heads[:, block_start:block_end]
        key_part = key_heads[:, :block_end]
        value_part = value_heads[:, :block_end]
        scores = causal_block(query_block, key_part, block_start)
        attn_prob = jnp.exp(scores - block_lse[block_index])
        grad_prob = jnp.einsum(
            "sqhd,skhd->shqk", grad_block, value_part, preferred_element_type=jnp.float32
        )
        row_dot = jnp.sum(attn_prob * grad_prob, axis=-1, keepdims=True)
        grad_score = (attn_prob * (grad_prob - row_dot)).astype(jnp.bfloat16)
        query_parts.append(
            jnp.einsum("shqk,skhd->sqhd", grad_score, key_part, preferred_element_type=jnp.float32)
            * score_scale
        )
        grad_key_sum = grad_key_sum.at[:, :block_end].add(
            jnp.einsum(
                "shqk,sqhd->skhd", grad_score, query_block, preferred_element_type=jnp.float32
            )
            * score_scale
        )
        grad_value_sum = grad_value_sum.at[:, :block_end].add(
            jnp.einsum(
                "shqk,sqhd->skhd",
                attn_prob.astype(jnp.bfloat16),
                grad_block,
                preferred_element_type=jnp.float32,
            )
        )
    grad_query_h = (
        jnp.concatenate(query_parts, axis=1)
        .astype(jnp.bfloat16)
        .reshape(seq_count, full_len, head_width)
    )
    grad_key_h = grad_key_sum.astype(jnp.bfloat16).reshape(seq_count, full_len, head_width)
    grad_value_h = grad_value_sum.astype(jnp.bfloat16).reshape(seq_count, full_len, head_width)
    grad_query_t, grad_key_t, grad_value_t = (
        lax.all_to_all(grad_query_h, "seq", split_axis=1, concat_axis=2, tiled=True),
        lax.all_to_all(grad_key_h, "seq", split_axis=1, concat_axis=2, tiled=True),
        lax.all_to_all(grad_value_h, "seq", split_axis=1, concat_axis=2, tiled=True),
    )
    grad_query = (
        rotary_back(grad_query_t.astype(jnp.float32), cosine, sine)
        .astype(jnp.bfloat16)
        .reshape(row_count, model_width)
    )
    grad_key = (
        rotary_back(grad_key_t.astype(jnp.float32), cosine, sine)
        .astype(jnp.bfloat16)
        .reshape(row_count, model_width)
    )
    grad_value = grad_value_t.reshape(row_count, model_width)
    grad_normed_one = (
        times_transposed(grad_query, query_w)
        + times_transposed(grad_key, key_w)
        + times_transposed(grad_value, value_w)
    )
    gain_one_term, grad_in = norm_back(
        grad_normed_one, residual_in, inverse_one, gain_one.astype(jnp.float32)
    )
    input_grad = (grad_mid + grad_in).reshape(seq_count, local_len, model_width)
    query_grad, key_grad, value_grad, output_grad, gain_one_grad = (
        lax.psum_scatter(
            outer_sum(normed_one, grad_query), ("seq", "fsdp"), scatter_dimension=0, tiled=True
        ),
        lax.psum_scatter(
            outer_sum(normed_one, grad_key), ("seq", "fsdp"), scatter_dimension=0, tiled=True
        ),
        lax.psum_scatter(
            outer_sum(normed_one, grad_value), ("seq", "fsdp"), scatter_dimension=0, tiled=True
        ),
        lax.psum_scatter(output_term, ("seq", "fsdp"), scatter_dimension=0, tiled=True),
        lax.psum_scatter(gain_one_term, ("seq", "fsdp"), scatter_dimension=0, tiled=True),
    )
    return (
        output,
        input_grad,
        gain_one_grad,
        query_grad,
        key_grad,
        value_grad,
        output_grad,
        gain_two_grad,
        gate_grad,
        up_grad,
        down_grad,
    )


def solution(mesh):
    in_specs = (
        P("fsdp", "seq", None),
        P(("seq", "fsdp")),
        P(("seq", "fsdp"), None),
        P(("seq", "fsdp"), None),
        P(("seq", "fsdp"), None),
        P(("seq", "fsdp"), None),
        P(("seq", "fsdp")),
        P(("seq", "fsdp"), None),
        P(("seq", "fsdp"), None),
        P(("seq", "fsdp"), None),
        P("fsdp", "seq", None),
    )
    out_specs = (
        P("fsdp", "seq", None),
        P("fsdp", "seq", None),
        P(("seq", "fsdp")),
        P(("seq", "fsdp"), None),
        P(("seq", "fsdp"), None),
        P(("seq", "fsdp"), None),
        P(("seq", "fsdp"), None),
        P(("seq", "fsdp")),
        P(("seq", "fsdp"), None),
        P(("seq", "fsdp"), None),
        P(("seq", "fsdp"), None),
    )
    return jax.shard_map(local, mesh=mesh, in_specs=in_specs, out_specs=out_specs, check_vma=False)
```

profile of v0, /device:TPU:5, one launch (start us, length us, event | category | flops | bytes accessed | tf_op | source)
XLA Modules:
  0.0 3974.3 jit_solution(12633569938991020945)
XLA Ops:
  12.4 40.4 %all-reduce.7 = (bf16[2048]{0:T(1024)(128)(2,1)S(1)}, bf16[2048]{0:T(1024)(128)(2,1)S(1)}) all-reduce(bf16[2048]{0:T(1024)(128)(2,1)S(1)} %dynamic-update-slice.10, bf16[2048]{0:T(1024)(128)(2,1)S(1)} %dynamic-update-slice.11), channel_id=1, replica_groups=mesh['seq'=4,'fsdp'=8] {'seq','fsdp'}, use_global_device_ids=true, to_apply=%add.2 | all-reduce | flops 4096 | bytes 16384
  60.7 29.6 all-gather.8.cloned.1.call-done
  100.3 11.7 reduce.20
  118.1 66.8 %all-gather.12.cloned.1.call-done = bf16[2048,2048]{1,0:T(8,128)(2,1)} async-done(((bf16[64,2048]{1,0:T(8,128)(2,1)}), bf16[2048,2048]{1,0:T(8,128)(2,1)}) %all-gather.12.cloned.1.call-update) | async-done | bytes 8388624 | tf_op jit(solution)/shard_map/all_gather | solution.py:107
  194.8 69.0 %all-gather.10.cloned.1.call-done = bf16[2048,2048]{1,0:T(8,128)(2,1)} async-done(((bf16[64,2048]{1,0:T(8,128)(2,1)}), bf16[2048,2048]{1,0:T(8,128)(2,1)}) %all-gather.10.cloned.1.call-update) | async-done | bytes 8388624 | tf_op jit(solution)/shard_map/all_gather | solution.py:106
  294.7 11.6 reduce.21
  315.3 11.6 reduce.22
  328.6 31.1 all-to-all-done.2
  382.5 21.8 all-to-all-done.1
  461.4 43.3 %all-to-all-done.3 = bf16[4,2,65536]{2,1,0:T(2,128)(2,1)S(1)} async-done(((bf16[4,2,65536]{2,1,0:T(2,128)(2,1)}), bf16[4,2,65536]{2,1,0:T(2,128)(2,1)S(1)}, u32[]{:S(2)}, u32[]{:S(2)}) %all-to-all-start.3) | async-done | bytes 1048608 | tf_op jit(solution)/shard_map/all_to_all | solution.py:159
  517.0 67.5 %all-gather.18.cloned.1.call-done = bf16[2048,8192]{1,0:T(8,128)(2,1)} async-done(((bf16[64,8192]{1,0:T(8,128)(2,1)}), bf16[2048,8192]{1,0:T(8,128)(2,1)}) %all-gather.18.cloned.1.call-update) | async-done | bytes 33554448 | tf_op jit(solution)/shard_map/all_gather | solution.py:166
  584.5 17.9 fusion.79
  602.4 177.7 %all-gather.16.cloned.1.call-done = bf16[2048,8192]{1,0:T(8,128)(2,1)} async-done(((bf16[64,8192]{1,0:T(8,128)(2,1)}), bf16[2048,8192]{1,0:T(8,128)(2,1)}) %all-gather.16.cloned.1.call-update) | async-done | bytes 33554448 | tf_op jit(solution)/shard_map/all_gather | solution.py:165
  780.1 17.8 fusion.78
  797.9 178.1 %all-gather.20.cloned.1.call-done = bf16[8192,2048]{1,0:T(8,128)(2,1)} async-done(((bf16[256,2048]{1,0:T(8,128)(2,1)}), bf16[8192,2048]{1,0:T(8,128)(2,1)}) %all-gather.20.cloned.1.call-update) | async-done | bytes 33554448 | tf_op jit(solution)/shard_map/all_gather | solution.py:167
  976.0 24.4 multiply_convert_fusion.2
  1000.4 17.0 fusion.80
  1017.4 16.9 multiply_reduce_fusion.2
  1054.6 11.6 reduce.24
  1071.5 25.6 all-to-all-done.4
  1129.5 29.1 all_to_all.108
  1269.8 14.4 all-to-all-done.6
  1318.9 26.0 fusion.52
  1346.2 26.2 fusion.83
  1372.4 26.1 fusion.82
  1400.2 17.8 fusion.22
  1436.7 102.1 %all-reduce.6 = (f32[2048]{0:T(1024)S(1)}, f32[2048]{0:T(1024)S(1)}) all-reduce(f32[2048]{0:T(1024)S(1)} %get-tuple-element.77, f32[2048]{0:T(1024)S(1)} %copy-done.48), channel_id=2, replica_groups=mesh['seq'=4,'fsdp'=8] {'seq','fsdp'}, use_global_device_ids=true, to_apply=%region_11.12.clone | all-reduce | flops 4096 | bytes 32768
  1543.6 100.3 %reduce-scatter.8.cloned.1.call-done = f32[64,2048]{1,0:T(8,128)} async-done(((f32[2048,2048]{1,0:T(8,128)}), f32[64,2048]{1,0:T(8,128)}) %reduce-scatter.8.cloned.1.call-update) | async-done | bytes 524304 | tf_op jit(solution)/shard_map/reduce_scatter | solution.py:292
  1643.9 187.4 %reduce-scatter.10.cloned.1.call-done = f32[64,2048]{1,0:T(8,128)} async-done(((f32[2048,2048]{1,0:T(8,128)}), f32[64,2048]{1,0:T(8,128)}) %reduce-scatter.10.cloned.1.call-update) | async-done | bytes 524304 | tf_op jit(solution)/shard_map/reduce_scatter | solution.py:295
  1831.3 710.0 %reduce-scatter.20.cloned.1.call-done = f32[256,2048]{1,0:T(8,128)} async-done(((f32[8192,2048]{1,0:T(8,128)}), f32[256,2048]{1,0:T(8,128)}) %reduce-scatter.20.cloned.1.call-update) | async-done | bytes 2097168 | tf_op jit(solution)/shard_map/reduce_scatter | solution.py:181
  2541.3 713.2 %reduce-scatter.18.cloned.1.call-done = f32[64,8192]{1,0:T(8,128)} async-done(((f32[2048,8192]{1,0:T(8,128)}), f32[64,8192]{1,0:T(8,128)}) %reduce-scatter.18.cloned.1.call-update) | async-done | bytes 2097168 | tf_op jit(solution)/shard_map/reduce_scatter | solution.py:206
  3254.5 713.1 %reduce-scatter.16.cloned.1.call-done = f32[64,8192]{1,0:T(8,128)} async-done(((f32[2048,8192]{1,0:T(8,128)}), f32[64,8192]{1,0:T(8,128)}) %reduce-scatter.16.cloned.1.call-update) | async-done | bytes 2097168 | tf_op jit(solution)/shard_map/reduce_scatter | solution.py:201
  (279 shorter events, 401.9 us)
Async XLA Ops:
  7.2 83.1 %all-gather.8.cloned.1.call-start = ((), (), s32[]{:S(2)}) async-start(), calls=%async_computation.15 | async-start | bytes 8650752 | tf_op jit(solution)/shard_map/all_gather | solution.py:108
  7.9 176.9 %all-gather.12.cloned.1.call-start = ((), (), s32[]{:S(2)}) async-start(), calls=%async_computation.17 | async-start | bytes 8650752 | tf_op jit(solution)/shard_map/all_gather | solution.py:107
  8.7 255.1 %all-gather.10.cloned.1.call-start = ((), (), s32[]{:S(2)}) async-start(), calls=%async_computation.16 | async-start | bytes 8650752 | tf_op jit(solution)/shard_map/all_gather | solution.py:106
  9.4 500.2 %all-gather.14.cloned.1.call-start = ((), (), s32[]{:S(2)}) async-start(), calls=%async_computation.18 | async-start | bytes 8650752 | tf_op jit(solution)/shard_map/all_gather | solution.py:109
  10.0 574.5 %all-gather.18.cloned.1.call-start = ((), (), s32[]{:S(2)}) async-start(), calls=%async_computation.20 | async-start | bytes 34603008 | tf_op jit(solution)/shard_map/all_gather | solution.py:166
  10.6 769.5 %all-gather.16.cloned.1.call-start = ((), (), s32[]{:S(2)}) async-start(), calls=%async_computation.19 | async-start | bytes 34603008 | tf_op jit(solution)/shard_map/all_gather | solution.py:165
  11.2 964.8 %all-gather.20.cloned.1.call-start = ((), (), s32[]{:S(2)}) async-start(), calls=%async_computation.21 | async-start | bytes 34603008 | tf_op jit(solution)/shard_map/all_gather | solution.py:167
  52.9 210.9 %copy-start.38 = (f32[2048]{0:T(1024)}, f32[2048]{0:T(1024)S(1)}, u32[]{:S(2)}) copy-start(f32[2048]{0:T(1024)S(1)} %convert_element_type.262) | copy-start | bytes 24580
  60.7 203.1 %copy-start.43 = (f32[256]{0:T(256)}, f32[256]{0:T(256)S(1)}, u32[]{:S(2)}) copy-start(f32[256]{0:T(256)S(1)} %add_rsqrt_fusion.1) | copy-start | bytes 3076
  113.6 194.4 %all-to-all-start = ((bf16[4,2,65536]{2,1,0:T(2,128)(2,1)}), bf16[4,2,65536]{2,1,0:T(2,128)(2,1)}, u32[]{:S(2)}, u32[]{:S(2)}) async-start(bf16[4,2,65536]{2,1,0:T(2,128)(2,1)} %reshape.873), calls=%async_computation | async-start | bytes 2097152 | tf_op jit(solution)/shard_map/all_to_all | solution.py:127
  308.0 51.7 %all-to-all-start.2 = ((bf16[4,2,65536]{2,1,0:T(2,128)(2,1)}), bf16[4,2,65536]{2,1,0:T(2,128)(2,1)S(1)}, u32[]{:S(2)}, u32[]{:S(2)}) async-start(bf16[4,2,65536]{2,1,0:T(2,128)(2,1)} %reshape.875), calls=%async_computation.2 | async-start | bytes 2097152 | tf_op jit(solution)/shard_map/all_to_all | solution.py:126
  359.7 44.6 %all-to-all-start.1 = ((bf16[4,2,65536]{2,1,0:T(2,128)(2,1)}), bf16[4,2,65536]{2,1,0:T(2,128)(2,1)}, u32[]{:S(2)}, u32[]{:S(2)}) async-start(bf16[4,2,65536]{2,1,0:T(2,128)(2,1)} %reshape.877), calls=%async_computation.1 | async-start | bytes 2097152 | tf_op jit(solution)/shard_map/all_to_all | solution.py:125
  380.9 45.4 %copy-start.19 = (bf16[1024,8,64]{0,2,1:T(8,128)(2,1)}, bf16[1024,8,64]{0,2,1:T(8,128)(2,1)S(1)}, u32[]{:S(2)}) copy-start(bf16[1024,8,64]{0,2,1:T(8,128)(2,1)S(1)} %reshape.847) | copy-start | bytes 3145732
  457.8 46.9 %all-to-all-start.3 = ((bf16[4,2,65536]{2,1,0:T(2,128)(2,1)}), bf16[4,2,65536]{2,1,0:T(2,128)(2,1)S(1)}, u32[]{:S(2)}, u32[]{:S(2)}) async-start(bf16[4,2,65536]{2,1,0:T(2,128)(2,1)} %reshape.879), calls=%async_computation.3 | async-start | bytes 2097152 | tf_op jit(solution)/shard_map/all_to_all | solution.py:159
  461.3 1082.3 %reduce-scatter.14.cloned.1.call-start = ((), (), s32[]{:S(2)}) async-start(), calls=%async_computation.25 | async-start | bytes 17301504 | tf_op jit(solution)/shard_map/reduce_scatter | solution.py:301
  517.0 263.1 %copy-start.17 = (bf16[256,2048]{1,0:T(8,128)(2,1)}, bf16[256,2048]{1,0:T(8,128)(2,1)S(1)}, u32[]{:S(2)}) copy-start(bf16[256,2048]{1,0:T(8,128)(2,1)S(1)} %multiply_convert_fusion.5) | copy-start | bytes 3145732
  1000.4 17.0 copy-start.13
  1017.4 16.9 copy-start.23
  1067.9 29.2 all-to-all-start.4
  1071.4 472.1 %reduce-scatter.12.cloned.1.call-start = ((), (), s32[]{:S(2)}) async-start(), calls=%async_computation.24 | async-start | bytes 17301504 | tf_op jit(solution)/shard_map/reduce_scatter | solution.py:298
  1225.7 29.8 all-to-all-start.5
  1255.5 28.8 all-to-all-start.6
  1259.0 384.9 %reduce-scatter.8.cloned.1.call-start = ((), (), s32[]{:S(2)}) async-start(), calls=%async_computation.22 | async-start | bytes 17301504 | tf_op jit(solution)/shard_map/reduce_scatter | solution.py:292
  1309.4 521.9 %reduce-scatter.10.cloned.1.call-start = ((), (), s32[]{:S(2)}) async-start(), calls=%async_computation.23 | async-start | bytes 17301504 | tf_op jit(solution)/shard_map/reduce_scatter | solution.py:295
  1317.7 1223.6 %reduce-scatter.20.cloned.1.call-start = ((), (), s32[]{:S(2)}) async-start(), calls=%async_computation.28 | async-start | bytes 69206016 | tf_op jit(solution)/shard_map/reduce_scatter | solution.py:181
  1345.0 1909.5 %reduce-scatter.18.cloned.1.call-start = ((), (), s32[]{:S(2)}) async-start(), calls=%async_computation.27 | async-start | bytes 69206016 | tf_op jit(solution)/shard_map/reduce_scatter | solution.py:206
  1372.4 2595.2 %reduce-scatter.16.cloned.1.call-start = ((), (), s32[]{:S(2)}) async-start(), calls=%async_computation.26 | async-start | bytes 69206016 | tf_op jit(solution)/shard_map/reduce_scatter | solution.py:201
  1400.2 17.8 copy-start.7
  1400.2 17.8 copy-start.9
  1400.2 17.8 copy-start.21
  1400.2 17.9 copy-start.35
  1432.5 107.5 %copy-start.11 = (f32[256,2048]{1,0:T(8,128)S(1)}, f32[256,2048]{1,0:T(8,128)}, u32[]{:S(2)}) copy-start(f32[256,2048]{1,0:T(8,128)} %copy-done.10) | copy-start | bytes 6291460
  (44 other events, 193.1 us)
Sparse Core Ops, SparseCore 0:
  10.9 79.3 all-gather.7
  93.2 91.6 all-gather.11
  187.7 76.0 all-gather.9
  266.5 96.0 all-gather.13
  365.4 219.1 all-gather.17
  587.2 192.8 all-gather.15
  783.0 192.9 all-gather.19
  1044.6 186.9 reduce-scatter.13
  1234.4 207.0 reduce-scatter.11
  1444.2 199.6 reduce-scatter.7
  1646.8 184.4 reduce-scatter.9
  1834.1 707.1 reduce-scatter.19
  2544.3 710.1 reduce-scatter.17
  3257.3 710.2 reduce-scatter.15
where the time goes:
time: 3990 us; the launch traced here: 3970 us
  waiting for transfers between devices  3160 us (79%)
  matrix products  323 us (8%)
  blocking collectives  172 us (4%)
  local copies, waits for them, and re-layouts  145 us (4%)
  other arithmetic  134 us (3%)
    reduce_scatter x1, waiting for transfers between devices, local(): lax.psum_scatter(outer_sum(normed_two, grad_up), ('seq', 'fsdp'), scatter...  713 us
    reduce_scatter x1, waiting for transfers between devices, local(): lax.psum_scatter(outer_sum(normed_two, grad_gate), ('seq', 'fsdp'), scatt...  713 us
    reduce_scatter x1, waiting for transfers between devices, local(): lax.psum_scatter(outer_sum(hidden, grad_outb), ('seq', 'fsdp'), scatter_d...  710 us
    reduce_scatter x1, waiting for transfers between devices, local(): lax.psum_scatter(outer_sum(normed_one, grad_key), ('seq', 'fsdp'), scatte...  187 us
    all_gather x1, waiting for transfers between devices, local(): lax.all_gather(w_down, ('seq', 'fsdp'), axis=0, tiled=True)  178 us
    all_gather x1, waiting for transfers between devices, local(): lax.all_gather(w_gate, ('seq', 'fsdp'), axis=0, tiled=True)  178 us
    unnamed x2, blocking collectives  143 us
    dot_general x7, matrix products, outer_sum(): lax.dot_general(left, right, (((0,), (0,)), ((), ())), preferred_element_...  111 us
  transfers between devices with their start and end apart: 21, of which 17 were waited for; matrix products, arithmetic and copies ran while one was open for 13% of the time, Pallas kernels for 0%

commit v1 on v0

v1 whole, which is shorter than its diff:
```python
import functools
import math

import jax
import jax.numpy as jnp
from jax import lax
from jax.experimental import pallas as pl
from jax.experimental.pallas import tpu as pltpu
from jax.sharding import Mesh
from jax.sharding import PartitionSpec as P

HEAD_DIM = 64
HALF = HEAD_DIM // 2
SCALE = HEAD_DIM ** (-0.5)
EPS = 1e-05
ROPE_BASE = 130000.0
BF = jnp.bfloat16
F32 = jnp.float32


def dot(left, right, dims):
    return lax.dot_general(left, right, (dims, ((), ())), preferred_element_type=F32)


def mm(left, right):
    return dot(left, right, ((left.ndim - 1,), (0,)))


def mm_nt(left, right):
    return dot(left, right, ((left.ndim - 1,), (1,)))


def mm_tn(left, right):
    return dot(left, right, ((0,), (0,)))


def qk_head(width, head):
    lane = lax.broadcasted_iota(jnp.int32, (1, width), 1)
    return (lane % (width // 2)) // HALF == head


def v_head(width, head):
    return lax.broadcasted_iota(jnp.int32, (1, width), 1) // HEAD_DIM == head


def causal(rows):
    key = lax.broadcasted_iota(jnp.int32, (rows, rows), 0)
    query = lax.broadcasted_iota(jnp.int32, (rows, rows), 1)
    return key <= query


def attend_kernel(heads, ring, where_ref, qkv_ref, send_ref, keep_ref, lse_ref, key_ref, vt_ref, ot_ref):
    rows, width = qkv_ref.shape[1], qkv_ref.shape[2] // 3
    block = pl.program_id(1)
    z = where_ref[0]

    @pl.when(block == 0)
    def _():
        for p in range(ring):
            at = lax.rem(z - p + ring, ring)
            key_ref[p * rows : (p + 1) * rows] = qkv_ref[at, :, width : 2 * width]
            vt_ref[:, p * rows : (p + 1) * rows] = qkv_ref[at, :, 2 * width :].T

    def one(p):
        done = p * rows
        query = qkv_ref[lax.rem(z - p + ring, ring), :, :width]
        keep = causal(rows)
        for head in range(heads):
            query_h = jnp.where(qk_head(width, head), query, jnp.zeros_like(query))
            diag = dot(key_ref[done : done + rows], query_h, ((1,), (1,))) * SCALE
            diag = jnp.where(keep, diag, -1e30)
            top = jnp.max(diag, axis=0, keepdims=True)
            if p:
                past = dot(key_ref[:done], query_h, ((1,), (1,))) * SCALE
                top = jnp.maximum(top, jnp.max(past, axis=0, keepdims=True))
                past = jnp.exp(past - top)
            diag = jnp.exp(diag - top)
            total = jnp.sum(diag, axis=0, keepdims=True)
            if p:
                total = total + jnp.sum(past, axis=0, keepdims=True)
            share = 1.0 / total
            at = slice(head * HEAD_DIM, (head + 1) * HEAD_DIM)
            out = mm(vt_ref[at, done : done + rows], (diag * share).astype(BF))
            if p:
                out = out + mm(vt_ref[at, :done], (past * share).astype(BF))
            ot_ref[at] = out
            lse_ref[head : head + 1] = top + jnp.log(total)
        out = ot_ref[...].T.astype(BF)
        send_ref[...] = out
        keep_ref[...] = out

    for p in range(ring):
        pl.when(block == p)(functools.partial(one, p))


def attend(qkv, where, heads):
    ring, pair, rows, full = qkv.shape
    width = full // 3
    return pl.pallas_call(
        functools.partial(attend_kernel, heads, ring),
        out_shape=(
            jax.ShapeDtypeStruct((ring * pair, rows, width), BF),
            jax.ShapeDtypeStruct((ring, pair, rows, width), BF),
            jax.ShapeDtypeStruct((pair, ring, heads, rows), F32),
        ),
        grid_spec=pltpu.PrefetchScalarGridSpec(
            num_scalar_prefetch=1,
            grid=(pair, ring),
            in_specs=[pl.BlockSpec((ring, None, rows, full), lambda i, p, w: (0, i, 0, 0))],
            out_specs=[
                pl.BlockSpec((None, rows, width), lambda i, p, w: (p * pair + lax.rem(w[1] + i, pair), 0, 0)),
                pl.BlockSpec((None, None, rows, width), lambda i, p, w: (lax.rem(w[0] - p + ring, ring), i, 0, 0)),
                pl.BlockSpec((None, None, heads, rows), lambda i, p, w: (i, p, 0, 0)),
            ],
            scratch_shapes=[
                pltpu.VMEM((ring * rows, width), BF),
                pltpu.VMEM((width, ring * rows), BF),
                pltpu.VMEM((width, rows), F32),
            ],
        ),
        compiler_params=pltpu.CompilerParams(vmem_limit_bytes=48 << 20),
        cost_estimate=pl.CostEstimate(
            flops=2 * 2 * pair * heads * (ring * rows) ** 2 * width * 5 // 8,
            bytes_accessed=2 * qkv.size * 2,
            transcendentals=pair * heads * (ring * rows) ** 2,
        ),
        name="attend",
    )(where, qkv)


def attend_back_kernel(
    heads, ring, where_ref, qkv_ref, datt_ref, lse_ref, cos_ref, sin_ref, out_ref,
    key_ref, kt_ref, val_ref, qt_ref, dk_ref, dv_ref,
):
    rows, width = qkv_ref.shape[1], qkv_ref.shape[2] // 3
    half = width // 2
    block = pl.program_id(1)
    z = where_ref[0]

    @pl.when(block == 0)
    def _():
        for p in range(ring):
            at = lax.rem(z - p + ring, ring)
            key = qkv_ref[at, :, width : 2 * width]
            key_ref[p * rows : (p + 1) * rows] = key
            kt_ref[:, p * rows : (p + 1) * rows] = key.T
            val_ref[p * rows : (p + 1) * rows] = qkv_ref[at, :, 2 * width :]
        dk_ref[...] = jnp.zeros_like(dk_ref)
        dv_ref[...] = jnp.zeros_like(dv_ref)

    def turn_back(grad, p):
        cosine, sine = cos_ref[p * rows : (p + 1) * rows], sin_ref[p * rows : (p + 1) * rows]
        grad = grad.astype(BF).astype(F32)
        first, second = grad[:, :half], grad[:, half:]
        return (first * cosine + second * sine).astype(BF), (second * cosine - first * sine).astype(BF)

    def one(p):
        done = p * rows
        at = lax.rem(z - p + ring, ring)
        query = qkv_ref[at, :, :width]
        grad = datt_ref[...]
        keep = causal(rows)
        for head in range(heads):
            query_h = jnp.where(qk_head(width, head), query, jnp.zeros_like(query))
            grad_h = jnp.where(v_head(width, head), grad, jnp.zeros_like(grad))
            lse = lse_ref[head : head + 1]
            parts = []
            for low, high in ([(0, done)] if p else []) + [(done, done + rows)]:
                score = dot(key_ref[low:high], query_h, ((1,), (1,))) * SCALE
                prob = jnp.exp(score - lse)
                if low == done:
                    prob = jnp.where(keep, prob, 0.0)
                dprob = dot(val_ref[low:high], grad_h, ((1,), (1,)))
                parts.append((low, high, prob, dprob))
            delta = sum(jnp.sum(prob * dprob, axis=0, keepdims=True) for _, _, prob, dprob in parts)
            turned = 0.0
            for low, high, prob, dprob in parts:
                dscore = (prob * (dprob - delta)).astype(BF)
                key_t = jnp.concatenate(
                    [
                        kt_ref[head * HALF : (head + 1) * HALF, low:high],
                        kt_ref[half + head * HALF : half + (head + 1) * HALF, low:high],
                    ],
                    axis=0,
                )
                turned = turned + mm(key_t, dscore)
                dk_ref[low:high] += mm(dscore, query_h)
                dv_ref[low:high] += mm(prob.astype(BF), grad_h)
            qt_ref[head * HALF : (head + 1) * HALF] = turned[:HALF]
            qt_ref[half + head * HALF : half + (head + 1) * HALF] = turned[HALF:]
        first, second = turn_back(qt_ref[...].T * SCALE, p)
        out_ref[at, :, :half] = first
        out_ref[at, :, half:width] = second

    for p in range(ring):
        pl.when(block == p)(functools.partial(one, p))

    @pl.when(block == ring - 1)
    def _():
        for p in range(ring):
            at = lax.rem(z - p + ring, ring)
            first, second = turn_back(dk_ref[p * rows : (p + 1) * rows] * SCALE, p)
            out_ref[at, :, width : width + half] = first
            out_ref[at, :, width + half : 2 * width] = second
            out_ref[at, :, 2 * width :] = dv_ref[p * rows : (p + 1) * rows].astype(BF)


def attend_back(qkv, datt, lse, cosine, sine, where, heads):
    ring, pair, rows, full = qkv.shape
    width = full // 3
    return pl.pallas_call(
        functools.partial(attend_back_kernel, heads, ring),
        out_shape=jax.ShapeDtypeStruct(qkv.shape, BF),
        grid_spec=pltpu.PrefetchScalarGridSpec(
            num_scalar_prefetch=1,
            grid=(pair, ring),
            in_specs=[
                pl.BlockSpec((ring, None, rows, full), lambda i, p, w: (0, i, 0, 0)),
                pl.BlockSpec((None, rows, width), lambda i, p, w: (p * pair + lax.rem(w[1] + i, pair), 0, 0)),
                pl.BlockSpec((None, None, heads, rows), lambda i, p, w: (i, p, 0, 0)),
                pl.BlockSpec((ring * rows, width // 2), lambda i, p, w: (0, 0)),
                pl.BlockSpec((ring * rows, width // 2), lambda i, p, w: (0, 0)),
            ],
            out_specs=pl.BlockSpec((ring, None, rows, full), lambda i, p, w: (0, i, 0, 0)),
            scratch_shapes=[
                pltpu.VMEM((ring * rows, width), BF),
                pltpu.VMEM((width, ring * rows), BF),
                pltpu.VMEM((ring * rows, width), BF),
                pltpu.VMEM((width, rows), F32),
                pltpu.VMEM((ring * rows, width), F32),
                pltpu.VMEM((ring * rows, width), F32),
            ],
        ),
        compiler_params=pltpu.CompilerParams(vmem_limit_bytes=52 << 20),
        cost_estimate=pl.CostEstimate(
            flops=5 * 2 * pair * heads * (ring * rows) ** 2 * width * 5 // 8,
            bytes_accessed=4 * qkv.size * 2,
            transcendentals=pair * heads * (ring * rows) ** 2,
        ),
        name="attend_back",
    )(where, qkv, datt, lse, cosine, sine)


def unit(values):
    inverse = lax.rsqrt(jnp.mean(values * values, axis=1, keepdims=True) + EPS)
    return values * inverse, inverse


def unit_back(grad, normed, inverse):
    return inverse * (grad - normed * jnp.mean(grad * normed, axis=1, keepdims=True))


def local(ring, plane, pair, inputs, norm1_gain, w_query, w_key, w_value, w_output, norm2_gain, w_gate, w_up, w_down, out_grad):
    seq_count, rows, model = inputs.shape
    parts = ring * pair
    own = w_query.shape[0]
    ff_own = w_down.shape[0]
    width = model // parts
    heads = width // HEAD_DIM
    half = width // 2
    ff = plane * ff_own
    group = ("seq", "core")
    z = lax.axis_index("seq")
    where = jnp.stack([z, lax.axis_index("core")]).astype(jnp.int32)
    ring_pairs = [(i, (i + 1) % ring) for i in range(ring)]
    core_pairs = [(i, (i + 1) % pair) for i in range(pair)]

    def hop(x):
        return lax.ppermute(x, "seq", ring_pairs)

    def swap(x):
        return lax.ppermute(x, "core", core_pairs)

    def ring_gather(x):
        blocks = [x]
        for _ in range(ring - 1):
            blocks.append(hop(blocks[-1]))
        return [jnp.stack([b, swap(b)]) for b in blocks]

    def ring_sum(terms):
        shares = [t[0].astype(F32) + swap(t[1]).astype(F32) for t in terms]
        total = shares[1].astype(BF)
        for k in range(2, ring):
            total = (hop(total).astype(F32) + shares[k]).astype(BF)
        return hop(total).astype(F32) + shares[0]

    def exchange(x):
        return lax.all_to_all(x, group, 0, 0, tiled=True)

    def plane_gather(x):
        return lax.all_gather(x, "yx", axis=0, tiled=True)

    def plane_sum(x):
        return lax.psum_scatter(x.astype(BF), "yx", scatter_dimension=0, tiled=True)

    def to_rows(x):
        return x.reshape(rows, ring, plane, pair * own).transpose(0, 2, 1, 3).reshape(rows, model)

    def from_rows(x):
        return x.reshape(rows, plane, ring, pair * own).transpose(0, 2, 1, 3).reshape(rows, model)

    def halves_out(w):
        return w.reshape(own, parts, heads, 2, HALF).transpose(1, 0, 3, 2, 4).reshape(parts, own, width)

    def halves_back(w):
        return w.reshape(parts, own, 2, heads, HALF).transpose(1, 0, 3, 2, 4).reshape(own, model)

    def heads_out(w):
        return w.reshape(own, parts, width).transpose(1, 0, 2)

    def heads_back(w):
        return w.transpose(1, 0, 2).reshape(own, model)

    def ff_out(w):
        return w.reshape(own, ring, plane, pair, ff_own).transpose(1, 3, 0, 2, 4).reshape(parts, own, ff)

    def ff_back(w):
        return w.reshape(ring, pair, own, plane, ff_own).transpose(2, 0, 3, 1, 4).reshape(own, parts * ff)

    gain_one, gain_two = norm1_gain.astype(F32)[:, None], norm2_gain.astype(F32)[:, None]

    def scaled(w, gain):
        return (w.astype(F32) * gain).astype(BF)

    qkv_w = exchange(
        jnp.concatenate(
            [halves_out(scaled(w_query, gain_one)), halves_out(scaled(w_key, gain_one)), heads_out(scaled(w_value, gain_one))],
            axis=2,
        )
    )
    qkv_w = plane_gather(qkv_w.reshape(parts * own, 3 * width))
    down_w = plane_gather(w_down)
    output_w = lax.all_gather(w_output, ("seq", "yx", "core"), axis=0, tiled=True)
    ff_w = exchange(jnp.concatenate([ff_out(scaled(w_gate, gain_two)), ff_out(scaled(w_up, gain_two))], axis=2))
    ff_w = plane_gather(ff_w.reshape(parts * own, 2 * ff))

    residual = inputs.reshape(rows, model).astype(F32)
    normed_one, inverse_one = unit(residual)
    ones = ring_gather(to_rows(normed_one.astype(BF)))

    freqs = jnp.exp(jnp.arange(HALF, dtype=F32) * (-2.0 * math.log(ROPE_BASE) / HEAD_DIM))
    angle = jnp.arange(ring * rows, dtype=jnp.int32).astype(F32)[:, None] * freqs[None, :]
    cosine, sine = jnp.tile(jnp.cos(angle), (1, heads)), jnp.tile(jnp.sin(angle), (1, heads))
    qkv = []
    for k in range(ring):
        start = lax.rem(z - k + ring, ring) * rows
        cos_k = lax.dynamic_slice_in_dim(cosine, start, rows)
        sin_k = lax.dynamic_slice_in_dim(sine, start, rows)
        flat = mm(ones[k].reshape(pair * rows, model), qkv_w).reshape(pair, rows, 3 * width)
        q1, q2 = flat[..., :half], flat[..., half:width]
        k1, k2 = flat[..., width : width + half], flat[..., width + half : 2 * width]
        qkv.append(
            jnp.concatenate(
                [
                    q1 * cos_k - q2 * sin_k,
                    q2 * cos_k + q1 * sin_k,
                    k1 * cos_k - k2 * sin_k,
                    k2 * cos_k + k1 * sin_k,
                    flat[..., 2 * width :],
                ],
                axis=-1,
            ).astype(BF)
        )
    qkv = jnp.stack(qkv)
    att_send, att_keep, lse = attend(qkv, where, heads)
    att = exchange(att_send).transpose(1, 0, 2).reshape(rows, model)
    mid = residual + mm(att, output_w)

    normed_two, inverse_two = unit(mid)
    twos = ring_gather(to_rows(normed_two.astype(BF)))
    grad_out = out_grad.reshape(rows, model)
    douts = ring_gather(grad_out)
    out_terms, two_terms, hiddens, dffs = [], [], [], []
    for k in range(ring):
        two, dout = twos[k].reshape(pair * rows, model), douts[k].reshape(pair * rows, model)
        both = mm(two, ff_w)
        gate, up = both[:, :ff], both[:, ff:]
        sig = jax.nn.sigmoid(gate)
        hidden = (gate * sig * up).astype(BF)
        out_terms.append(mm(hidden, down_w).astype(BF).reshape(pair, rows, model))
        dhid = mm_nt(dout, down_w)
        dgate = (dhid * up * sig * (1.0 + gate * (1.0 - sig))).astype(BF)
        dup = (dhid * gate * sig).astype(BF)
        dff = jnp.concatenate([dgate, dup], axis=1)
        two_terms.append(mm_nt(dff, ff_w).astype(BF).reshape(pair, rows, model))
        hiddens.append(hidden)
        dffs.append(dff)
    grad_two = from_rows(ring_sum(two_terms))
    output = (mid + ring_sum(out_terms)).astype(BF).reshape(inputs.shape)
    tokens = ring * pair * rows
    twos, douts = jnp.stack(twos).reshape(tokens, model), jnp.stack(douts).reshape(tokens, model)
    down_grad = plane_sum(mm_tn(jnp.concatenate(hiddens), douts)).astype(F32)
    ff_grad = plane_sum(mm_tn(twos, jnp.concatenate(dffs)))
    ff_grad = exchange(ff_grad.reshape(parts, own, 2 * ff)).astype(F32)
    gate_hat, up_hat = ff_back(ff_grad[..., :ff]), ff_back(ff_grad[..., ff:])
    gain_two_grad = jnp.sum(w_gate.astype(F32) * gate_hat + w_up.astype(F32) * up_hat, axis=1)

    grad_mid = grad_out.astype(F32) + unit_back(grad_two, normed_two, inverse_two)
    proj = grad_mid.astype(BF)
    datt = mm_nt(proj, output_w).astype(BF)
    datt = exchange(datt.reshape(rows, parts, width).transpose(1, 0, 2))
    dqkv = attend_back(qkv, datt, lse, cosine, sine, where, heads)
    projs = jnp.stack(ring_gather(proj)).reshape(tokens, model)
    output_grad = plane_sum(mm_tn(att_keep.reshape(tokens, width), projs)).astype(BF)
    moves = [(y * pair + c, c * plane + y) for y in range(plane) for c in range(pair)]
    output_grad = lax.ppermute(output_grad, ("yx", "core"), moves).astype(F32)

    one_terms = [mm_nt(dqkv[k].reshape(pair * rows, 3 * width), qkv_w).astype(BF).reshape(pair, rows, model) for k in range(ring)]
    ones = jnp.stack(ones).reshape(tokens, model)
    qkv_grad = plane_sum(mm_tn(ones, dqkv.reshape(tokens, 3 * width)))
    qkv_grad = exchange(qkv_grad.reshape(parts, own, 3 * width)).astype(F32)
    query_hat = halves_back(qkv_grad[..., :width])
    key_hat = halves_back(qkv_grad[..., width : 2 * width])
    value_hat = heads_back(qkv_grad[..., 2 * width :])
    gain_one_grad = jnp.sum(
        w_query.astype(F32) * query_hat + w_key.astype(F32) * key_hat + w_value.astype(F32) * value_hat, axis=1
    )
    grad_one = from_rows(ring_sum(one_terms))
    input_grad = (grad_mid + unit_back(grad_one, normed_one, inverse_one)).reshape(inputs.shape)
    return (
        output,
        input_grad,
        gain_one_grad,
        query_hat * gain_one,
        key_hat * gain_one,
        value_hat * gain_one,
        output_grad,
        gain_two_grad,
        gate_hat * gain_two,
        up_hat * gain_two,
        down_grad,
    )


def solution(mesh):
    ring, fsdp = mesh.shape["seq"], mesh.shape["fsdp"]
    pair = 2
    plane = fsdp // pair
    fine = Mesh(mesh.devices.reshape(ring, plane, pair), ("seq", "yx", "core"))
    tokens = P(("yx", "core"), "seq", None)
    every = ("seq", "yx", "core")
    weight, gain = P(every, None), P(every)
    return jax.shard_map(
        functools.partial(local, ring, plane, pair),
        mesh=fine,
        in_specs=(tokens, gain, weight, weight, weight, weight, gain, weight, weight, weight, tokens),
        out_specs=(tokens, tokens, gain, weight, weight, weight, weight, gain, weight, weight, weight),
        check_vma=False,
    )
```

time: 3990 us -> 1040 us (0.26)
  waiting for transfers between devices: 3160 us -> 356 us
  matrix products: 323 us -> 188 us
  blocking collectives: 172 us -> 78.1 us
  starting transfers between devices: 28.2 us -> 109 us
  Pallas kernels: 0 us -> 45.4 us
    reduce_scatter x7 -> x4, waiting for transfers between devices: 2420 us -> 0.03 us  [plane_sum(): return lax.psum_scatter(x.astype(BF), 'yx', scatter_dimension=0, tiled=True)]
    all_gather x7 -> x4, waiting for transfers between devices: 589 us -> 0.01 us  [the longest x3 0.01 us: plane_gather(): return lax.all_gather(x, 'yx', axis=0, tiled=True)]
    ppermute x0 -> x50, waiting for transfers between devices: none -> 303 us  [the longest x21 301 us: hop(): return lax.ppermute(x, 'seq', ring_pairs)]
    unnamed x2 -> x0, blocking collectives: 143 us -> none
    dot_general x33 -> x30, matrix products: 323 us -> 188 us  [dot(): lax.dot_general(left, right, (dims, ((), ())), preferred_element_type=F32)]
    ppermute x0 -> x50, starting transfers between devices: none -> 88 us  [the longest x28 74.4 us: swap(): return lax.ppermute(x, 'core', core_pairs)]
    all_to_all x7 -> x4, waiting for transfers between devices: 139 us -> 51.1 us  [exchange(): return lax.all_to_all(x, group, 0, 0, tiled=True)]
    unnamed x12 -> x17, other arithmetic: 87.1 us -> 1.23 us
  transfers between devices with their start and end apart: 21 -> 62, of which waited for: 17 -> 17; matrix products, arithmetic and copies ran while one was open for 13% -> 32% of each run, Pallas kernels for 0% -> 2%
where the time goes in v1:
time: 1040 us; the launch traced here: 1020 us
  waiting for transfers between devices  356 us (34%)
  matrix products  188 us (18%)
  local copies, waits for them, and re-layouts  125 us (12%)
  starting transfers between devices  109 us (10%)
  other arithmetic  108 us (10%)
  blocking collectives  78.1 us (8%)
  Pallas kernels  45.4 us (4%)
  between operations  15.9 us (2%)
    ppermute x21, waiting for transfers between devices, hop(): return lax.ppermute(x, 'seq', ring_pairs)  301 us
    dot_general x30, matrix products, dot(): lax.dot_general(left, right, (dims, ((), ())), preferred_element_type=F32)  188 us
    all_to_all x2, blocking collectives, exchange(): return lax.all_to_all(x, group, 0, 0, tiled=True)  78.1 us
    ppermute x28, starting transfers between devices, swap(): return lax.ppermute(x, 'core', core_pairs)  74.4 us
    all_to_all x4, waiting for transfers between devices, exchange(): return lax.all_to_all(x, group, 0, 0, tiled=True)  51.1 us
    unnamed x184, local copies, waits for them, and re-layouts  28.4 us
    pallas_call x1, Pallas kernels, attend_back(): pl.pallas_call(functools.partial(attend_back_kernel, heads, ring), out_sh...  26.1 us
  transfers between devices with their start and end apart: 62, of which 17 were waited for; matrix products, arithmetic and copies ran while one was open for 32% of the time, Pallas kernels for 2%

profile of v1, /device:TPU:5, one launch (start us, length us, event | category | flops | bytes accessed | tf_op | source)
XLA Modules:
  0.0 1024.8 jit_solution(4859626020041210552)
XLA Ops:
  13.9 25.6 %all_to_all.30 = bf16[8,64,768]{2,1,0:T(8,128)(2,1)} all-to-all(bf16[8,64,768]{2,1,0:T(8,128)(2,1)} %copy.116), channel_id=1, replica_groups=mesh['seq'=4,'yx'=4,'core'=2] {'seq','core'}, dimensions={0} | all-to-all | bytes 1572864 | tf_op jit(solution)/shard_map/all_to_all | solution.py:288
  46.2 52.5 %all_to_all.31 = bf16[8,64,2048]{2,1,0:T(8,128)(2,1)} all-to-all(bf16[8,64,2048]{2,1,0:T(8,128)(2,1)S(1)} %pad_maximum_fusion.8), channel_id=1, replica_groups=mesh['seq'=4,'yx'=4,'core'=2] {'seq','core'}, dimensions={0} | all-to-all | bytes 4194304 | tf_op jit(solution)/shard_map/all_to_all | solution.py:288
  105.0 35.3 %collective-permute-done.1 = bf16[256,2048]{1,0:T(8,128)(2,1)S(1)} collective-permute-done((bf16[256,2048]{1,0:T(8,128)(2,1)}, bf16[256,2048]{1,0:T(8,128)(2,1)S(1)}, u32[]{:S(2)}, u32[]{:S(2)}) %collective-permute-start.1) | collective-permute-done | bytes 1048608 | tf_op jit(solution)/shard_map/ppermute | solution.py:269
  141.3 44.0 %collective-permute-done.3 = bf16[256,2048]{1,0:T(8,128)(2,1)} collective-permute-done((bf16[256,2048]{1,0:T(8,128)(2,1)S(1)}, bf16[256,2048]{1,0:T(8,128)(2,1)}, u32[]{:S(2)}, u32[]{:S(2)}) %collective-permute-start.3) | collective-permute-done | bytes 1048608 | tf_op jit(solution)/shard_map/ppermute | solution.py:269
  196.1 13.8 %collective-permute-done.5 = bf16[256,2048]{1,0:T(8,128)(2,1)} collective-permute-done((bf16[256,2048]{1,0:T(8,128)(2,1)}, bf16[256,2048]{1,0:T(8,128)(2,1)}, u32[]{:S(2)}, u32[]{:S(2)}) %collective-permute-start.5) | collective-permute-done | bytes 1048608 | tf_op jit(solution)/shard_map/ppermute | solution.py:269
  209.9 9.8 collective-permute-start.6
  235.5 19.3 %attend.1 = (bf16[8,256,256]{2,1,0:T(8,128)(2,1)}, bf16[4,2,256,256]{3,2,1,0:T(8,128)(2,1)S(1)}, f32[2,4,4,256]{3,2,1,0:T(4,128)S(1)}) custom-call(s32[2]{0:T(128)S(1)} %pad_add_fusion.where_ref, bf16[4,2,256,768]{3,2,1,0:T(8,128)(2,1)S(1)} %pad_maximum_fusion.2.qkv_ref), custom_call_target="tpu_custom_call" | custom-call | flops 5368709120 | bytes 6291456 | tf_op jit(solution)/shard_map/attend/pallas_call | solution.py:99
  261.0 41.0 %collective-permute-done.25 = bf16[256,2048]{1,0:T(8,128)(2,1)} collective-permute-done((bf16[256,2048]{1,0:T(8,128)(2,1)}, bf16[256,2048]{1,0:T(8,128)(2,1)}, u32[]{:S(2)}, u32[]{:S(2)}) %collective-permute-start.25) | collective-permute-done | bytes 1048608 | tf_op jit(solution)/shard_map/ppermute | solution.py:269
  307.9 7.1 multiply_reduce_fusion.2
  322.2 32.9 %collective-permute-start.22 = (bf16[256,2048]{1,0:T(8,128)(2,1)}, bf16[256,2048]{1,0:T(8,128)(2,1)S(1)}, u32[]{:S(2)}, u32[]{:S(2)}) collective-permute-start(bf16[256,2048]{1,0:T(8,128)(2,1)} %collective-permute-done.21), channel_id=1, source_target_pairs={{0,1},{1,0},{2,3},{3,2},{4,5},{5,4},{6,7},{7,6},{8,9},{9,8},{10,11... | collective-permute-start | bytes 3145736 | tf_op jit(solution)/shard_map/ppermute | solution.py:272
  359.6 12.5 %collective-permute-start.8 = (bf16[256,2048]{0,1:T(8,128)(2,1)}, bf16[256,2048]{0,1:T(8,128)(2,1)}, u32[]{:S(2)}, u32[]{:S(2)}) collective-permute-start(bf16[256,2048]{0,1:T(8,128)(2,1)} %collective-permute-done.7), channel_id=1, source_target_pairs={{0,1},{1,0},{2,3},{3,2},{4,5},{5,4},{6,7},{7,6},{8,9},{9,8},{10,11... | collective-permute-start | bytes 3145736 | tf_op jit(solution)/shard_map/ppermute | solution.py:272
  396.9 10.5 %fusion.161 = f32[512,2048]{1,0:T(8,128)} fusion(bf16[512,2048]{1,0:T(8,128)(2,1)} %bitcast.340, bf16[2048,2048]{1,0:T(8,128)(2,1)} %all-gather.9.cloned.1.call-done), kind=kOutput, calls=%fused_computation.280 | convolution fusion | flops 4294967296 | bytes 14680064 | tf_op jit(solution)/shard_map/dot_general | solution.py:22
  407.4 8.3 multiply_convert_fusion.7
  440.4 7.0 fusion.162
  447.5 8.8 collective-permute-done.15
  500.0 8.9 convolution_convert_fusion.9
  510.4 8.1 convolution_convert_fusion.8
  521.4 24.6 %collective-permute-done.32 = bf16[256,2048]{1,0:T(8,128)(2,1)S(1)} collective-permute-done((bf16[256,2048]{1,0:T(8,128)(2,1)S(1)}, bf16[256,2048]{1,0:T(8,128)(2,1)S(1)}, u32[]{:S(2)}, u32[]{:S(2)}) %collective-permute-start.32) | collective-permute-done | bytes 1048608 | tf_op jit(solution)/shard_map/ppermute | solution.py:269
  589.3 13.0 %all-to-all-done.3.datt_ref = bf16[8,256,256]{2,1,0:T(8,128)(2,1)} async-done(((bf16[8,256,256]{2,1,0:T(8,128)(2,1)}), bf16[8,256,256]{2,1,0:T(8,128)(2,1)}, u32[]{:S(2)}, u32[]{:S(2)}) %all-to-all-start.3) | async-done | bytes 1048608 | tf_op jit(solution)/shard_map/all_to_all | solution.py:288
  602.3 26.1 %attend_back.1 = bf16[4,2,256,768]{3,2,1,0:T(8,128)(2,1)} custom-call(s32[2]{0:T(128)S(1)} %copy-done.2, bf16[4,2,256,768]{3,2,1,0:T(8,128)(2,1)} %copy-done, bf16[8,256,256]{2,1,0:T(8,128)(2,1)} %all-to-all-done.3.datt_ref, f32[2,4,4,256]{3,2,1,0:T(4,128)S(1)} %get-tuple-element.15.lse_ref, f32[1024,128]{1,0:T(8,128)S(1)} %copy.136.cos_ref, ...), custom_call_target="tpu_custom_call" | custom-call | flops 13421772800 | bytes 12582912 | tf_op jit(solution)/shard_map/attend_back/pallas_call | solution.py:211
  628.4 10.4 %bitcast_convert_fusion = bf16[2048,768]{1,0:T(8,128)(2,1)} fusion(bf16[4,2,256,768]{3,2,1,0:T(8,128)(2,1)} %attend_back.1, bf16[1,2,256,2048]{3,2,1,0:T(8,128)(2,1)S(1)} %copy-done.44, bf16[1,2,256,2048]{3,2,1,0:T(8,128)(2,1)S(1)} %copy-done.42, bf16[1,2,256,2048]{3,2,1,0:T(8,128)(2,1)S(1)} %copy-done.41, bf16[1,2,256,2048]{3,2,1,0:T(8,128)(2,1)S(1)} %copy-done.40), kind=kOutput, calls=%fused_computation.35 | convolution fusion | flops 6456606720 | bytes 14680064 | tf_op jit(solution)/shard_map/dot_general | solution.py:22
  647.2 11.7 %copy.144 = bf16[4,2,256,2048]{3,2,1,0:T(8,128)(2,1)} copy(bf16[4,2,256,2048]{2,3,1,0:T(8,128)(2,1)} %pad_maximum_fusion) | data formatting | bytes 16777216 | tf_op jit(solution)/shard_map/stack | solution.py:391
  658.9 26.2 %fusion.32 = bf16[2048,2048]{1,0:T(8,128)(2,1)} fusion(bf16[2048,2048]{1,0:T(8,128)(2,1)} %bitcast.310, bf16[512,1024]{1,0:T(8,128)(2,1)} %copy-done.86, bf16[512,1024]{1,0:T(8,128)(2,1)} %copy-done.85, bf16[512,1024]{1,0:T(8,128)(2,1)} %get-tuple-element.53, bf16[512,1024]{1,0:T(8,128)(2,1)} %get-tuple-element.52, bf16[512,1024]{1,0:T(8,128)(2,1)S(1)} %copy-done.82, ...), kind=kOutput, calls=%fused_computation.34 | convolution fusion | flops 17251172352 | bytes 25165824 | tf_op jit(solution)/shard_map/dot_general | solution.py:22
  686.3 25.2 %collective-permute-done.43 = bf16[256,2048]{1,0:T(8,128)(2,1)S(1)} collective-permute-done((bf16[256,2048]{1,0:T(8,128)(2,1)S(1)}, bf16[256,2048]{1,0:T(8,128)(2,1)S(1)}, u32[]{:S(2)}, u32[]{:S(2)}) %collective-permute-start.43) | collective-permute-done | bytes 1048608 | tf_op jit(solution)/shard_map/ppermute | solution.py:269
  716.2 19.5 %collective-permute-done.45 = bf16[256,2048]{1,0:T(8,128)(2,1)S(1)} collective-permute-done((bf16[256,2048]{1,0:T(8,128)(2,1)S(1)}, bf16[256,2048]{1,0:T(8,128)(2,1)S(1)}, u32[]{:S(2)}, u32[]{:S(2)}) %collective-permute-start.45) | collective-permute-done | bytes 1048608 | tf_op jit(solution)/shard_map/ppermute | solution.py:269
  743.9 15.2 %collective-permute-done.47 = bf16[256,2048]{1,0:T(8,128)(2,1)S(1)} collective-permute-done((bf16[256,2048]{1,0:T(8,128)(2,1)S(1)}, bf16[256,2048]{1,0:T(8,128)(2,1)S(1)}, u32[]{:S(2)}, u32[]{:S(2)}) %collective-permute-start.47) | collective-permute-done | bytes 1048608 | tf_op jit(solution)/shard_map/ppermute | solution.py:269
  769.5 13.5 %fusion.43 = bf16[1024,2048]{1,0:T(8,128)(2,1)} fusion(bf16[2048,2048]{1,0:T(8,128)(2,1)} %bitcast.309, bf16[512,1024]{1,0:T(8,128)(2,1)} %get-tuple-element.60, bf16[512,1024]{1,0:T(8,128)(2,1)} %get-tuple-element.59, bf16[512,1024]{1,0:T(8,128)(2,1)S(1)} %copy-done.76, bf16[512,1024]{1,0:T(8,128)(2,1)S(1)} %copy-done.75), kind=kOutput, calls=%fused_computation.44 | convolution fusion | flops 8608808960 | bytes 16777216 | tf_op jit(solution)/shard_map/dot_general | solution.py:22
  802.6 19.9 %collective-permute-done.36 = bf16[256,2048]{1,0:T(8,128)(2,1)S(1)} collective-permute-done((bf16[256,2048]{1,0:T(8,128)(2,1)S(1)}, bf16[256,2048]{1,0:T(8,128)(2,1)S(1)}, u32[]{:S(2)}, u32[]{:S(2)}) %collective-permute-start.36) | collective-permute-done | bytes 1048608 | tf_op jit(solution)/shard_map/ppermute | solution.py:269
  824.0 7.1 all-to-all-start.4
  840.5 27.1 %collective-permute-done.38 = bf16[256,2048]{1,0:T(8,128)(2,1)} collective-permute-done((bf16[256,2048]{1,0:T(8,128)(2,1)}, bf16[256,2048]{1,0:T(8,128)(2,1)}, u32[]{:S(2)}, u32[]{:S(2)}) %collective-permute-start.38) | collective-permute-done | bytes 1048608 | tf_op jit(solution)/shard_map/ppermute | solution.py:269
  870.7 36.9 %all-to-all-done.4 = bf16[8,64,768]{2,1,0:T(8,128)(2,1)S(1)} async-done(((bf16[8,64,768]{2,1,0:T(8,128)(2,1)}), bf16[8,64,768]{2,1,0:T(8,128)(2,1)S(1)}, u32[]{:S(2)}, u32[]{:S(2)}) %all-to-all-start.4) | async-done | bytes 786464 | tf_op jit(solution)/shard_map/all_to_all | solution.py:288
  946.8 26.8 %collective-permute-done.18 = bf16[256,2048]{1,0:T(8,128)(2,1)} collective-permute-done((bf16[256,2048]{1,0:T(8,128)(2,1)}, bf16[256,2048]{1,0:T(8,128)(2,1)}, u32[]{:S(2)}, u32[]{:S(2)}) %collective-permute-start.18) | collective-permute-done | bytes 1048608 | tf_op jit(solution)/shard_map/ppermute | solution.py:269
  (459 shorter events, 360.1 us)
Async XLA Ops:
  7.2 212.6 %all-gather.5.cloned.1.call-start = ((), (), s32[]{:S(2)}) async-start(), calls=%async_computation.10 | async-start | bytes 3932160 | tf_op jit(solution)/shard_map/all_gather | solution.py:291
  39.5 268.4 %all-gather.7.cloned.1.call-start = ((), (), s32[]{:S(2)}) async-start(), calls=%async_computation.11 | async-start | bytes 8650752 | tf_op jit(solution)/shard_map/all_gather | solution.py:333
  40.2 356.7 %all-gather.9.cloned.1.call-start = ((), (), s32[]{:S(2)}) async-start(), calls=%async_computation.12 | async-start | bytes 10485760 | tf_op jit(solution)/shard_map/all_gather | solution.py:291
  105.0 35.3 %collective-permute-start.1 = (bf16[256,2048]{1,0:T(8,128)(2,1)}, bf16[256,2048]{1,0:T(8,128)(2,1)S(1)}, u32[]{:S(2)}, u32[]{:S(2)}) collective-permute-start(bf16[256,2048]{1,0:T(8,128)(2,1)} %reshape.646), channel_id=1, source_target_pairs={{0,8},{8,16},{16,24},{24,0},{1,9},{9,17},{17,25},{25,1},{2,10},{10... | collective-permute-start | bytes 3145736 | tf_op jit(solution)/shard_map/ppermute | solution.py:269
  141.3 44.0 %collective-permute-start.3 = (bf16[256,2048]{1,0:T(8,128)(2,1)S(1)}, bf16[256,2048]{1,0:T(8,128)(2,1)}, u32[]{:S(2)}, u32[]{:S(2)}) collective-permute-start(bf16[256,2048]{1,0:T(8,128)(2,1)S(1)} %collective-permute-done.1), channel_id=1, source_target_pairs={{0,8},{8,16},{16,24},{24,0},{1,9},{9,17},{17,25},{25,1},{2,10},{10... | collective-permute-start | bytes 3145736 | tf_op jit(solution)/shard_map/ppermute | solution.py:269
  185.3 34.4 %collective-permute-start = (bf16[256,2048]{1,0:T(8,128)(2,1)}, bf16[256,2048]{1,0:T(8,128)(2,1)}, u32[]{:S(2)}, u32[]{:S(2)}) collective-permute-start(bf16[256,2048]{1,0:T(8,128)(2,1)} %reshape.646), channel_id=1, source_target_pairs={{0,1},{1,0},{2,3},{3,2},{4,5},{5,4},{6,7},{7,6},{8,9},{9,8},{10,11... | collective-permute-start | bytes 3145736 | tf_op jit(solution)/shard_map/ppermute | solution.py:272
  191.5 67.4 %collective-permute-start.21 = (bf16[256,2048]{1,0:T(8,128)(2,1)}, bf16[256,2048]{1,0:T(8,128)(2,1)}, u32[]{:S(2)}, u32[]{:S(2)}) collective-permute-start(bf16[256,2048]{1,0:T(8,128)(2,1)} %bitcast.64), channel_id=1, source_target_pairs={{0,8},{8,16},{16,24},{24,0},{1,9},{9,17},{17,25},{25,1},{2,10},{10... | collective-permute-start | bytes 3145736 | tf_op jit(solution)/shard_map/ppermute | solution.py:269
  195.6 31.9 %collective-permute-start.4 = (bf16[256,2048]{1,0:T(8,128)(2,1)}, bf16[256,2048]{1,0:T(8,128)(2,1)}, u32[]{:S(2)}, u32[]{:S(2)}) collective-permute-start(bf16[256,2048]{1,0:T(8,128)(2,1)} %collective-permute-done.3), channel_id=1, source_target_pairs={{0,1},{1,0},{2,3},{3,2},{4,5},{5,4},{6,7},{7,6},{8,9},{9,8},{10,11... | collective-permute-start | bytes 3145736 | tf_op jit(solution)/shard_map/ppermute | solution.py:272
  254.8 51.7 %all-to-all-start.1 = ((bf16[8,256,256]{2,1,0:T(8,128)(2,1)}), bf16[8,256,256]{2,1,0:T(8,128)(2,1)S(1)}, u32[]{:S(2)}, u32[]{:S(2)}) async-start(bf16[8,256,256]{2,1,0:T(8,128)(2,1)} %get-tuple-element.14), calls=%async_computation.1 | async-start | bytes 2097152 | tf_op jit(solution)/shard_map/all_to_all | solution.py:288
  258.4 149.1 %all-gather.11.cloned.1.call-start = ((), (), s32[]{:S(2)}) async-start(), calls=%async_computation.13 | async-start | bytes 5242880 | tf_op jit(solution)/shard_map/all_gather | solution.py:291
  258.9 43.1 %collective-permute-start.25 = (bf16[256,2048]{1,0:T(8,128)(2,1)}, bf16[256,2048]{1,0:T(8,128)(2,1)}, u32[]{:S(2)}, u32[]{:S(2)}) collective-permute-start(bf16[256,2048]{1,0:T(8,128)(2,1)} %collective-permute-done.21), channel_id=1, source_target_pairs={{0,8},{8,16},{16,24},{24,0},{1,9},{9,17},{17,25},{25,1},{2,10},{10... | collective-permute-start | bytes 3145736 | tf_op jit(solution)/shard_map/ppermute | solution.py:269
  260.3 95.3 %collective-permute-start.33 = (bf16[256,2048]{1,0:T(8,128)(2,1)}, bf16[256,2048]{1,0:T(8,128)(2,1)}, u32[]{:S(2)}, u32[]{:S(2)}) collective-permute-start(bf16[256,2048]{1,0:T(8,128)(2,1)} %bitcast.64), channel_id=1, source_target_pairs={{0,1},{1,0},{2,3},{3,2},{4,5},{5,4},{6,7},{7,6},{8,9},{9,8},{10,11... | collective-permute-start | bytes 3145736 | tf_op jit(solution)/shard_map/ppermute | solution.py:272
  302.0 53.2 %collective-permute-start.29 = (bf16[256,2048]{1,0:T(8,128)(2,1)}, bf16[256,2048]{1,0:T(8,128)(2,1)}, u32[]{:S(2)}, u32[]{:S(2)}) collective-permute-start(bf16[256,2048]{1,0:T(8,128)(2,1)} %collective-permute-done.25), channel_id=1, source_target_pairs={{0,8},{8,16},{16,24},{24,0},{1,9},{9,17},{17,25},{25,1},{2,10},{10... | collective-permute-start | bytes 3145736 | tf_op jit(solution)/shard_map/ppermute | solution.py:269
  321.3 38.3 %collective-permute-start.7 = (bf16[256,2048]{0,1:T(8,128)(2,1)}, bf16[256,2048]{0,1:T(8,128)(2,1)}, u32[]{:S(2)}, u32[]{:S(2)}) collective-permute-start(bf16[256,2048]{0,1:T(8,128)(2,1)} %bitcast.325), channel_id=1, source_target_pairs={{0,8},{8,16},{16,24},{24,0},{1,9},{9,17},{17,25},{25,1},{2,10},{10... | collective-permute-start | bytes 3145736 | tf_op jit(solution)/shard_map/ppermute | solution.py:269
  322.2 49.9 %collective-permute-start.22 = (bf16[256,2048]{1,0:T(8,128)(2,1)}, bf16[256,2048]{1,0:T(8,128)(2,1)S(1)}, u32[]{:S(2)}, u32[]{:S(2)}) collective-permute-start(bf16[256,2048]{1,0:T(8,128)(2,1)} %collective-permute-done.21), channel_id=1, source_target_pairs={{0,1},{1,0},{2,3},{3,2},{4,5},{5,4},{6,7},{7,6},{8,9},{9,8},{10,11... | collective-permute-start | bytes 3145736 | tf_op jit(solution)/shard_map/ppermute | solution.py:272
  389.1 32.5 %collective-permute-start.11 = (bf16[256,2048]{0,1:T(8,128)(2,1)}, bf16[256,2048]{0,1:T(8,128)(2,1)}, u32[]{:S(2)}, u32[]{:S(2)}) collective-permute-start(bf16[256,2048]{0,1:T(8,128)(2,1)} %collective-permute-done.7), channel_id=1, source_target_pairs={{0,8},{8,16},{16,24},{24,0},{1,9},{9,17},{17,25},{25,1},{2,10},{10... | collective-permute-start | bytes 3145736 | tf_op jit(solution)/shard_map/ppermute | solution.py:269
  439.9 46.0 %collective-permute-start.24 = (bf16[256,2048]{1,0:T(8,128)(2,1)}, bf16[256,2048]{1,0:T(8,128)(2,1)}, u32[]{:S(2)}, u32[]{:S(2)}) collective-permute-start(bf16[256,2048]{1,0:T(8,128)(2,1)} %add_convert_fusion.5), channel_id=1, source_target_pairs={{0,8},{8,16},{16,24},{24,0},{1,9},{9,17},{17,25},{25,1},{2,10},{10... | collective-permute-start | bytes 3145736 | tf_op jit(solution)/shard_map/ppermute | solution.py:269
  576.4 247.6 %reduce-scatter.5.cloned.1.call-start = ((), (), s32[]{:S(2)}) async-start(), calls=%async_computation.14 | async-start | bytes 3932160 | tf_op jit(solution)/shard_map/reduce_scatter | solution.py:294
  638.9 268.7 %reduce-scatter.9.cloned.1.call-start = ((), (), s32[]{:S(2)}) async-start(), calls=%async_computation.16 | async-start | bytes 10485760 | tf_op jit(solution)/shard_map/reduce_scatter | solution.py:294
  685.1 257.4 %reduce-scatter.7.cloned.1.call-start = ((), (), s32[]{:S(2)}) async-start(), calls=%async_computation.15 | async-start | bytes 1310720 | tf_op jit(solution)/shard_map/reduce_scatter | solution.py:294
  764.5 31.8 %collective-permute-start.10 = (bf16[256,2048]{1,0:T(8,128)(2,1)}, bf16[256,2048]{1,0:T(8,128)(2,1)}, u32[]{:S(2)}, u32[]{:S(2)}) collective-permute-start(bf16[256,2048]{1,0:T(8,128)(2,1)} %add_convert_fusion.9), channel_id=1, source_target_pairs={{0,8},{8,16},{16,24},{24,0},{1,9},{9,17},{17,25},{25,1},{2,10},{10... | collective-permute-start | bytes 3145736 | tf_op jit(solution)/shard_map/ppermute | solution.py:269
  769.4 210.5 %reduce-scatter.11.cloned.1.call-start = ((), (), s32[]{:S(2)}) async-start(), calls=%async_computation.17 | async-start | bytes 5242880 | tf_op jit(solution)/shard_map/reduce_scatter | solution.py:294
  799.2 119.9 %collective-permute-start.14 = (bf16[256,2048]{1,0:T(8,128)(2,1)}, bf16[256,2048]{1,0:T(8,128)(2,1)}, u32[]{:S(2)}, u32[]{:S(2)}) collective-permute-start(bf16[256,2048]{1,0:T(8,128)(2,1)} %add_convert_fusion.8), channel_id=1, source_target_pairs={{0,8},{8,16},{16,24},{24,0},{1,9},{9,17},{17,25},{25,1},{2,10},{10... | collective-permute-start | bytes 3145736 | tf_op jit(solution)/shard_map/ppermute | solution.py:269
  802.2 38.3 %collective-permute-start.39 = (bf16[256,2048]{1,0:T(8,128)(2,1)}, bf16[256,2048]{1,0:T(8,128)(2,1)}, u32[]{:S(2)}, u32[]{:S(2)}) collective-permute-start(bf16[256,2048]{1,0:T(8,128)(2,1)} %slice.324), channel_id=1, source_target_pairs={{0,1},{1,0},{2,3},{3,2},{4,5},{5,4},{6,7},{7,6},{8,9},{9,8},{10,11... | collective-permute-start | bytes 3145736 | tf_op jit(solution)/shard_map/ppermute | solution.py:272
  824.0 43.6 %collective-permute-start.38 = (bf16[256,2048]{1,0:T(8,128)(2,1)}, bf16[256,2048]{1,0:T(8,128)(2,1)}, u32[]{:S(2)}, u32[]{:S(2)}) collective-permute-start(bf16[256,2048]{1,0:T(8,128)(2,1)} %add_convert_fusion.1), channel_id=1, source_target_pairs={{0,8},{8,16},{16,24},{24,0},{1,9},{9,17},{17,25},{25,1},{2,10},{10... | collective-permute-start | bytes 3145736 | tf_op jit(solution)/shard_map/ppermute | solution.py:269
  824.0 83.5 %all-to-all-start.4 = ((bf16[8,64,768]{2,1,0:T(8,128)(2,1)}), bf16[8,64,768]{2,1,0:T(8,128)(2,1)S(1)}, u32[]{:S(2)}, u32[]{:S(2)}) async-start(bf16[8,64,768]{2,1,0:T(8,128)(2,1)} %bitcast.365), calls=%async_computation.5 | async-start | bytes 1572864 | tf_op jit(solution)/shard_map/all_to_all | solution.py:288
  837.0 82.2 %collective-permute-start.17 = (bf16[256,2048]{1,0:T(8,128)(2,1)}, bf16[256,2048]{1,0:T(8,128)(2,1)}, u32[]{:S(2)}, u32[]{:S(2)}) collective-permute-start(bf16[256,2048]{1,0:T(8,128)(2,1)} %slice.303), channel_id=1, source_target_pairs={{0,1},{1,0},{2,3},{3,2},{4,5},{5,4},{6,7},{7,6},{8,9},{9,8},{10,11... | collective-permute-start | bytes 3145736 | tf_op jit(solution)/shard_map/ppermute | solution.py:272
  840.5 84.9 %collective-permute-start.41 = (bf16[256,2048]{1,0:T(8,128)(2,1)}, bf16[256,2048]{1,0:T(8,128)(2,1)}, u32[]{:S(2)}, u32[]{:S(2)}) collective-permute-start(bf16[256,2048]{1,0:T(8,128)(2,1)} %slice.327), channel_id=1, source_target_pairs={{0,1},{1,0},{2,3},{3,2},{4,5},{5,4},{6,7},{7,6},{8,9},{9,8},{10,11... | collective-permute-start | bytes 3145736 | tf_op jit(solution)/shard_map/ppermute | solution.py:272
  870.6 54.7 %collective-permute-start.40 = (bf16[256,2048]{1,0:T(8,128)(2,1)}, bf16[256,2048]{1,0:T(8,128)(2,1)}, u32[]{:S(2)}, u32[]{:S(2)}) collective-permute-start(bf16[256,2048]{1,0:T(8,128)(2,1)} %add_convert_fusion), channel_id=1, source_target_pairs={{0,8},{8,16},{16,24},{24,0},{1,9},{9,17},{17,25},{25,1},{2,10},{10... | collective-permute-start | bytes 3145736 | tf_op jit(solution)/shard_map/ppermute | solution.py:269
  908.5 82.0 %all-to-all-start.5 = ((bf16[8,64,2048]{2,1,0:T(8,128)(2,1)}), bf16[8,64,2048]{2,1,0:T(8,128)(2,1)}, u32[]{:S(2)}, u32[]{:S(2)}) async-start(bf16[8,64,2048]{2,1,0:T(8,128)(2,1)} %bitcast.336), calls=%async_computation.8 | async-start | bytes 4194304 | tf_op jit(solution)/shard_map/all_to_all | solution.py:288
  923.8 49.9 %collective-permute-start.18 = (bf16[256,2048]{1,0:T(8,128)(2,1)}, bf16[256,2048]{1,0:T(8,128)(2,1)}, u32[]{:S(2)}, u32[]{:S(2)}) collective-permute-start(bf16[256,2048]{1,0:T(8,128)(2,1)} %add_convert_fusion.7), channel_id=1, source_target_pairs={{0,8},{8,16},{16,24},{24,0},{1,9},{9,17},{17,25},{25,1},{2,10},{10... | collective-permute-start | bytes 3145736 | tf_op jit(solution)/shard_map/ppermute | solution.py:269
  942.4 40.3 %collective-permute-start.49 = (bf16[64,2048]{1,0:T(8,128)(2,1)}, bf16[64,2048]{1,0:T(8,128)(2,1)S(1)}, u32[]{:S(2)}, u32[]{:S(2)}) collective-permute-start(bf16[64,2048]{1,0:T(8,128)(2,1)} %reduce-scatter.7.cloned.1.call-done), channel_id=1, source_target_pairs={{0,0},{1,4},{2,1},{3,5},{4,2},{5,6},{6,3},{7,7},{8,8},{9,12},{10,9... | collective-permute-start | bytes 786440 | tf_op jit(solution)/shard_map/ppermute | solution.py:406
  (119 other events, 2005.0 us)
Sparse Core Ops, SparseCore 0:
  39.6 43.1 all-gather.4
  85.7 106.8 all-gather.6
  194.4 85.3 all-gather.8
  281.5 52.6 all-gather.10
  639.0 42.9 reduce-scatter.4
  685.2 86.0 reduce-scatter.8
  774.4 27.7 reduce-scatter.6
  805.2 52.6 reduce-scatter.10

commit v2 on v1

--- a/solution.py
+++ b/solution.py
@@ -16,6 +16,7 @@
 ROPE_BASE = 130000.0
 BF = jnp.bfloat16
 F32 = jnp.float32
+QUICK = pl.CostEstimate(flops=1, bytes_accessed=1, transcendentals=0)
 
 
 def dot(left, right, dims):
@@ -49,7 +50,7 @@
     return key <= query
 
 
-def attend_kernel(heads, ring, where_ref, qkv_ref, send_ref, keep_ref, lse_ref, key_ref, vt_ref, ot_ref):
+def attend_kernel(heads, ring, where_ref, qkv_ref, send_ref, lse_ref, key_ref, vt_ref, ot_ref):
     rows, width = qkv_ref.shape[1], qkv_ref.shape[2] // 3
     block = pl.program_id(1)
     z = where_ref[0]
@@ -85,9 +86,7 @@
                 out = out + mm(vt_ref[at, :done], (past * share).astype(BF))
             ot_ref[at] = out
             lse_ref[head : head + 1] = top + jnp.log(total)
-        out = ot_ref[...].T.astype(BF)
-        send_ref[...] = out
-        keep_ref[...] = out
+        send_ref[...] = ot_ref[...].T.astype(BF)
 
     for p in range(ring):
         pl.when(block == p)(functools.partial(one, p))
@@ -100,7 +99,6 @@
         functools.partial(attend_kernel, heads, ring),
         out_shape=(
             jax.ShapeDtypeStruct((ring * pair, rows, width), BF),
-            jax.ShapeDtypeStruct((ring, pair, rows, width), BF),
             jax.ShapeDtypeStruct((pair, ring, heads, rows), F32),
         ),
         grid_spec=pltpu.PrefetchScalarGridSpec(
@@ -109,7 +107,6 @@
             in_specs=[pl.BlockSpec((ring, None, rows, full), lambda i, p, w: (0, i, 0, 0))],
             out_specs=[
                 pl.BlockSpec((None, rows, width), lambda i, p, w: (p * pair + lax.rem(w[1] + i, pair), 0, 0)),
-                pl.BlockSpec((None, None, rows, width), lambda i, p, w: (lax.rem(w[0] - p + ring, ring), i, 0, 0)),
                 pl.BlockSpec((None, None, heads, rows), lambda i, p, w: (i, p, 0, 0)),
             ],
             scratch_shapes=[
@@ -119,11 +116,7 @@
             ],
         ),
         compiler_params=pltpu.CompilerParams(vmem_limit_bytes=48 << 20),
-        cost_estimate=pl.CostEstimate(
-            flops=2 * 2 * pair * heads * (ring * rows) ** 2 * width * 5 // 8,
-            bytes_accessed=2 * qkv.size * 2,
-            transcendentals=pair * heads * (ring * rows) ** 2,
-        ),
+        cost_estimate=pl.CostEstimate(flops=20 * 10**9, bytes_accessed=2 * qkv.size * 2, transcendentals=0),
         name="attend",
     )(where, qkv)
 
@@ -232,13 +225,253 @@
             ],
         ),
         compiler_params=pltpu.CompilerParams(vmem_limit_bytes=52 << 20),
-        cost_estimate=pl.CostEstimate(
-            flops=5 * 2 * pair * heads * (ring * rows) ** 2 * width * 5 // 8,
-            bytes_accessed=4 * qkv.size * 2,
-            transcendentals=pair * heads * (ring * rows) ** 2,
-        ),
+        cost_estimate=pl.CostEstimate(flops=28 * 10**9, bytes_accessed=4 * qkv.size * 2, transcendentals=0),
         name="attend_back",
     )(where, qkv, datt, lse, cosine, sine)
+
+
+def feed_kernel(
+    steps, two_ref, two_other_ref, dout_ref, dout_other_ref, ff_in_ref, down_in_ref, ff_back_ref, down_out_ref, *refs,
+):
+    x_ref, dy_ref, hidden_ref, dff_ref, out_ref, out_other_ref, back_ref, back_other_ref = refs[-8:]
+    rows = two_ref.shape[0]
+    chunk = down_in_ref.shape[0]
+    step = pl.program_id(0)
+
+    @pl.when(step == 0)
+    def _():
+        x_ref[:rows], x_ref[rows:] = two_ref[...], two_other_ref[...]
+        dy_ref[:rows], dy_ref[rows:] = dout_ref[...], dout_other_ref[...]
+
+    def hidden_units(j):
+        both = mm(x_ref[...], ff_in_ref[...])
+        dhid = mm_nt(dy_ref[...], down_in_ref[...])
+        gate, up = both[:, :chunk], both[:, chunk:]
+        sig = jax.nn.sigmoid(gate)
+        act = gate * sig
+        hidden_ref[:, j * chunk : (j + 1) * chunk] = (act * up).astype(BF)
+        dgate = dhid * up * (sig * (1.0 + gate * (1.0 - sig)))
+        dff_ref[:, 2 * j * chunk : (2 * j + 1) * chunk] = dgate.astype(BF)
+        dff_ref[:, (2 * j + 1) * chunk : (2 * j + 2) * chunk] = (dhid * act).astype(BF)
+
+    for j in range(steps):
+        pl.when(step == j)(functools.partial(hidden_units, j))
+
+    @pl.when(step >= steps)
+    def _():
+        out = mm(hidden_ref[...], down_out_ref[...]).astype(BF)
+        out_ref[...], out_other_ref[...] = out[:rows], out[rows:]
+        back = mm_nt(dff_ref[...], ff_back_ref[...]).astype(BF)
+        back_ref[...], back_other_ref[...] = back[:rows], back[rows:]
+
+
+def feed(k, blocks, kept, two, two_other, dout, dout_other, ff_w, down_w, chunk):
+    rows, model = two.shape
+    ff = down_w.shape[0]
+    steps = ff // chunk
+    part = model // steps
+    whole = pl.BlockSpec((rows, model), lambda j: (0, 0))
+    share = pl.BlockSpec((rows, part), lambda j: (0, jnp.maximum(j - steps, 0)))
+    widths = (model, model, ff, 2 * ff)
+    *kept, out, out_other, back, back_other = pl.pallas_call(
+        functools.partial(feed_kernel, steps),
+        out_shape=[jax.ShapeDtypeStruct((blocks * 2 * rows, w), BF) for w in widths] + [jax.ShapeDtypeStruct((rows, model), BF)] * 4,
+        grid=(2 * steps,),
+        in_specs=[
+            whole, whole, whole, whole,
+            pl.BlockSpec((model, 2 * chunk), lambda j: (0, jnp.minimum(j, steps - 1))),
+            pl.BlockSpec((chunk, model), lambda j: (jnp.minimum(j, steps - 1), 0)),
+            pl.BlockSpec((part, 2 * ff), lambda j: (jnp.maximum(j - steps, 0), 0)),
+            pl.BlockSpec((ff, part), lambda j: (0, jnp.maximum(j - steps, 0))),
+        ] + [pl.BlockSpec(memory_space=pl.ANY)] * len(kept),
+        out_specs=[pl.BlockSpec((2 * rows, w), lambda j: (k, 0)) for w in widths] + [share] * 4,
+        input_output_aliases={8 + i: i for i in range(len(kept))},
+        compiler_params=pltpu.CompilerParams(vmem_limit_bytes=56 << 20),
+        cost_estimate=pl.CostEstimate(flops=2 * rows * model * ff * 6, bytes_accessed=1, transcendentals=0),
+        name="feed",
+    )(two, two_other, dout, dout_other, ff_w, down_w, ff_w, down_w, *kept)
+    return kept, (out, out_other), (back, back_other)
+
+
+def project_kernel(where_ref, one_ref, other_ref, w_ref, cos_ref, sin_ref, *refs):
+    x_ref, out_ref = refs[-2:]
+    rows = one_ref.shape[0]
+    half = w_ref.shape[1] // 2
+    step = pl.program_id(0)
+
+    @pl.when(step == 0)
+    def _():
+        x_ref[:rows], x_ref[rows:] = one_ref[...], other_ref[...]
+
+    flat = mm(x_ref[...], w_ref[...])
+
+    @pl.when(step < 2)
+    def _():
+        cosine, sine = cos_ref[...], sin_ref[...]
+        for i in range(2):
+            first, second = flat[i * rows : (i + 1) * rows, :half], flat[i * rows : (i + 1) * rows, half:]
+            out_ref[i, :, :half] = (first * cosine - second * sine).astype(BF)
+            out_ref[i, :, half:] = (second * cosine + first * sine).astype(BF)
+
+    @pl.when(step == 2)
+    def _():
+        out_ref[0], out_ref[1] = flat[:rows].astype(BF), flat[rows:].astype(BF)
+
+
+def project(k, blocks, kept, where, one, other, w, cosine, sine):
+    rows, model = one.shape
+    width = w.shape[1] // 3
+    whole = pl.BlockSpec((rows, model), lambda j, at: (0, 0))
+    table = pl.BlockSpec((rows, width // 2), lambda j, at: (lax.rem(at[0] - k + blocks, blocks), 0))
+    return pl.pallas_call(
+        project_kernel,
+        out_shape=(
+            jax.ShapeDtypeStruct((blocks * 2 * rows, model), BF),
+            jax.ShapeDtypeStruct((blocks, 2, rows, 3 * width), BF),
+        ),
+        grid_spec=pltpu.PrefetchScalarGridSpec(
+            num_scalar_prefetch=1,
+            grid=(3,),
+            in_specs=[whole, whole, pl.BlockSpec((model, width), lambda j, at: (0, j)), table, table]
+            + [pl.BlockSpec(memory_space=pl.ANY)] * len(kept),
+            out_specs=(
+                pl.BlockSpec((2 * rows, model), lambda j, at: (k, 0)),
+                pl.BlockSpec((None, 2, rows, width), lambda j, at: (k, 0, 0, j)),
+            ),
+        ),
+        input_output_aliases={6 + i: i for i in range(len(kept))},
+        compiler_params=pltpu.CompilerParams(vmem_limit_bytes=40 << 20),
+        cost_estimate=QUICK,
+        name="project",
+    )(where, one, other, w, cosine, sine, *kept)
+
+
+def ff_out_kernel(turn, gain_ref, gate_ref, up_ref, out_ref):
+    pair = out_ref.shape[0]
+    gain = gain_ref[...]
+    for y in range(out_ref.shape[2] // (2 * turn)):
+        for c in range(pair):
+            at = (y * pair + c) * turn
+            for i, ref in enumerate((gate_ref, up_ref)):
+                cols = (ref[:, at : at + turn].astype(F32) * gain).astype(BF)
+                out_ref[c, :, (2 * y + i) * turn : (2 * y + i + 1) * turn] = cols
+
+
+def ff_out(ring, pair, turn, gain, w_gate, w_up):
+    own, full = w_gate.shape
+    part = pl.BlockSpec((own, full // ring), lambda s: (0, s))
+    return pl.pallas_call(
+        functools.partial(ff_out_kernel, turn),
+        out_shape=jax.ShapeDtypeStruct((ring * pair, own, 2 * full // (ring * pair)), BF),
+        grid=(ring,),
+        in_specs=[pl.BlockSpec((own, 1), lambda s: (0, 0)), part, part],
+        out_specs=pl.BlockSpec((pair, own, 2 * full // (ring * pair)), lambda s: (s, 0, 0)),
+        cost_estimate=pl.CostEstimate(flops=1, bytes_accessed=8 * w_gate.size, transcendentals=0),
+        name="ff_out",
+    )(gain, w_gate, w_up)
+
+
+def ff_back_kernel(turn, gain_ref, hat_ref, gate_ref, up_ref, gate_out, up_out, sum_ref):
+    pair = hat_ref.shape[0]
+    gain = gain_ref[...]
+    total = jnp.zeros(gain.shape, F32)
+    for y in range(hat_ref.shape[2] // (2 * turn)):
+        for c in range(pair):
+            at = (y * pair + c) * turn
+            for i, (ref, out) in enumerate(((gate_ref, gate_out), (up_ref, up_out))):
+                hat = hat_ref[c, :, (2 * y + i) * turn : (2 * y + i + 1) * turn].astype(F32)
+                total += jnp.sum(hat * ref[:, at : at + turn].astype(F32), axis=1, keepdims=True)
+                out[:, at : at + turn] = hat * gain
+
+    @pl.when(pl.program_id(0) == 0)
+    def _():
+        sum_ref[...] = total
+
+    @pl.when(pl.program_id(0) > 0)
+    def _():
+        sum_ref[...] += total
+
+
+def ff_back(ring, turn, gain, hat, w_gate, w_up):
+    own, full = w_gate.shape
+    pair = hat.shape[0] // ring
+    part = pl.BlockSpec((own, full // ring), lambda s: (0, s))
+    column = pl.BlockSpec((own, 1), lambda s: (0, 0))
+    return pl.pallas_call(
+        functools.partial(ff_back_kernel, turn),
+        out_shape=(jax.ShapeDtypeStruct((own, full), F32),) * 2 + (jax.ShapeDtypeStruct((own, 1), F32),),
+        grid=(ring,),
+        in_specs=[column, pl.BlockSpec((pair, *hat.shape[1:]), lambda s: (s, 0, 0)), part, part],
+        out_specs=(part, part, column),
+        cost_estimate=pl.CostEstimate(flops=1, bytes_accessed=16 * w_gate.size, transcendentals=0),
+        name="ff_back",
+    )(gain, hat, w_gate, w_up)
+
+
+def qkv_out_kernel(gain_ref, query_ref, key_ref, value_ref, out_ref):
+    width = query_ref.shape[1]
+    gain = gain_ref[...]
+    for i, ref in enumerate((query_ref, key_ref)):
+        cols = ref[...].astype(F32) * gain
+        parts = [cols[:, j : j + HALF] for start in (0, HALF) for j in range(start, width, HEAD_DIM)]
+        out_ref[:, i * width : (i + 1) * width] = jnp.concatenate(parts, axis=1).astype(BF)
+    out_ref[:, 2 * width :] = (value_ref[...].astype(F32) * gain).astype(BF)
+
+
+def qkv_out(parts, gain, *ws):
+    own, full = ws[0].shape
+    width = full // parts
+    return pl.pallas_call(
+        qkv_out_kernel,
+        out_shape=jax.ShapeDtypeStruct((parts, own, 3 * width), BF),
+        grid=(parts,),
+        in_specs=[pl.BlockSpec((own, 1), lambda t: (0, 0))] + [pl.BlockSpec((own, width), lambda t: (0, t))] * 3,
+        out_specs=pl.BlockSpec((None, own, 3 * width), lambda t: (t, 0, 0)),
+        cost_estimate=pl.CostEstimate(flops=1, bytes_accessed=12 * ws[0].size, transcendentals=0),
+        name="qkv_out",
+    )(gain, *ws)
+
+
+def qkv_back_kernel(gain_ref, hat_ref, query_ref, key_ref, value_ref, query_out, key_out, value_out, sum_ref):
+    width = query_ref.shape[1]
+    gain = gain_ref[...]
+    total = jnp.zeros(gain.shape, F32)
+    for i, (ref, out) in enumerate(((query_ref, query_out), (key_ref, key_out), (value_ref, value_out))):
+        hat = hat_ref[:, i * width : (i + 1) * width].astype(F32)
+        if i < 2:
+            parts = [hat[:, j : j + HALF] for at in range(0, width // 2, HALF) for j in (at, width // 2 + at)]
+            hat = jnp.concatenate(parts, axis=1)
+        total += jnp.sum(hat * ref[...].astype(F32), axis=1, keepdims=True)
+        out[...] = hat * gain
+
+    @pl.when(pl.program_id(0) == 0)
+    def _():
+        sum_ref[...] = total
+
+    @pl.when(pl.program_id(0) > 0)
+    def _():
+        sum_ref[...] += total
+
+
+def qkv_back(gain, hat, *ws):
+    own, full = ws[0].shape
+    parts = hat.shape[0]
+    width = full // parts
+    part = pl.BlockSpec((own, width), lambda t: (0, t))
+    column = pl.BlockSpec((own, 1), lambda t: (0, 0))
+    return pl.pallas_call(
+        qkv_back_kernel,
+        out_shape=(jax.ShapeDtypeStruct((own, full), F32),) * 3 + (jax.ShapeDtypeStruct((own, 1), F32),),
+        grid=(parts,),
+        in_specs=[column, pl.BlockSpec((None, own, 3 * width), lambda t: (t, 0, 0)), part, part, part],
+        out_specs=(part, part, part, column),
+        cost_estimate=pl.CostEstimate(flops=1, bytes_accessed=24 * ws[0].size, transcendentals=0),
+        name="qkv_back",
+    )(gain, hat, *ws)
+
+
+def after(value, *others):
+    return lax.optimization_barrier((value, *others))[0] if others else value
 
 
 def unit(values):
@@ -261,7 +494,8 @@
     ff = plane * ff_own
     group = ("seq", "core")
     z = lax.axis_index("seq")
-    where = jnp.stack([z, lax.axis_index("core")]).astype(jnp.int32)
+    c = lax.axis_index("core")
+    where = jnp.stack([z, c]).astype(jnp.int32)
     ring_pairs = [(i, (i + 1) % ring) for i in range(ring)]
     core_pairs = [(i, (i + 1) % pair) for i in range(pair)]
 
@@ -271,163 +505,152 @@
     def swap(x):
         return lax.ppermute(x, "core", core_pairs)
 
-    def ring_gather(x):
-        blocks = [x]
-        for _ in range(ring - 1):
-            blocks.append(hop(blocks[-1]))
-        return [jnp.stack([b, swap(b)]) for b in blocks]
-
-    def ring_sum(terms):
-        shares = [t[0].astype(F32) + swap(t[1]).astype(F32) for t in terms]
+    def ring_sum(shares, *fill):
         total = shares[1].astype(BF)
         for k in range(2, ring):
             total = (hop(total).astype(F32) + shares[k]).astype(BF)
+            total = after(total, *fill[k - 2 : k - 1])
         return hop(total).astype(F32) + shares[0]
+
+    def both_cores(term):
+        return term[0].astype(F32) + swap(term[1]).astype(F32)
 
     def exchange(x):
         return lax.all_to_all(x, group, 0, 0, tiled=True)
 
-    def plane_gather(x):
-        return lax.all_gather(x, "yx", axis=0, tiled=True)
-
-    def plane_sum(x):
-        return lax.psum_scatter(x.astype(BF), "yx", scatter_dimension=0, tiled=True)
-
-    def to_rows(x):
-        return x.reshape(rows, ring, plane, pair * own).transpose(0, 2, 1, 3).reshape(rows, model)
-
-    def from_rows(x):
-        return x.reshape(rows, plane, ring, pair * own).transpose(0, 2, 1, 3).reshape(rows, model)
-
-    def halves_out(w):
-        return w.reshape(own, parts, heads, 2, HALF).transpose(1, 0, 3, 2, 4).reshape(parts, own, width)
-
-    def halves_back(w):
-        return w.reshape(parts, own, 2, heads, HALF).transpose(1, 0, 3, 2, 4).reshape(own, model)
-
-    def heads_out(w):
-        return w.reshape(own, parts, width).transpose(1, 0, 2)
-
-    def heads_back(w):
-        return w.transpose(1, 0, 2).reshape(own, model)
-
-    def ff_out(w):
-        return w.reshape(own, ring, plane, pair, ff_own).transpose(1, 3, 0, 2, 4).reshape(parts, own, ff)
-
-    def ff_back(w):
-        return w.reshape(ring, pair, own, plane, ff_own).transpose(2, 0, 3, 1, 4).reshape(own, parts * ff)
+    def exchange_rows(x):
+        return exchange(x).reshape(ring, pair * own, x.shape[2])
+
+    def gather_rows(x):
+        return lax.all_gather(x, "yx", axis=1, tiled=True).reshape(model, x.shape[2])
+
+    def sum_rows(x):
+        x = x.reshape(ring, plane * pair * own, x.shape[1])
+        return lax.psum_scatter(x, "yx", scatter_dimension=1, tiled=True)
+
+    def return_rows(x):
+        return exchange(x.reshape(parts, own, x.shape[2]))
 
     gain_one, gain_two = norm1_gain.astype(F32)[:, None], norm2_gain.astype(F32)[:, None]
-
-    def scaled(w, gain):
-        return (w.astype(F32) * gain).astype(BF)
-
-    qkv_w = exchange(
-        jnp.concatenate(
-            [halves_out(scaled(w_query, gain_one)), halves_out(scaled(w_key, gain_one)), heads_out(scaled(w_value, gain_one))],
-            axis=2,
-        )
-    )
-    qkv_w = plane_gather(qkv_w.reshape(parts * own, 3 * width))
-    down_w = plane_gather(w_down)
-    output_w = lax.all_gather(w_output, ("seq", "yx", "core"), axis=0, tiled=True)
-    ff_w = exchange(jnp.concatenate([ff_out(scaled(w_gate, gain_two)), ff_out(scaled(w_up, gain_two))], axis=2))
-    ff_w = plane_gather(ff_w.reshape(parts * own, 2 * ff))
 
     residual = inputs.reshape(rows, model).astype(F32)
     normed_one, inverse_one = unit(residual)
-    ones = ring_gather(to_rows(normed_one.astype(BF)))
+    one = normed_one.astype(BF)
+    qkv_w = qkv_out(parts, gain_one, w_query, w_key, w_value)
+    ff_w = ff_out(ring, pair, ff_own, gain_two, w_gate, w_up)
+    down_w = lax.all_gather(w_down, "yx", axis=0, tiled=True)
+    ones = [one, hop(one)]
+    qkv_w = exchange_rows(after(qkv_w, ones[1]))
+    for k in range(1, ring - 1):
+        ones.append(hop(after(ones[k], qkv_w if k == 1 else ff_w)))
+    qkv_w = gather_rows(after(qkv_w, down_w))
+    ff_w = exchange_rows(after(ff_w, ones[-1]))
+    output_w = lax.all_gather(after(w_output, ones[1]), ("seq", "yx", "core"), axis=0, tiled=True)
 
     freqs = jnp.exp(jnp.arange(HALF, dtype=F32) * (-2.0 * math.log(ROPE_BASE) / HEAD_DIM))
     angle = jnp.arange(ring * rows, dtype=jnp.int32).astype(F32)[:, None] * freqs[None, :]
     cosine, sine = jnp.tile(jnp.cos(angle), (1, heads)), jnp.tile(jnp.sin(angle), (1, heads))
-    qkv = []
+    kept = []
     for k in range(ring):
-        start = lax.rem(z - k + ring, ring) * rows
-        cos_k = lax.dynamic_slice_in_dim(cosine, start, rows)
-        sin_k = lax.dynamic_slice_in_dim(sine, start, rows)
-        flat = mm(ones[k].reshape(pair * rows, model), qkv_w).reshape(pair, rows, 3 * width)
-        q1, q2 = flat[..., :half], flat[..., half:width]
-        k1, k2 = flat[..., width : width + half], flat[..., width + half : 2 * width]
-        qkv.append(
-            jnp.concatenate(
-                [
-                    q1 * cos_k - q2 * sin_k,
-                    q2 * cos_k + q1 * sin_k,
-                    k1 * cos_k - k2 * sin_k,
-                    k2 * cos_k + k1 * sin_k,
-                    flat[..., 2 * width :],
-                ],
-                axis=-1,
-            ).astype(BF)
-        )
-    qkv = jnp.stack(qkv)
-    att_send, att_keep, lse = attend(qkv, where, heads)
+        kept = project(k, ring, kept, where, ones[k], swap(ones[k]), qkv_w, cosine, sine)
+    all_ones, qkv = kept
+    att_send, lse = attend(qkv, where, heads)
+    att_send, ff_w = lax.optimization_barrier((att_send, ff_w))
+    ff_w = gather_rows(ff_w)
     att = exchange(att_send).transpose(1, 0, 2).reshape(rows, model)
     mid = residual + mm(att, output_w)
 
     normed_two, inverse_two = unit(mid)
-    twos = ring_gather(to_rows(normed_two.astype(BF)))
+    twos = [normed_two.astype(BF)]
     grad_out = out_grad.reshape(rows, model)
-    douts = ring_gather(grad_out)
-    out_terms, two_terms, hiddens, dffs = [], [], [], []
-    for k in range(ring):
-        two, dout = twos[k].reshape(pair * rows, model), douts[k].reshape(pair * rows, model)
-        both = mm(two, ff_w)
-        gate, up = both[:, :ff], both[:, ff:]
-        sig = jax.nn.sigmoid(gate)
-        hidden = (gate * sig * up).astype(BF)
-        out_terms.append(mm(hidden, down_w).astype(BF).reshape(pair, rows, model))
-        dhid = mm_nt(dout, down_w)
-        dgate = (dhid * up * sig * (1.0 + gate * (1.0 - sig))).astype(BF)
-        dup = (dhid * gate * sig).astype(BF)
-        dff = jnp.concatenate([dgate, dup], axis=1)
-        two_terms.append(mm_nt(dff, ff_w).astype(BF).reshape(pair, rows, model))
-        hiddens.append(hidden)
-        dffs.append(dff)
-    grad_two = from_rows(ring_sum(two_terms))
-    output = (mid + ring_sum(out_terms)).astype(BF).reshape(inputs.shape)
+    douts = [grad_out, hop(after(grad_out, att))]
+    for k in range(1, ring):
+        twos.append(hop(twos[-1]))
+        if k < ring - 1:
+            douts.append(hop(after(douts[-1], att if k == 1 else twos[k - 1])))
+    kept, out_terms = [], [None] * ring
+    for k in [1, 0, *range(2, ring)]:
+        if k == 2:
+            total = first_share
+        two = after(twos[k], total) if k > 1 else twos[k]
+        kept, out_terms[k], back = feed(k, ring, kept, two, swap(twos[k]), douts[k], swap(douts[k]), ff_w, down_w, ff_own)
+        if k == 0:
+            own_share = both_cores(back)
+        elif k == 1:
+            first_share = both_cores(back).astype(BF)
+        else:
+            here = hop(total).astype(F32) + back[0].astype(F32)
+            if k == ring - 1:
+                all_twos, all_douts, hiddens, dffs = kept
+                ff_grad = mm_tn(after(all_twos, total), dffs).astype(BF)
+                here = after(here, ff_grad)
+            else:
+                here = after(here, own_share)
+            total = (here + swap(back[1]).astype(F32)).astype(BF)
     tokens = ring * pair * rows
-    twos, douts = jnp.stack(twos).reshape(tokens, model), jnp.stack(douts).reshape(tokens, model)
-    down_grad = plane_sum(mm_tn(jnp.concatenate(hiddens), douts)).astype(F32)
-    ff_grad = plane_sum(mm_tn(twos, jnp.concatenate(dffs)))
-    ff_grad = exchange(ff_grad.reshape(parts, own, 2 * ff)).astype(F32)
-    gate_hat, up_hat = ff_back(ff_grad[..., :ff]), ff_back(ff_grad[..., ff:])
-    gain_two_grad = jnp.sum(w_gate.astype(F32) * gate_hat + w_up.astype(F32) * up_hat, axis=1)
+    ff_grad = sum_rows(after(ff_grad, total))
+    down_grad = mm_tn(hiddens, after(all_douts, total)).astype(BF)
+    grad_two = after(hop(total).astype(F32) + own_share, down_grad)
 
     grad_mid = grad_out.astype(F32) + unit_back(grad_two, normed_two, inverse_two)
     proj = grad_mid.astype(BF)
     datt = mm_nt(proj, output_w).astype(BF)
-    datt = exchange(datt.reshape(rows, parts, width).transpose(1, 0, 2))
+    shares = [both_cores(after(t, grad_two)) for t in out_terms]
+    total = (hop(shares[1].astype(BF)).astype(F32) + shares[2]).astype(BF)
+    datt = datt.reshape(rows, parts, width).transpose(1, 0, 2)
+
+    split = model // pair
+    mine = lax.dynamic_slice_in_dim(att, c * split, split, axis=1)
+    others = swap(lax.dynamic_slice_in_dim(att, (pair - 1 - c) * split, split, axis=1))
+    output_grad = mm_tn(jnp.concatenate([mine, others]), jnp.concatenate([proj, swap(proj)])).astype(BF)
+    datt = after(exchange(after(datt, total)), output_grad)
+    output_grad = lax.psum_scatter(output_grad, "yx", scatter_dimension=0, tiled=True)
     dqkv = attend_back(qkv, datt, lse, cosine, sine, where, heads)
-    projs = jnp.stack(ring_gather(proj)).reshape(tokens, model)
-    output_grad = plane_sum(mm_tn(att_keep.reshape(tokens, width), projs)).astype(BF)
-    moves = [(y * pair + c, c * plane + y) for y in range(plane) for c in range(pair)]
-    output_grad = lax.ppermute(output_grad, ("yx", "core"), moves).astype(F32)
-
-    one_terms = [mm_nt(dqkv[k].reshape(pair * rows, 3 * width), qkv_w).astype(BF).reshape(pair, rows, model) for k in range(ring)]
-    ones = jnp.stack(ones).reshape(tokens, model)
-    qkv_grad = plane_sum(mm_tn(ones, dqkv.reshape(tokens, 3 * width)))
-    qkv_grad = exchange(qkv_grad.reshape(parts, own, 3 * width)).astype(F32)
-    query_hat = halves_back(qkv_grad[..., :width])
-    key_hat = halves_back(qkv_grad[..., width : 2 * width])
-    value_hat = heads_back(qkv_grad[..., 2 * width :])
-    gain_one_grad = jnp.sum(
-        w_query.astype(F32) * query_hat + w_key.astype(F32) * key_hat + w_value.astype(F32) * value_hat, axis=1
+    total = after(total, datt)
+    for k in range(3, ring):
+        total = (hop(total).astype(F32) + shares[k]).astype(BF)
+    dqkv = after(dqkv, ff_grad, total)
+    output = (mid + (hop(total).astype(F32) + shares[0])).astype(BF).reshape(inputs.shape)
+    ff_grad = return_rows(ff_grad)
+    gate_grad, up_grad, gain_two_grad = ff_back(ring, ff_own, gain_two, ff_grad, w_gate, w_up)
+
+    qkv_grad = mm_tn(all_ones, dqkv.reshape(tokens, 3 * width)).astype(BF)
+    dqkv = after(dqkv, qkv_grad)
+    down_grad = lax.psum_scatter(after(down_grad, qkv_grad), "yx", scatter_dimension=0, tiled=True).astype(F32)
+    qkv_grad = sum_rows(qkv_grad)
+    one_terms = [[mm_nt(dqkv[k, i], qkv_w).astype(BF) for i in range(pair)] for k in range(ring)]
+    shares = [both_cores(t) for t in one_terms]
+    total = after(shares[1].astype(BF), output, ff_grad)
+    qkv_grad = return_rows(after(qkv_grad, output))
+    total = after((hop(total).astype(F32) + shares[2]).astype(BF), qkv_grad)
+    output_grad = after(output_grad, total)
+    output_grad = output_grad.reshape(ring, own, model)
+    output_grad = ring_sum(
+        [lax.dynamic_index_in_dim(output_grad, lax.rem(z - k + ring, ring), keepdims=False).astype(F32) for k in range(ring)]
+    ).astype(BF)
+    moves = [((s * plane + y) * pair + h, (h * plane + y) * ring + s) for s in range(ring) for y in range(plane) for h in range(pair)]
+    output_grad = lax.ppermute(output_grad, ("seq", "yx", "core"), moves).astype(F32)
+
+    query_grad, key_grad, value_grad, gain_one_grad = qkv_back(gain_one, qkv_grad, w_query, w_key, w_value)
+    for k in range(3, ring):
+        total = (hop(total).astype(F32) + shares[k]).astype(BF)
+    total = after(total, qkv_grad)
+    total, gate_grad, up_grad, gain_two_grad, output_grad = lax.optimization_barrier(
+        (total, gate_grad, up_grad, gain_two_grad, output_grad)
     )
-    grad_one = from_rows(ring_sum(one_terms))
+    grad_one = hop(total).astype(F32) + shares[0]
     input_grad = (grad_mid + unit_back(grad_one, normed_one, inverse_one)).reshape(inputs.shape)
     return (
         output,
         input_grad,
-        gain_one_grad,
-        query_hat * gain_one,
-        key_hat * gain_one,
-        value_hat * gain_one,
+        gain_one_grad[:, 0],
+        query_grad,
+        key_grad,
+        value_grad,
         output_grad,
-        gain_two_grad,
-        gate_hat * gain_two,
-        up_hat * gain_two,
+        gain_two_grad[:, 0],
+        gate_grad,
+        up_grad,
         down_grad,
     )
 

time: 1040 us -> 850 us (0.82)
  Pallas kernels: 45.4 us -> 182 us
  local copies, waits for them, and re-layouts: 125 us -> 22.7 us
  matrix products: 188 us -> 86.1 us
  other arithmetic: 108 us -> 41.8 us
  starting transfers between devices: 109 us -> 66.2 us
    pallas_call x0 -> x12, Pallas kernels: none -> 137 us  [the longest x4 93.2 us: feed(): pl.pallas_call(functools.partial(feed_kernel, steps), out_shape=[jax.Shap...]
    dot_general x30 -> x14, matrix products: 188 us -> 86.1 us  [dot(): lax.dot_general(left, right, (dims, ((), ())), preferred_element_type=F32)]
    ppermute x28 -> x26, starting transfers between devices: 74.4 us -> 17.1 us  [swap(): return lax.ppermute(x, 'core', core_pairs)]
    another operation x20 -> x1, other arithmetic: 51.8 us -> 0.07 us  [local(): where = jnp.stack([z, c]).astype(jnp.int32)]
    reshape x21 -> x1, local copies, waits for them, and re-layouts: 45.9 us -> 1.31 us  [local(): datt = datt.reshape(rows, parts, width).transpose(1, 0, 2)]
    all_gather x4, waiting for transfers between devices: 0.01 us -> 34.4 us  [the longest x2 32.4 us: gather_rows(): lax.all_gather(x, 'yx', axis=1, tiled=True).reshape(model, x.shape[2])]
    ppermute x21, waiting for transfers between devices: 301 us -> 270 us  [hop(): return lax.ppermute(x, 'seq', ring_pairs)]
    another operation x6 -> x0, local copies, waits for them, and re-layouts: 28.6 us -> none  [the longest x5 16.9 us: ring_gather(): return [jnp.stack([b, swap(b)]) for b in blocks]]
  transfers between devices with their start and end apart: 62 -> 60, of which waited for: 17 -> 24; matrix products, arithmetic and copies ran while one was open for 32% -> 14% of each run, Pallas kernels for 2% -> 22%
where the time goes in v2:
time: 850 us; the launch traced here: 838 us
  waiting for transfers between devices  354 us (42%)
  Pallas kernels  182 us (21%)
  matrix products  86.1 us (10%)
  blocking collectives  69.7 us (8%)
  starting transfers between devices  66.2 us (8%)
  other arithmetic  41.8 us (5%)
  local copies, waits for them, and re-layouts  22.7 us (3%)
  between operations  15.3 us (2%)
    ppermute x21, waiting for transfers between devices, hop(): return lax.ppermute(x, 'seq', ring_pairs)  270 us
    pallas_call x4, Pallas kernels, feed(): pl.pallas_call(functools.partial(feed_kernel, steps), out_shape=[jax.Shap...  93.2 us
    dot_general x14, matrix products, dot(): lax.dot_general(left, right, (dims, ((), ())), preferred_element_type=F32)  86.1 us
    all_to_all x2, blocking collectives, exchange(): return lax.all_to_all(x, group, 0, 0, tiled=True)  69.7 us
    all_to_all x4, waiting for transfers between devices, exchange(): return lax.all_to_all(x, group, 0, 0, tiled=True)  36.7 us
    all_gather x2, waiting for transfers between devices, gather_rows(): lax.all_gather(x, 'yx', axis=1, tiled=True).reshape(model, x.shape[2])  32.4 us
    pallas_call x1, Pallas kernels, attend_back(): pl.pallas_call(functools.partial(attend_back_kernel, heads, ring), out_sh...  25.9 us
    ppermute x21, starting transfers between devices, hop(): return lax.ppermute(x, 'seq', ring_pairs)  24.4 us
  transfers between devices with their start and end apart: 60, of which 24 were waited for; matrix products, arithmetic and copies ran while one was open for 14% of the time, Pallas kernels for 22%

profile of v2, /device:TPU:5, one launch (start us, length us, event | category | flops | bytes accessed | tf_op | source)
XLA Modules:
  0.0 837.7 jit_solution(3587849081306183348)
XLA Ops:
  17.5 18.7 %collective-permute-done.one_ref = bf16[256,2048]{1,0:T(8,128)(2,1)} collective-permute-done((bf16[256,2048]{1,0:T(8,128)(2,1)S(1)}, bf16[256,2048]{1,0:T(8,128)(2,1)}, u32[]{:S(2)}, u32[]{:S(2)}) %collective-permute-start) | collective-permute-done | bytes 1048608 | tf_op jit(solution)/shard_map/ppermute | solution.py:503
  36.2 25.6 %all_to_all.30 = bf16[8,64,768]{2,1,0:T(8,128)(2,1)} all-to-all(bf16[8,64,768]{2,1,0:T(8,128)(2,1)} %qkv_out.1), channel_id=1, replica_groups=mesh['seq'=4,'yx'=4,'core'=2] {'seq','core'}, dimensions={0} | all-to-all | bytes 1572864 | tf_op jit(solution)/shard_map/all_to_all | solution.py:519
  70.5 20.2 %collective-permute-done.1.one_ref = bf16[256,2048]{1,0:T(8,128)(2,1)} collective-permute-done((bf16[256,2048]{1,0:T(8,128)(2,1)}, bf16[256,2048]{1,0:T(8,128)(2,1)}, u32[]{:S(2)}, u32[]{:S(2)}) %collective-permute-start.1) | collective-permute-done | bytes 1048608 | tf_op jit(solution)/shard_map/ppermute | solution.py:503
  90.8 25.2 %collective-permute-done.2.one_ref = bf16[256,2048]{1,0:T(8,128)(2,1)} collective-permute-done((bf16[256,2048]{1,0:T(8,128)(2,1)}, bf16[256,2048]{1,0:T(8,128)(2,1)}, u32[]{:S(2)}, u32[]{:S(2)}) %collective-permute-start.2) | collective-permute-done | bytes 1048608 | tf_op jit(solution)/shard_map/ppermute | solution.py:503
  116.0 6.7 all-to-all-start.1
  156.9 18.3 %attend.1 = (bf16[8,256,256]{2,1,0:T(8,128)(2,1)S(1)}, f32[2,4,4,256]{3,2,1,0:T(4,128)S(1)}) custom-call(s32[2]{0:T(128)S(1)} %pad_add_fusion.where_ref, bf16[4,2,256,768]{3,2,1,0:T(8,128)(2,1)S(1)} %get-tuple-element.113.qkv_ref), custom_call_target="tpu_custom_call" | custom-call | flops 20000000000 | bytes 6291456 | tf_op jit(solution)/shard_map/attend/pallas_call | solution.py:98
  176.2 10.8 %all-to-all-done.1 = bf16[8,64,2048]{2,1,0:T(8,128)(2,1)} async-done(((bf16[8,64,2048]{2,1,0:T(8,128)(2,1)}), bf16[8,64,2048]{2,1,0:T(8,128)(2,1)}, u32[]{:S(2)}, u32[]{:S(2)}) %all-to-all-start.1) | async-done | bytes 2097184 | tf_op jit(solution)/shard_map/all_to_all | solution.py:519
  188.2 44.0 %all_to_all.31 = bf16[8,256,256]{2,1,0:T(8,128)(2,1)S(1)} all-to-all(bf16[8,256,256]{2,1,0:T(8,128)(2,1)S(1)} %copy-done.13), channel_id=1, replica_groups=mesh['seq'=4,'yx'=4,'core'=2] {'seq','core'}, dimensions={0} | all-to-all | bytes 2097152 | tf_op jit(solution)/shard_map/all_to_all | solution.py:519
  233.8 6.2 multiply_reduce_fusion.1
  240.2 19.8 %collective-permute-done.9.dout_ref = bf16[256,2048]{1,0:T(8,128)(2,1)} collective-permute-done((bf16[256,2048]{1,0:T(8,128)(2,1)}, bf16[256,2048]{1,0:T(8,128)(2,1)}, u32[]{:S(2)}, u32[]{:S(2)}) %collective-permute-start.9) | collective-permute-done | bytes 1048608 | tf_op jit(solution)/shard_map/ppermute | solution.py:503
  262.4 20.0 %collective-permute-done.7.two_ref = bf16[256,2048]{1,0:T(8,128)(2,1)} collective-permute-done((bf16[256,2048]{1,0:T(8,128)(2,1)S(1)}, bf16[256,2048]{1,0:T(8,128)(2,1)}, u32[]{:S(2)}, u32[]{:S(2)}) %collective-permute-start.7) | collective-permute-done | bytes 1048608 | tf_op jit(solution)/shard_map/ppermute | solution.py:503
  286.5 32.4 %all-gather.11.cloned.1.call-done = bf16[4,512,2048]{2,1,0:T(8,128)(2,1)} async-done(((bf16[4,128,2048]{2,1,0:T(8,128)(2,1)}), bf16[4,512,2048]{2,1,0:T(8,128)(2,1)}) %all-gather.11.cloned.1.call-update) | async-done | bytes 8388624 | tf_op jit(solution)/shard_map/all_gather | solution.py:525
  318.9 23.3 %feed.4 = (bf16[2048,2048]{1,0:T(8,128)(2,1)}, bf16[2048,2048]{1,0:T(8,128)(2,1)}, bf16[2048,1024]{1,0:T(8,128)(2,1)}, bf16[2048,2048]{1,0:T(8,128)(2,1)}, bf16[...) custom-call(bf16[256,2048]{1,0:T(8,128)(2,1)} %collective-permute-done., ...), custom_call_target="tpu_custom_call" | custom-call | flops 6442450944 | bytes 1 | tf_op jit(solution)/shard_map/feed/pallas_call | solution.py:276
  346.5 23.3 %feed.5 = (bf16[2048,2048]{1,0:T(8,128)(2,1)}, bf16[2048,2048]{1,0:T(8,128)(2,1)}, bf16[2048,1024]{1,0:T(8,128)(2,1)}, bf16[2048,2048]{1,0:T(8,128)(2,1)}, bf16[...) custom-call(bf16[256,2048]{1,0:T(8,128)(2,1)} %copy-done.23, ...), custom_call_target="tpu_custom_call", output_to_operand_aliasing={{0}: (8, {}), {1}: (9, {}), {2}: (10, {}), {3}: (11, {})} | custom-call | flops 6442450944 | bytes 1 | tf_op jit(solution)/shard_map/feed/pallas_call | solution.py:276
  375.2 23.2 %feed.6 = (bf16[2048,2048]{1,0:T(8,128)(2,1)}, bf16[2048,2048]{1,0:T(8,128)(2,1)}, bf16[2048,1024]{1,0:T(8,128)(2,1)}, bf16[2048,2048]{1,0:T(8,128)(2,1)}, bf16[...) custom-call(bf16[256,2048]{1,0:T(8,128)(2,1)} %collective-permute-do, ...), custom_call_target="tpu_custom_call", output_to_operand_aliasing={{0}: (8, {}), {1}: (9, {}), {2}: (10, {}), {3}: (11, {})} | custom-call | flops 6442450944 | bytes 1 | tf_op jit(solution)/shard_map/feed/pallas_call | solution.py:276
  399.6 14.6 %collective-permute-done.12 = bf16[256,2048]{1,0:T(8,128)(2,1)S(1)} collective-permute-done((bf16[256,2048]{1,0:T(8,128)(2,1)}, bf16[256,2048]{1,0:T(8,128)(2,1)S(1)}, u32[]{:S(2)}, u32[]{:S(2)}) %collective-permute-start.12) | collective-permute-done | bytes 1048608 | tf_op jit(solution)/shard_map/ppermute | solution.py:503
  417.9 23.4 %feed.7 = (bf16[2048,2048]{1,0:T(8,128)(2,1)}, bf16[2048,2048]{1,0:T(8,128)(2,1)}, bf16[2048,1024]{1,0:T(8,128)(2,1)}, bf16[2048,2048]{1,0:T(8,128)(2,1)}, bf16[...) custom-call(bf16[256,2048]{1,0:T(8,128)(2,1)} %copy-done.25, ...), custom_call_target="tpu_custom_call", output_to_operand_aliasing={{0}: (8, {}), {1}: (9, {}), {2}: (10, {}), {3}: (11, {})} | custom-call | flops 6442450944 | bytes 1 | tf_op jit(solution)/shard_map/feed/pallas_call | solution.py:276
  442.6 24.2 %convolution_convert_fusion = bf16[2048,2048]{1,0:T(8,128)(2,1)} fusion(bf16[2048,2048]{1,0:T(8,128)(2,1)} %get-tuple-element.147, bf16[2048,2048]{1,0:T(8,128)(2,1)} %get-tuple-element.148), kind=kOutput, calls=%fused_computation | convolution fusion | flops 17184063488 | bytes 25165824 | tf_op jit(solution)/shard_map/dot_general | solution.py:23
  470.7 14.2 %convolution_convert_fusion.2 = bf16[1024,2048]{1,0:T(8,128)(2,1)} fusion(bf16[2048,1024]{1,0:T(8,128)(2,1)} %get-tuple-element.151, bf16[2048,2048]{1,0:T(8,128)(2,1)} %get-tuple-element.153), kind=kOutput, calls=%fused_computation.2 | convolution fusion | flops 8592031744 | bytes 16777216 | tf_op jit(solution)/shard_map/dot_general | solution.py:23
  484.9 11.9 %collective-permute-done.27 = bf16[256,2048]{1,0:T(8,128)(2,1)} collective-permute-done((bf16[256,2048]{1,0:T(8,128)(2,1)}, bf16[256,2048]{1,0:T(8,128)(2,1)}, u32[]{:S(2)}, u32[]{:S(2)}) %collective-permute-start.27) | collective-permute-done | bytes 1048608 | tf_op jit(solution)/shard_map/ppermute | solution.py:503
  510.3 19.2 %collective-permute-done.29 = bf16[256,2048]{1,0:T(8,128)(2,1)} collective-permute-done((bf16[256,2048]{1,0:T(8,128)(2,1)S(1)}, bf16[256,2048]{1,0:T(8,128)(2,1)}, u32[]{:S(2)}, u32[]{:S(2)}) %collective-permute-start.29) | collective-permute-done | bytes 1048608 | tf_op jit(solution)/shard_map/ppermute | solution.py:503
  546.8 15.8 %all-to-all-done.3.datt_ref = bf16[8,256,256]{2,1,0:T(8,128)(2,1)S(1)} async-done(((bf16[8,256,256]{2,1,0:T(8,128)(2,1)}), bf16[8,256,256]{2,1,0:T(8,128)(2,1)S(1)}, u32[]{:S(2)}, u32[]{:S(2)}) %all-to-all-start.3) | async-done | bytes 1048608 | tf_op jit(solution)/shard_map/all_to_all | solution.py:519
  563.5 25.9 %attend_back.1 = bf16[4,2,256,768]{3,2,1,0:T(8,128)(2,1)} custom-call(s32[2]{0:T(128)S(1)} %pad_add_fusion.where_ref, bf16[4,2,256,768]{3,2,1,0:T(8,128)(2,1)} %copy-done.3, bf16[8,256,256]{2,1,0:T(8,128)(2,1)} %copy-done.33, f32[2,4,4,256]{3,2,1,0:T(4,128)S(1)} %get-tuple-element.172.lse_ref, f32[1024,128]{1,0:T(8,128)S(1)} %copy-done.5, ...), custom_call_target="tpu_custom_call" | custom-call | flops 28000000000 | bytes 12582912 | tf_op jit(solution)/shard_map/attend_back/pallas_call | solution.py:204
  592.4 10.6 %convolution_convert_fusion.3 = bf16[2048,768]{1,0:T(8,128)(2,1)} fusion(bf16[2048,2048]{1,0:T(8,128)(2,1)} %get-tuple-element.175, bf16[2048,768]{1,0:T(8,128)(2,1)S(1)} %bitcast.134), kind=kOutput, calls=%fused_computation.3 | convolution fusion | flops 6444023808 | bytes 14680064 | tf_op jit(solution)/shard_map/dot_general | solution.py:23
  613.6 55.9 %collective-permute-done.35 = bf16[256,2048]{1,0:T(8,128)(2,1)} collective-permute-done((bf16[256,2048]{1,0:T(8,128)(2,1)}, bf16[256,2048]{1,0:T(8,128)(2,1)}, u32[]{:S(2)}, u32[]{:S(2)}) %collective-permute-start.35) | collective-permute-done | bytes 1048608 | tf_op jit(solution)/shard_map/ppermute | solution.py:503
  679.7 8.3 collective-permute-start.38
  694.4 16.4 %collective-permute-done.38 = bf16[256,2048]{1,0:T(8,128)(2,1)} collective-permute-done((bf16[256,2048]{1,0:T(8,128)(2,1)}, bf16[256,2048]{1,0:T(8,128)(2,1)}, u32[]{:S(2)}, u32[]{:S(2)}) %collective-permute-start.38) | collective-permute-done | bytes 1048608 | tf_op jit(solution)/shard_map/ppermute | solution.py:503
  713.9 9.9 %all-to-all-done.5.hat_ref = bf16[8,64,768]{2,1,0:T(8,128)(2,1)} async-done(((bf16[8,64,768]{2,1,0:T(8,128)(2,1)}), bf16[8,64,768]{2,1,0:T(8,128)(2,1)}, u32[]{:S(2)}, u32[]{:S(2)}) %all-to-all-start.5) | async-done | bytes 786464 | tf_op jit(solution)/shard_map/all_to_all | solution.py:519
  730.9 8.8 %collective-permute-done.42 = bf16[64,2048]{1,0:T(8,128)(2,1)} collective-permute-done((bf16[64,2048]{1,0:T(8,128)(2,1)S(1)}, bf16[64,2048]{1,0:T(8,128)(2,1)}, u32[]{:S(2)}, u32[]{:S(2)}) %collective-permute-start.42) | collective-permute-done | bytes 262176 | tf_op jit(solution)/shard_map/ppermute | solution.py:503
  755.0 23.4 %collective-permute-done.44 = bf16[64,2048]{1,0:T(8,128)(2,1)S(1)} collective-permute-done((bf16[64,2048]{1,0:T(8,128)(2,1)S(1)}, bf16[64,2048]{1,0:T(8,128)(2,1)S(1)}, u32[]{:S(2)}, u32[]{:S(2)}) %collective-permute-start.44) | collective-permute-done | bytes 262176 | tf_op jit(solution)/shard_map/ppermute | solution.py:503
  798.9 6.5 qkv_back.1
  810.3 12.4 %collective-permute-done.46 = bf16[256,2048]{1,0:T(8,128)(2,1)} collective-permute-done((bf16[256,2048]{1,0:T(8,128)(2,1)}, bf16[256,2048]{1,0:T(8,128)(2,1)}, u32[]{:S(2)}, u32[]{:S(2)}) %collective-permute-start.46) | collective-permute-done | bytes 1048608 | tf_op jit(solution)/shard_map/ppermute | solution.py:503
  (273 shorter events, 203.4 us)
Async XLA Ops:
  7.2 56.6 %all-gather.5.cloned.1.call-start = ((), (), s32[]{:S(2)}) async-start(), calls=%async_computation.10 | async-start | bytes 5242880 | tf_op jit(solution)/shard_map/all_gather | solution.py:541
  7.9 119.5 %all-gather.7.cloned.1.call-start = ((), (), s32[]{:S(2)}) async-start(), calls=%async_computation.11 | async-start | bytes 3932160 | tf_op jit(solution)/shard_map/all_gather | solution.py:525
  63.8 169.9 %all-gather.9.cloned.1.call-start = ((), (), s32[]{:S(2)}) async-start(), calls=%async_computation.12 | async-start | bytes 8650752 | tf_op jit(solution)/shard_map/all_gather | solution.py:548
  116.0 71.0 %all-to-all-start.1 = ((bf16[8,64,2048]{2,1,0:T(8,128)(2,1)}), bf16[8,64,2048]{2,1,0:T(8,128)(2,1)}, u32[]{:S(2)}, u32[]{:S(2)}) async-start(bf16[8,64,2048]{2,1,0:T(8,128)(2,1)} %ff_out.1), calls=%async_computation.1 | async-start | bytes 4194304 | tf_op jit(solution)/shard_map/all_to_all | solution.py:519
  122.7 196.2 %all-gather.11.cloned.1.call-start = ((), (), s32[]{:S(2)}) async-start(), calls=%async_computation.13 | async-start | bytes 10485760 | tf_op jit(solution)/shard_map/all_gather | solution.py:525
  187.0 405.3 %reduce-scatter.5.cloned.1.call-start = ((), (), s32[]{:S(2)}) async-start(), calls=%async_computation.14 | async-start | bytes 10485760 | tf_op jit(solution)/shard_map/reduce_scatter | solution.py:529
  240.2 42.3 %collective-permute-start.7 = (bf16[256,2048]{1,0:T(8,128)(2,1)S(1)}, bf16[256,2048]{1,0:T(8,128)(2,1)}, u32[]{:S(2)}, u32[]{:S(2)}) collective-permute-start(bf16[256,2048]{1,0:T(8,128)(2,1)S(1)} %multiply_convert_fusion.two_ref), channel_id=1, source_target_pairs={{0,8},{8,16},{16,24},{24,0},{1,9},{9,17},{17,25},{25,1},{2,10},{10... | collective-permute-start | bytes 3145736 | tf_op jit(solution)/shard_map/ppermute | solution.py:503
  283.9 59.0 %collective-permute-start.15 = (bf16[256,2048]{1,0:T(8,128)(2,1)}, bf16[256,2048]{1,0:T(8,128)(2,1)}, u32[]{:S(2)}, u32[]{:S(2)}) collective-permute-start(bf16[256,2048]{1,0:T(8,128)(2,1)} %collective-permute-done.9.dout_ref), channel_id=1, source_target_pairs={{0,8},{8,16},{16,24},{24,0},{1,9},{9,17},{17,25},{25,1},{2,10},{10... | collective-permute-start | bytes 3145736 | tf_op jit(solution)/shard_map/ppermute | solution.py:503
  283.9 59.1 %collective-permute-start.18 = (bf16[256,2048]{1,0:T(8,128)(2,1)}, bf16[256,2048]{1,0:T(8,128)(2,1)}, u32[]{:S(2)}, u32[]{:S(2)}) collective-permute-start(bf16[256,2048]{1,0:T(8,128)(2,1)} %bitcast.13.dout_ref), channel_id=1, source_target_pairs={{0,1},{1,0},{2,3},{3,2},{4,5},{5,4},{6,7},{7,6},{8,9},{9,8},{10,11... | collective-permute-start | bytes 3145736 | tf_op jit(solution)/shard_map/ppermute | solution.py:506
  283.9 60.3 %collective-permute-start.13 = (bf16[256,2048]{1,0:T(8,128)(2,1)}, bf16[256,2048]{1,0:T(8,128)(2,1)}, u32[]{:S(2)}, u32[]{:S(2)}) collective-permute-start(bf16[256,2048]{1,0:T(8,128)(2,1)} %collective-permute-done.7.two_ref), channel_id=1, source_target_pairs={{0,8},{8,16},{16,24},{24,0},{1,9},{9,17},{17,25},{25,1},{2,10},{10... | collective-permute-start | bytes 3145736 | tf_op jit(solution)/shard_map/ppermute | solution.py:503
  283.9 61.0 %collective-permute-start.17 = (bf16[256,2048]{1,0:T(8,128)(2,1)S(1)}, bf16[256,2048]{1,0:T(8,128)(2,1)}, u32[]{:S(2)}, u32[]{:S(2)}) collective-permute-start(bf16[256,2048]{1,0:T(8,128)(2,1)S(1)} %multiply_convert_fusion.two_ref), channel_id=1, source_target_pairs={{0,1},{1,0},{2,3},{3,2},{4,5},{5,4},{6,7},{7,6},{8,9},{9,8},{10,11... | collective-permute-start | bytes 3145736 | tf_op jit(solution)/shard_map/ppermute | solution.py:506
  342.2 27.7 %collective-permute-start.11 = (bf16[256,2048]{1,0:T(8,128)(2,1)}, bf16[256,2048]{1,0:T(8,128)(2,1)}, u32[]{:S(2)}, u32[]{:S(2)}) collective-permute-start(bf16[256,2048]{1,0:T(8,128)(2,1)} %get-tuple-element.123), channel_id=1, source_target_pairs={{0,1},{1,0},{2,3},{3,2},{4,5},{5,4},{6,7},{7,6},{8,9},{9,8},{10,11... | collective-permute-start | bytes 3145736 | tf_op jit(solution)/shard_map/ppermute | solution.py:506
  342.9 31.0 %collective-permute-start.16 = (bf16[256,2048]{1,0:T(8,128)(2,1)}, bf16[256,2048]{1,0:T(8,128)(2,1)S(1)}, u32[]{:S(2)}, u32[]{:S(2)}) collective-permute-start(bf16[256,2048]{1,0:T(8,128)(2,1)} %collective-permute-done.15.dout_ref), channel_id=1, source_target_pairs={{0,1},{1,0},{2,3},{3,2},{4,5},{5,4},{6,7},{7,6},{8,9},{9,8},{10,11... | collective-permute-start | bytes 3145736 | tf_op jit(solution)/shard_map/ppermute | solution.py:506
  343.0 56.1 %collective-permute-start.24 = (bf16[256,2048]{1,0:T(8,128)(2,1)}, bf16[256,2048]{1,0:T(8,128)(2,1)S(1)}, u32[]{:S(2)}, u32[]{:S(2)}) collective-permute-start(bf16[256,2048]{1,0:T(8,128)(2,1)} %collective-permute-done.15.dout_ref), channel_id=1, source_target_pairs={{0,8},{8,16},{16,24},{24,0},{1,9},{9,17},{17,25},{25,1},{2,10},{10... | collective-permute-start | bytes 3145736 | tf_op jit(solution)/shard_map/ppermute | solution.py:503
  344.2 29.7 %collective-permute-start.14 = (bf16[256,2048]{1,0:T(8,128)(2,1)}, bf16[256,2048]{1,0:T(8,128)(2,1)S(1)}, u32[]{:S(2)}, u32[]{:S(2)}) collective-permute-start(bf16[256,2048]{1,0:T(8,128)(2,1)} %collective-permute-done.13.two_ref), channel_id=1, source_target_pairs={{0,1},{1,0},{2,3},{3,2},{4,5},{5,4},{6,7},{7,6},{8,9},{9,8},{10,11... | collective-permute-start | bytes 3145736 | tf_op jit(solution)/shard_map/ppermute | solution.py:506
  344.9 54.3 %collective-permute-start.22 = (bf16[256,2048]{1,0:T(8,128)(2,1)}, bf16[256,2048]{1,0:T(8,128)(2,1)S(1)}, u32[]{:S(2)}, u32[]{:S(2)}) collective-permute-start(bf16[256,2048]{1,0:T(8,128)(2,1)} %collective-permute-done.13.two_ref), channel_id=1, source_target_pairs={{0,8},{8,16},{16,24},{24,0},{1,9},{9,17},{17,25},{25,1},{2,10},{10... | collective-permute-start | bytes 3145736 | tf_op jit(solution)/shard_map/ppermute | solution.py:503
  372.5 41.8 %collective-permute-start.12 = (bf16[256,2048]{1,0:T(8,128)(2,1)}, bf16[256,2048]{1,0:T(8,128)(2,1)S(1)}, u32[]{:S(2)}, u32[]{:S(2)}) collective-permute-start(bf16[256,2048]{1,0:T(8,128)(2,1)} %add_convert_fusion.9), channel_id=1, source_target_pairs={{0,8},{8,16},{16,24},{24,0},{1,9},{9,17},{17,25},{25,1},{2,10},{10... | collective-permute-start | bytes 3145736 | tf_op jit(solution)/shard_map/ppermute | solution.py:503
  416.2 50.6 %collective-permute-start.21 = (bf16[256,2048]{1,0:T(8,128)(2,1)S(1)}, bf16[256,2048]{1,0:T(8,128)(2,1)}, u32[]{:S(2)}, u32[]{:S(2)}) collective-permute-start(bf16[256,2048]{1,0:T(8,128)(2,1)S(1)} %add_convert_fusion.8), channel_id=1, source_target_pairs={{0,8},{8,16},{16,24},{24,0},{1,9},{9,17},{17,25},{25,1},{2,10},{10... | collective-permute-start | bytes 3145736 | tf_op jit(solution)/shard_map/ppermute | solution.py:503
  531.9 30.7 %all-to-all-start.3 = ((bf16[8,256,256]{2,1,0:T(8,128)(2,1)}), bf16[8,256,256]{2,1,0:T(8,128)(2,1)S(1)}, u32[]{:S(2)}, u32[]{:S(2)}) async-start(bf16[8,256,256]{2,1,0:T(8,128)(2,1)} %bitcast.16), calls=%async_computation.3 | async-start | bytes 2097152 | tf_op jit(solution)/shard_map/all_to_all | solution.py:519
  536.8 151.2 %reduce-scatter.7.cloned.1.call-start = ((), (), s32[]{:S(2)}) async-start(), calls=%async_computation.15 | async-start | bytes 3932160 | tf_op jit(solution)/shard_map/reduce_scatter | solution.py:529
  537.5 52.0 %collective-permute-start.34 = (bf16[256,2048]{1,0:T(8,128)(2,1)}, bf16[256,2048]{1,0:T(8,128)(2,1)}, u32[]{:S(2)}, u32[]{:S(2)}) collective-permute-start(bf16[256,2048]{1,0:T(8,128)(2,1)} %get-tuple-element.167), channel_id=1, source_target_pairs={{0,1},{1,0},{2,3},{3,2},{4,5},{5,4},{6,7},{7,6},{8,9},{9,8},{10,11... | collective-permute-start | bytes 3145736 | tf_op jit(solution)/shard_map/ppermute | solution.py:506
  603.0 120.8 %reduce-scatter.9.cloned.1.call-start = ((), (), s32[]{:S(2)}) async-start(), calls=%async_computation.16 | async-start | bytes 5242880 | tf_op jit(solution)/shard_map/reduce_scatter | solution.py:607
  603.8 75.9 %all-to-all-start.4 = ((bf16[8,64,2048]{2,1,0:T(8,128)(2,1)}), bf16[8,64,2048]{2,1,0:T(8,128)(2,1)}, u32[]{:S(2)}, u32[]{:S(2)}) async-start(bf16[8,64,2048]{2,1,0:T(8,128)(2,1)} %bitcast.22), calls=%async_computation.5 | async-start | bytes 4194304 | tf_op jit(solution)/shard_map/all_to_all | solution.py:519
  609.0 197.9 %reduce-scatter.11.cloned.1.call-start = ((), (), s32[]{:S(2)}) async-start(), calls=%async_computation.17 | async-start | bytes 5242880 | tf_op jit(solution)/shard_map/reduce_scatter | solution.py:619
  609.2 60.3 %collective-permute-start.35 = (bf16[256,2048]{1,0:T(8,128)(2,1)}, bf16[256,2048]{1,0:T(8,128)(2,1)}, u32[]{:S(2)}, u32[]{:S(2)}) collective-permute-start(bf16[256,2048]{1,0:T(8,128)(2,1)} %add_convert_fusion.4), channel_id=1, source_target_pairs={{0,8},{8,16},{16,24},{24,0},{1,9},{9,17},{17,25},{25,1},{2,10},{10... | collective-permute-start | bytes 3145736 | tf_op jit(solution)/shard_map/ppermute | solution.py:503
  613.5 63.1 %collective-permute-start.37 = (bf16[256,2048]{1,0:T(8,128)(2,1)S(1)}, bf16[256,2048]{1,0:T(8,128)(2,1)S(1)}, u32[]{:S(2)}, u32[]{:S(2)}) collective-permute-start(bf16[256,2048]{1,0:T(8,128)(2,1)S(1)} %convolution_convert_fusion.10), channel_id=1, source_target_pairs={{0,1},{1,0},{2,3},{3,2},{4,5},{5,4},{6,7},{7,6},{8,9},{9,8},{10,11... | collective-permute-start | bytes 3145736 | tf_op jit(solution)/shard_map/ppermute | solution.py:506
  679.7 31.1 %collective-permute-start.38 = (bf16[256,2048]{1,0:T(8,128)(2,1)}, bf16[256,2048]{1,0:T(8,128)(2,1)}, u32[]{:S(2)}, u32[]{:S(2)}) collective-permute-start(bf16[256,2048]{1,0:T(8,128)(2,1)} %add_convert_fusion.2), channel_id=1, source_target_pairs={{0,8},{8,16},{16,24},{24,0},{1,9},{9,17},{17,25},{25,1},{2,10},{10... | collective-permute-start | bytes 3145736 | tf_op jit(solution)/shard_map/ppermute | solution.py:503
  688.0 35.9 %all-to-all-start.5 = ((bf16[8,64,768]{2,1,0:T(8,128)(2,1)}), bf16[8,64,768]{2,1,0:T(8,128)(2,1)}, u32[]{:S(2)}, u32[]{:S(2)}) async-start(bf16[8,64,768]{2,1,0:T(8,128)(2,1)} %bitcast.133), calls=%async_computation.7 | async-start | bytes 1572864 | tf_op jit(solution)/shard_map/all_to_all | solution.py:519
  743.9 51.4 %collective-permute-start.41 = (bf16[256,2048]{1,0:T(8,128)(2,1)}, bf16[256,2048]{1,0:T(8,128)(2,1)}, u32[]{:S(2)}, u32[]{:S(2)}) collective-permute-start(bf16[256,2048]{1,0:T(8,128)(2,1)} %convolution_convert_fusion.6), channel_id=1, source_target_pairs={{0,1},{1,0},{2,3},{3,2},{4,5},{5,4},{6,7},{7,6},{8,9},{9,8},{10,11... | collective-permute-start | bytes 3145736 | tf_op jit(solution)/shard_map/ppermute | solution.py:506
  745.3 50.0 %collective-permute-start.40 = (bf16[256,2048]{1,0:T(8,128)(2,1)}, bf16[256,2048]{1,0:T(8,128)(2,1)}, u32[]{:S(2)}, u32[]{:S(2)}) collective-permute-start(bf16[256,2048]{1,0:T(8,128)(2,1)} %add_convert_fusion.1), channel_id=1, source_target_pairs={{0,8},{8,16},{16,24},{24,0},{1,9},{9,17},{17,25},{25,1},{2,10},{10... | collective-permute-start | bytes 3145736 | tf_op jit(solution)/shard_map/ppermute | solution.py:503
  749.0 29.4 %collective-permute-start.44 = (bf16[64,2048]{1,0:T(8,128)(2,1)S(1)}, bf16[64,2048]{1,0:T(8,128)(2,1)S(1)}, u32[]{:S(2)}, u32[]{:S(2)}) collective-permute-start(bf16[64,2048]{1,0:T(8,128)(2,1)S(1)} %fusion.21), channel_id=1, source_target_pairs={{0,8},{8,16},{16,24},{24,0},{1,9},{9,17},{17,25},{25,1},{2,10},{10... | collective-permute-start | bytes 786440 | tf_op jit(solution)/shard_map/ppermute | solution.py:503
  752.1 58.2 %collective-permute-start.47 = (bf16[256,2048]{1,0:T(8,128)(2,1)}, bf16[256,2048]{1,0:T(8,128)(2,1)}, u32[]{:S(2)}, u32[]{:S(2)}) collective-permute-start(bf16[256,2048]{1,0:T(8,128)(2,1)} %convolution_convert_fusion.4), channel_id=1, source_target_pairs={{0,1},{1,0},{2,3},{3,2},{4,5},{5,4},{6,7},{7,6},{8,9},{9,8},{10,11... | collective-permute-start | bytes 3145736 | tf_op jit(solution)/shard_map/ppermute | solution.py:506
  (78 other events, 1550.5 us)
Sparse Core Ops, SparseCore 0:
  9.9 53.8 all-gather.4
  65.7 43.9 all-gather.6
  112.5 118.2 all-gather.8
  232.5 86.3 all-gather.10
  469.8 86.2 reduce-scatter.4
  603.2 43.7 reduce-scatter.6
  650.2 52.6 reduce-scatter.8
  705.9 52.6 reduce-scatter.10

commit v3 on v2

--- a/solution.py
+++ b/solution.py
@@ -287,7 +287,7 @@
         out_specs=[pl.BlockSpec((2 * rows, w), lambda j: (k, 0)) for w in widths] + [share] * 4,
         input_output_aliases={8 + i: i for i in range(len(kept))},
         compiler_params=pltpu.CompilerParams(vmem_limit_bytes=56 << 20),
-        cost_estimate=pl.CostEstimate(flops=2 * rows * model * ff * 6, bytes_accessed=1, transcendentals=0),
+        cost_estimate=pl.CostEstimate(flops=2 * rows * model * ff * 6 // 4, bytes_accessed=1, transcendentals=0),
         name="feed",
     )(two, two_other, dout, dout_other, ff_w, down_w, ff_w, down_w, *kept)
     return kept, (out, out_other), (back, back_other)
@@ -319,7 +319,7 @@
 
 
 def project(k, blocks, kept, where, one, other, w, cosine, sine):
-    rows, model = one.shape
+    rows, model = cosine.shape[0] // blocks, one.shape[1]
     width = w.shape[1] // 3
     whole = pl.BlockSpec((rows, model), lambda j, at: (0, 0))
     table = pl.BlockSpec((rows, width // 2), lambda j, at: (lax.rem(at[0] - k + blocks, blocks), 0))
@@ -535,17 +535,19 @@
 
     residual = inputs.reshape(rows, model).astype(F32)
     normed_one, inverse_one = unit(residual)
-    one = normed_one.astype(BF)
+    one = jnp.concatenate([normed_one.astype(BF), w_output])
     qkv_w = qkv_out(parts, gain_one, w_query, w_key, w_value)
     ff_w = ff_out(ring, pair, ff_own, gain_two, w_gate, w_up)
     down_w = lax.all_gather(w_down, "yx", axis=0, tiled=True)
     ones = [one, hop(one)]
     qkv_w = exchange_rows(after(qkv_w, ones[1]))
+    qkv_sent, qkv_w = qkv_w, gather_rows(after(qkv_w, down_w))
     for k in range(1, ring - 1):
-        ones.append(hop(after(ones[k], qkv_w if k == 1 else ff_w)))
-    qkv_w = gather_rows(after(qkv_w, down_w))
-    ff_w = exchange_rows(after(ff_w, ones[-1]))
-    output_w = lax.all_gather(after(w_output, ones[1]), ("seq", "yx", "core"), axis=0, tiled=True)
+        ones.append(hop(after(ones[k], qkv_sent if k == 1 else ff_w, *([qkv_w] if k == ring - 2 else []))))
+    ff_w = exchange_rows(after(ff_w, ones[-1], qkv_w))
+    output_w = jnp.stack([ones[k][rows:] for k in reversed(range(ring))] * 2)
+    output_w = lax.dynamic_slice_in_dim(output_w, ring - 1 - z, ring)
+    output_w = lax.all_gather(output_w, ("yx", "core"), axis=1, tiled=True).reshape(model, model)
 
     freqs = jnp.exp(jnp.arange(HALF, dtype=F32) * (-2.0 * math.log(ROPE_BASE) / HEAD_DIM))
     angle = jnp.arange(ring * rows, dtype=jnp.int32).astype(F32)[:, None] * freqs[None, :]
@@ -580,31 +582,26 @@
             first_share = both_cores(back).astype(BF)
         else:
             here = hop(total).astype(F32) + back[0].astype(F32)
-            if k == ring - 1:
-                all_twos, all_douts, hiddens, dffs = kept
-                ff_grad = mm_tn(after(all_twos, total), dffs).astype(BF)
-                here = after(here, ff_grad)
-            else:
-                here = after(here, own_share)
+            here = after(here, own_share)
             total = (here + swap(back[1]).astype(F32)).astype(BF)
     tokens = ring * pair * rows
-    ff_grad = sum_rows(after(ff_grad, total))
-    down_grad = mm_tn(hiddens, after(all_douts, total)).astype(BF)
-    grad_two = after(hop(total).astype(F32) + own_share, down_grad)
+    all_twos, all_douts, hiddens, dffs = kept
+    ff_grad = mm_tn(after(all_twos, total), dffs).astype(BF)
+    grad_two = after(hop(total).astype(F32) + own_share, ff_grad)
+    ff_grad = sum_rows(after(ff_grad, grad_two))
 
     grad_mid = grad_out.astype(F32) + unit_back(grad_two, normed_two, inverse_two)
     proj = grad_mid.astype(BF)
     datt = mm_nt(proj, output_w).astype(BF)
-    shares = [both_cores(after(t, grad_two)) for t in out_terms]
-    total = (hop(shares[1].astype(BF)).astype(F32) + shares[2]).astype(BF)
     datt = datt.reshape(rows, parts, width).transpose(1, 0, 2)
 
     split = model // pair
     mine = lax.dynamic_slice_in_dim(att, c * split, split, axis=1)
     others = swap(lax.dynamic_slice_in_dim(att, (pair - 1 - c) * split, split, axis=1))
     output_grad = mm_tn(jnp.concatenate([mine, others]), jnp.concatenate([proj, swap(proj)])).astype(BF)
-    datt = after(exchange(after(datt, total)), output_grad)
-    output_grad = lax.psum_scatter(output_grad, "yx", scatter_dimension=0, tiled=True)
+    shares = [both_cores(after(t, grad_two)) for t in out_terms]
+    total = (hop(shares[1].astype(BF)).astype(F32) + shares[2]).astype(BF)
+    datt = after(exchange(datt), output_grad, total)
     dqkv = attend_back(qkv, datt, lse, cosine, sine, where, heads)
     total = after(total, datt)
     for k in range(3, ring):
@@ -616,28 +613,26 @@
 
     qkv_grad = mm_tn(all_ones, dqkv.reshape(tokens, 3 * width)).astype(BF)
     dqkv = after(dqkv, qkv_grad)
-    down_grad = lax.psum_scatter(after(down_grad, qkv_grad), "yx", scatter_dimension=0, tiled=True).astype(F32)
+    down_grad = mm_tn(hiddens, after(all_douts, dqkv)).astype(BF)
+    down_grad = lax.psum_scatter(down_grad, "yx", scatter_dimension=0, tiled=True).astype(F32)
     qkv_grad = sum_rows(qkv_grad)
     one_terms = [[mm_nt(dqkv[k, i], qkv_w).astype(BF) for i in range(pair)] for k in range(ring)]
     shares = [both_cores(t) for t in one_terms]
-    total = after(shares[1].astype(BF), output, ff_grad)
-    qkv_grad = return_rows(after(qkv_grad, output))
-    total = after((hop(total).astype(F32) + shares[2]).astype(BF), qkv_grad)
-    output_grad = after(output_grad, total)
-    output_grad = output_grad.reshape(ring, own, model)
+    total = (hop(shares[1].astype(BF)).astype(F32) + shares[2]).astype(BF)
+    output_grad = lax.psum_scatter(after(output_grad, one_terms[1][0]), "yx", scatter_dimension=0, tiled=True)
+    qkv_grad = return_rows(qkv_grad)
+    total, qkv_grad, gate_grad, up_grad, gain_two_grad, output = lax.optimization_barrier(
+        (total, qkv_grad, gate_grad, up_grad, gain_two_grad, output)
+    )
+    query_grad, key_grad, value_grad, gain_one_grad = qkv_back(gain_one, qkv_grad, w_query, w_key, w_value)
+    for k in range(3, ring):
+        total = (hop(total).astype(F32) + shares[k]).astype(BF)
+    output_grad = after(output_grad, total).reshape(ring, own, model)
     output_grad = ring_sum(
         [lax.dynamic_index_in_dim(output_grad, lax.rem(z - k + ring, ring), keepdims=False).astype(F32) for k in range(ring)]
     ).astype(BF)
     moves = [((s * plane + y) * pair + h, (h * plane + y) * ring + s) for s in range(ring) for y in range(plane) for h in range(pair)]
     output_grad = lax.ppermute(output_grad, ("seq", "yx", "core"), moves).astype(F32)
-
-    query_grad, key_grad, value_grad, gain_one_grad = qkv_back(gain_one, qkv_grad, w_query, w_key, w_value)
-    for k in range(3, ring):
-        total = (hop(total).astype(F32) + shares[k]).astype(BF)
-    total = after(total, qkv_grad)
-    total, gate_grad, up_grad, gain_two_grad, output_grad = lax.optimization_barrier(
-        (total, gate_grad, up_grad, gain_two_grad, output_grad)
-    )
     grad_one = hop(total).astype(F32) + shares[0]
     input_grad = (grad_mid + unit_back(grad_one, normed_one, inverse_one)).reshape(inputs.shape)
     return (

time: 850 us -> 831 us (0.978)
  waiting for transfers between devices: 354 us -> 338 us
  starting transfers between devices: 66.2 us -> 52.6 us
  blocking collectives: 69.7 us -> 56.3 us
  other arithmetic: 41.8 us -> 52.4 us
  local copies, waits for them, and re-layouts: 22.7 us -> 32.9 us
    all_to_all x4, waiting for transfers between devices: 36.7 us -> 75.9 us  [exchange(): return lax.all_to_all(x, group, 0, 0, tiled=True)]
    ppermute x21, waiting for transfers between devices: 270 us -> 234 us  [hop(): return lax.ppermute(x, 'seq', ring_pairs)]
    all_gather x2, waiting for transfers between devices: 32.4 us -> 16 us  [gather_rows(): lax.all_gather(x, 'yx', axis=1, tiled=True).reshape(model, x.shape[2])]
    all_to_all x2, blocking collectives: 69.7 us -> 56.3 us  [exchange(): return lax.all_to_all(x, group, 0, 0, tiled=True)]
    ppermute x21, starting transfers between devices: 24.4 us -> 11.9 us  [hop(): return lax.ppermute(x, 'seq', ring_pairs)]
  transfers between devices with their start and end apart: 60 -> 60, of which waited for: 24 -> 22; matrix products, arithmetic and copies ran while one was open for 14% -> 17% of each run, Pallas kernels for 22% -> 22%
where the time goes in v3:
time: 831 us; the launch traced here: 819 us
  waiting for transfers between devices  338 us (41%)
  Pallas kernels  182 us (22%)
  matrix products  88.8 us (11%)
  blocking collectives  56.3 us (7%)
  starting transfers between devices  52.6 us (6%)
  other arithmetic  52.4 us (6%)
  local copies, waits for them, and re-layouts  32.9 us (4%)
  between operations  15.3 us (2%)
    ppermute x21, waiting for transfers between devices, hop(): return lax.ppermute(x, 'seq', ring_pairs)  234 us
    pallas_call x4, Pallas kernels, feed(): pl.pallas_call(functools.partial(feed_kernel, steps), out_shape=[jax.Shap...  93.4 us
    dot_general x14, matrix products, dot(): lax.dot_general(left, right, (dims, ((), ())), preferred_element_type=F32)  88.8 us
    all_to_all x4, waiting for transfers between devices, exchange(): return lax.all_to_all(x, group, 0, 0, tiled=True)  75.9 us
    all_to_all x2, blocking collectives, exchange(): return lax.all_to_all(x, group, 0, 0, tiled=True)  56.3 us
    pallas_call x1, Pallas kernels, attend_back(): pl.pallas_call(functools.partial(attend_back_kernel, heads, ring), out_sh...  25.8 us
    pallas_call x4, Pallas kernels, project(): pl.pallas_call(project_kernel, out_shape=(jax.ShapeDtypeStruct((blocks *...  23.9 us
    all_to_all x4, starting transfers between devices, exchange(): return lax.all_to_all(x, group, 0, 0, tiled=True)  20.2 us
  transfers between devices with their start and end apart: 60, of which 22 were waited for; matrix products, arithmetic and copies ran while one was open for 17% of the time, Pallas kernels for 22%

profile of v3, /device:TPU:5, one launch (start us, length us, event | category | flops | bytes accessed | tf_op | source)
XLA Modules:
  0.0 818.8 jit_solution(2360124770827038302)
XLA Ops:
  17.4 24.2 %collective-permute-done.one_ref = bf16[320,2048]{1,0:T(8,128)(2,1)S(1)} collective-permute-done((bf16[320,2048]{1,0:T(8,128)(2,1)S(1)}, bf16[320,2048]{1,0:T(8,128)(2,1)S(1)}, u32[]{:S(2)}, u32[]{:S(2)}) %collective-permute-start) | collective-permute-done | bytes 1310752 | tf_op jit(solution)/shard_map/ppermute | solution.py:503
  41.6 25.6 %all_to_all.30 = bf16[8,64,768]{2,1,0:T(8,128)(2,1)} all-to-all(bf16[8,64,768]{2,1,0:T(8,128)(2,1)} %qkv_out.1), channel_id=1, replica_groups=mesh['seq'=4,'yx'=4,'core'=2] {'seq','core'}, dimensions={0} | all-to-all | bytes 1572864 | tf_op jit(solution)/shard_map/all_to_all | solution.py:519
  72.1 26.4 %collective-permute-done.1.one_ref = bf16[320,2048]{1,0:T(8,128)(2,1)} collective-permute-done((bf16[320,2048]{1,0:T(8,128)(2,1)S(1)}, bf16[320,2048]{1,0:T(8,128)(2,1)}, u32[]{:S(2)}, u32[]{:S(2)}) %collective-permute-start.1) | collective-permute-done | bytes 1310752 | tf_op jit(solution)/shard_map/ppermute | solution.py:503
  98.5 12.1 %all-gather.7.cloned.1.call-done = bf16[4,512,768]{2,1,0:T(8,128)(2,1)} async-done(((bf16[4,128,768]{2,1,0:T(8,128)(2,1)}), bf16[4,512,768]{2,1,0:T(8,128)(2,1)}) %all-gather.7.cloned.1.call-update) | async-done | bytes 3145744 | tf_op jit(solution)/shard_map/all_gather | solution.py:525
  111.8 30.4 %collective-permute-done.2.one_ref = bf16[320,2048]{1,0:T(8,128)(2,1)S(1)} collective-permute-done((bf16[320,2048]{1,0:T(8,128)(2,1)}, bf16[320,2048]{1,0:T(8,128)(2,1)S(1)}, u32[]{:S(2)}, u32[]{:S(2)}) %collective-permute-start.2) | collective-permute-done | bytes 1310752 | tf_op jit(solution)/shard_map/ppermute | solution.py:503
  145.7 5.8 all-to-all-start.1
  168.2 5.8 project.5
  174.0 6.6 project.6
  180.6 5.8 project.7
  186.4 18.3 %attend.1 = (bf16[8,256,256]{2,1,0:T(8,128)(2,1)S(1)}, f32[2,4,4,256]{3,2,1,0:T(4,128)S(1)}) custom-call(s32[2]{0:T(128)S(1)} %pad_add_fusion.where_ref, bf16[4,2,256,768]{3,2,1,0:T(8,128)(2,1)S(1)} %get-tuple-element.108.qkv_ref), custom_call_target="tpu_custom_call" | custom-call | flops 20000000000 | bytes 6291456 | tf_op jit(solution)/shard_map/attend/pallas_call | solution.py:98
  207.4 30.7 %all_to_all.31 = bf16[8,256,256]{2,1,0:T(8,128)(2,1)} all-to-all(bf16[8,256,256]{2,1,0:T(8,128)(2,1)} %copy-done.12), channel_id=1, replica_groups=mesh['seq'=4,'yx'=4,'core'=2] {'seq','core'}, dimensions={0} | all-to-all | bytes 2097152 | tf_op jit(solution)/shard_map/all_to_all | solution.py:519
  240.6 6.5 multiply_reduce_fusion.1
  249.6 16.7 %collective-permute-done.9.dout_ref = bf16[256,2048]{1,0:T(8,128)(2,1)} collective-permute-done((bf16[256,2048]{1,0:T(8,128)(2,1)}, bf16[256,2048]{1,0:T(8,128)(2,1)}, u32[]{:S(2)}, u32[]{:S(2)}) %collective-permute-start.9) | collective-permute-done | bytes 1048608 | tf_op jit(solution)/shard_map/ppermute | solution.py:503
  269.8 18.9 %collective-permute-done.7.two_ref = bf16[256,2048]{1,0:T(8,128)(2,1)} collective-permute-done((bf16[256,2048]{1,0:T(8,128)(2,1)}, bf16[256,2048]{1,0:T(8,128)(2,1)}, u32[]{:S(2)}, u32[]{:S(2)}) %collective-permute-start.7) | collective-permute-done | bytes 1048608 | tf_op jit(solution)/shard_map/ppermute | solution.py:503
  295.1 23.3 %feed.4 = (bf16[2048,2048]{1,0:T(8,128)(2,1)}, bf16[2048,2048]{1,0:T(8,128)(2,1)}, bf16[2048,1024]{1,0:T(8,128)(2,1)}, bf16[2048,2048]{1,0:T(8,128)(2,1)}, bf16[...) custom-call(bf16[256,2048]{1,0:T(8,128)(2,1)} %collective-permute-done., ...), custom_call_target="tpu_custom_call" | custom-call | flops 1610612736 | bytes 1 | tf_op jit(solution)/shard_map/feed/pallas_call | solution.py:276
  320.5 19.6 %collective-permute-done.13.two_ref = bf16[256,2048]{1,0:T(8,128)(2,1)} collective-permute-done((bf16[256,2048]{1,0:T(8,128)(2,1)}, bf16[256,2048]{1,0:T(8,128)(2,1)}, u32[]{:S(2)}, u32[]{:S(2)}) %collective-permute-start.13) | collective-permute-done | bytes 1048608 | tf_op jit(solution)/shard_map/ppermute | solution.py:503
  341.6 23.4 %feed.5 = (bf16[2048,2048]{1,0:T(8,128)(2,1)}, bf16[2048,2048]{1,0:T(8,128)(2,1)}, bf16[2048,1024]{1,0:T(8,128)(2,1)}, bf16[2048,2048]{1,0:T(8,128)(2,1)}, bf16[...) custom-call(bf16[256,2048]{1,0:T(8,128)(2,1)} %multiply_convert_fusi, ...), custom_call_target="tpu_custom_call", output_to_operand_aliasing={{0}: (8, {}), {1}: (9, {}), {2}: (10, {}), {3}: (11, {})} | custom-call | flops 1610612736 | bytes 1 | tf_op jit(solution)/shard_map/feed/pallas_call | solution.py:276
  368.7 23.3 %feed.6 = (bf16[2048,2048]{1,0:T(8,128)(2,1)}, bf16[2048,2048]{1,0:T(8,128)(2,1)}, bf16[2048,1024]{1,0:T(8,128)(2,1)}, bf16[2048,2048]{1,0:T(8,128)(2,1)}, bf16[...) custom-call(bf16[256,2048]{1,0:T(8,128)(2,1)} %collective-permute-do, ...), custom_call_target="tpu_custom_call", output_to_operand_aliasing={{0}: (8, {}), {1}: (9, {}), {2}: (10, {}), {3}: (11, {})} | custom-call | flops 1610612736 | bytes 1 | tf_op jit(solution)/shard_map/feed/pallas_call | solution.py:276
  392.7 14.8 %collective-permute-done.12 = bf16[256,2048]{1,0:T(8,128)(2,1)} collective-permute-done((bf16[256,2048]{1,0:T(8,128)(2,1)}, bf16[256,2048]{1,0:T(8,128)(2,1)}, u32[]{:S(2)}, u32[]{:S(2)}) %collective-permute-start.12) | collective-permute-done | bytes 1048608 | tf_op jit(solution)/shard_map/ppermute | solution.py:503
  412.2 23.4 %feed.7 = (bf16[2048,2048]{1,0:T(8,128)(2,1)}, bf16[2048,2048]{1,0:T(8,128)(2,1)}, bf16[2048,1024]{1,0:T(8,128)(2,1)}, bf16[2048,2048]{1,0:T(8,128)(2,1)}, bf16[...) custom-call(bf16[256,2048]{1,0:T(8,128)(2,1)} %copy-done.23, ...), custom_call_target="tpu_custom_call", output_to_operand_aliasing={{0}: (8, {}), {1}: (9, {}), {2}: (10, {}), {3}: (11, {})} | custom-call | flops 1610612736 | bytes 1 | tf_op jit(solution)/shard_map/feed/pallas_call | solution.py:276
  440.9 22.2 %convolution_convert_fusion = bf16[2048,2048]{1,0:T(8,128)(2,1)} fusion(bf16[2048,2048]{1,0:T(8,128)(2,1)S(1)} %copy-done.13, bf16[2048,2048]{1,0:T(8,128)(2,1)} %get-tuple-element.142), kind=kOutput, calls=%fused_computation | convolution fusion | flops 17184063488 | bytes 25165824 | tf_op jit(solution)/shard_map/dot_general | solution.py:23
  476.7 7.1 convolution_convert_fusion.12
  500.9 5.9 convolution_convert_fusion.2
  506.8 29.9 %collective-permute-done.31 = bf16[256,2048]{1,0:T(8,128)(2,1)} collective-permute-done((bf16[256,2048]{1,0:T(8,128)(2,1)}, bf16[256,2048]{1,0:T(8,128)(2,1)}, u32[]{:S(2)}, u32[]{:S(2)}) %collective-permute-start.31) | collective-permute-done | bytes 1048608 | tf_op jit(solution)/shard_map/ppermute | solution.py:503
  545.6 25.8 %attend_back.1 = bf16[4,2,256,768]{3,2,1,0:T(8,128)(2,1)} custom-call(s32[2]{0:T(128)S(1)} %pad_add_fusion.where_ref, bf16[4,2,256,768]{3,2,1,0:T(8,128)(2,1)} %copy-done.1, bf16[8,256,256]{2,1,0:T(8,128)(2,1)} %all-to-all-done.3.datt_ref, f32[2,4,4,256]{3,2,1,0:T(4,128)S(1)} %get-tuple-element.153.lse_ref, f32[1024,128]{1,0:T(8,128)S(1)} %copy-done.3, ...), custom_call_target="tpu_custom_call" | custom-call | flops 28000000000 | bytes 12582912 | tf_op jit(solution)/shard_map/attend_back/pallas_call | solution.py:204
  574.3 11.6 %convolution_convert_fusion.3 = bf16[2048,768]{1,0:T(8,128)(2,1)} fusion(bf16[2048,2048]{1,0:T(8,128)(2,1)} %get-tuple-element.161, bf16[2048,768]{1,0:T(8,128)(2,1)} %bitcast.158), kind=kOutput, calls=%fused_computation.3 | convolution fusion | flops 6444023808 | bytes 14680064 | tf_op jit(solution)/shard_map/dot_general | solution.py:23
  598.7 14.3 %convolution_convert_fusion.1 = bf16[1024,2048]{1,0:T(8,128)(2,1)} fusion(bf16[2048,1024]{1,0:T(8,128)(2,1)} %get-tuple-element.182, bf16[2048,2048]{1,0:T(8,128)(2,1)} %get-tuple-element.184), kind=kOutput, calls=%fused_computation.1 | convolution fusion | flops 8592031744 | bytes 16777216 | tf_op jit(solution)/shard_map/dot_general | solution.py:23
  619.6 72.4 %all-to-all-done.5.hat_ref = bf16[8,64,2048]{2,1,0:T(8,128)(2,1)} async-done(((bf16[8,64,2048]{2,1,0:T(8,128)(2,1)}), bf16[8,64,2048]{2,1,0:T(8,128)(2,1)}, u32[]{:S(2)}, u32[]{:S(2)}) %all-to-all-start.5) | async-done | bytes 2097184 | tf_op jit(solution)/shard_map/all_to_all | solution.py:519
  719.4 23.9 %collective-permute-done.40 = bf16[256,2048]{1,0:T(8,128)(2,1)} collective-permute-done((bf16[256,2048]{1,0:T(8,128)(2,1)}, bf16[256,2048]{1,0:T(8,128)(2,1)}, u32[]{:S(2)}, u32[]{:S(2)}) %collective-permute-start.40) | collective-permute-done | bytes 1048608 | tf_op jit(solution)/shard_map/ppermute | solution.py:503
  756.4 6.5 qkv_back.1
  767.8 17.6 %collective-permute-done.45 = bf16[64,2048]{1,0:T(8,128)(2,1)} collective-permute-done((bf16[64,2048]{1,0:T(8,128)(2,1)S(1)}, bf16[64,2048]{1,0:T(8,128)(2,1)}, u32[]{:S(2)}, u32[]{:S(2)}) %collective-permute-start.45) | collective-permute-done | bytes 262176 | tf_op jit(solution)/shard_map/ppermute | solution.py:503
  802.8 7.9 collective-permute-done.47
  (254 shorter events, 196.6 us)
Async XLA Ops:
  7.2 60.0 %all-gather.5.cloned.1.call-start = ((), (), s32[]{:S(2)}) async-start(), calls=%async_computation.10 | async-start | bytes 5242880 | tf_op jit(solution)/shard_map/all_gather | solution.py:541
  7.9 102.7 %all-gather.7.cloned.1.call-start = ((), (), s32[]{:S(2)}) async-start(), calls=%async_computation.11 | async-start | bytes 3932160 | tf_op jit(solution)/shard_map/all_gather | solution.py:525
  10.1 31.6 %collective-permute-start = (bf16[320,2048]{1,0:T(8,128)(2,1)S(1)}, bf16[320,2048]{1,0:T(8,128)(2,1)S(1)}, u32[]{:S(2)}, u32[]{:S(2)}) collective-permute-start(bf16[320,2048]{1,0:T(8,128)(2,1)S(1)} %pad_maximum_fusion.one_ref), channel_id=1, source_target_pairs={{0,8},{8,16},{16,24},{24,0},{1,9},{9,17},{17,25},{25,1},{2,10},{10... | collective-permute-start | bytes 3932168 | tf_op jit(solution)/shard_map/ppermute | solution.py:503
  67.3 173.3 %all-gather.9.cloned.1.call-start = ((), (), s32[]{:S(2)}) async-start(), calls=%async_computation.12 | async-start | bytes 9437184 | tf_op jit(solution)/shard_map/all_gather | solution.py:550
  67.3 31.2 %collective-permute-start.1 = (bf16[320,2048]{1,0:T(8,128)(2,1)S(1)}, bf16[320,2048]{1,0:T(8,128)(2,1)}, u32[]{:S(2)}, u32[]{:S(2)}) collective-permute-start(bf16[320,2048]{1,0:T(8,128)(2,1)S(1)} %collective-permute-done.one_ref), channel_id=1, source_target_pairs={{0,8},{8,16},{16,24},{24,0},{1,9},{9,17},{17,25},{25,1},{2,10},{10... | collective-permute-start | bytes 3932168 | tf_op jit(solution)/shard_map/ppermute | solution.py:503
  110.6 31.7 %collective-permute-start.2 = (bf16[320,2048]{1,0:T(8,128)(2,1)}, bf16[320,2048]{1,0:T(8,128)(2,1)S(1)}, u32[]{:S(2)}, u32[]{:S(2)}) collective-permute-start(bf16[320,2048]{1,0:T(8,128)(2,1)} %collective-permute-done.1.one_ref), channel_id=1, source_target_pairs={{0,8},{8,16},{16,24},{24,0},{1,9},{9,17},{17,25},{25,1},{2,10},{10... | collective-permute-start | bytes 3932168 | tf_op jit(solution)/shard_map/ppermute | solution.py:503
  145.7 61.6 %all-to-all-start.1 = ((bf16[8,64,2048]{2,1,0:T(8,128)(2,1)}), bf16[8,64,2048]{2,1,0:T(8,128)(2,1)}, u32[]{:S(2)}, u32[]{:S(2)}) async-start(bf16[8,64,2048]{2,1,0:T(8,128)(2,1)} %ff_out.1), calls=%async_computation.1 | async-start | bytes 4194304 | tf_op jit(solution)/shard_map/all_to_all | solution.py:519
  151.5 143.6 %all-gather.11.cloned.1.call-start = ((), (), s32[]{:S(2)}) async-start(), calls=%async_computation.13 | async-start | bytes 10485760 | tf_op jit(solution)/shard_map/all_gather | solution.py:525
  207.3 366.9 %reduce-scatter.5.cloned.1.call-start = ((), (), s32[]{:S(2)}) async-start(), calls=%async_computation.14 | async-start | bytes 10485760 | tf_op jit(solution)/shard_map/reduce_scatter | solution.py:529
  249.6 39.2 %collective-permute-start.7 = (bf16[256,2048]{1,0:T(8,128)(2,1)}, bf16[256,2048]{1,0:T(8,128)(2,1)}, u32[]{:S(2)}, u32[]{:S(2)}) collective-permute-start(bf16[256,2048]{1,0:T(8,128)(2,1)} %multiply_convert_fusion.two_ref), channel_id=1, source_target_pairs={{0,8},{8,16},{16,24},{24,0},{1,9},{9,17},{17,25},{25,1},{2,10},{10... | collective-permute-start | bytes 3145736 | tf_op jit(solution)/shard_map/ppermute | solution.py:503
  290.7 49.4 %collective-permute-start.13 = (bf16[256,2048]{1,0:T(8,128)(2,1)}, bf16[256,2048]{1,0:T(8,128)(2,1)}, u32[]{:S(2)}, u32[]{:S(2)}) collective-permute-start(bf16[256,2048]{1,0:T(8,128)(2,1)} %collective-permute-done.7.two_ref), channel_id=1, source_target_pairs={{0,8},{8,16},{16,24},{24,0},{1,9},{9,17},{17,25},{25,1},{2,10},{10... | collective-permute-start | bytes 3145736 | tf_op jit(solution)/shard_map/ppermute | solution.py:503
  290.7 50.5 %collective-permute-start.17 = (bf16[256,2048]{1,0:T(8,128)(2,1)}, bf16[256,2048]{1,0:T(8,128)(2,1)}, u32[]{:S(2)}, u32[]{:S(2)}) collective-permute-start(bf16[256,2048]{1,0:T(8,128)(2,1)} %multiply_convert_fusion.two_ref), channel_id=1, source_target_pairs={{0,1},{1,0},{2,3},{3,2},{4,5},{5,4},{6,7},{7,6},{8,9},{9,8},{10,11... | collective-permute-start | bytes 3145736 | tf_op jit(solution)/shard_map/ppermute | solution.py:506
  318.4 46.6 %collective-permute-start.11 = (bf16[256,2048]{1,0:T(8,128)(2,1)}, bf16[256,2048]{1,0:T(8,128)(2,1)}, u32[]{:S(2)}, u32[]{:S(2)}) collective-permute-start(bf16[256,2048]{1,0:T(8,128)(2,1)} %get-tuple-element.115), channel_id=1, source_target_pairs={{0,1},{1,0},{2,3},{3,2},{4,5},{5,4},{6,7},{7,6},{8,9},{9,8},{10,11... | collective-permute-start | bytes 3145736 | tf_op jit(solution)/shard_map/ppermute | solution.py:506
  319.2 48.6 %collective-permute-start.16 = (bf16[256,2048]{1,0:T(8,128)(2,1)}, bf16[256,2048]{1,0:T(8,128)(2,1)S(1)}, u32[]{:S(2)}, u32[]{:S(2)}) collective-permute-start(bf16[256,2048]{1,0:T(8,128)(2,1)} %collective-permute-done.15.dout_ref), channel_id=1, source_target_pairs={{0,1},{1,0},{2,3},{3,2},{4,5},{5,4},{6,7},{7,6},{8,9},{9,8},{10,11... | collective-permute-start | bytes 3145736 | tf_op jit(solution)/shard_map/ppermute | solution.py:506
  319.2 48.7 %collective-permute-start.24 = (bf16[256,2048]{1,0:T(8,128)(2,1)}, bf16[256,2048]{1,0:T(8,128)(2,1)S(1)}, u32[]{:S(2)}, u32[]{:S(2)}) collective-permute-start(bf16[256,2048]{1,0:T(8,128)(2,1)} %collective-permute-done.15.dout_ref), channel_id=1, source_target_pairs={{0,8},{8,16},{16,24},{24,0},{1,9},{9,17},{17,25},{25,1},{2,10},{10... | collective-permute-start | bytes 3145736 | tf_op jit(solution)/shard_map/ppermute | solution.py:503
  341.2 51.3 %collective-permute-start.22 = (bf16[256,2048]{1,0:T(8,128)(2,1)}, bf16[256,2048]{1,0:T(8,128)(2,1)S(1)}, u32[]{:S(2)}, u32[]{:S(2)}) collective-permute-start(bf16[256,2048]{1,0:T(8,128)(2,1)} %collective-permute-done.13.two_ref), channel_id=1, source_target_pairs={{0,8},{8,16},{16,24},{24,0},{1,9},{9,17},{17,25},{25,1},{2,10},{10... | collective-permute-start | bytes 3145736 | tf_op jit(solution)/shard_map/ppermute | solution.py:503
  367.7 39.7 %collective-permute-start.12 = (bf16[256,2048]{1,0:T(8,128)(2,1)}, bf16[256,2048]{1,0:T(8,128)(2,1)}, u32[]{:S(2)}, u32[]{:S(2)}) collective-permute-start(bf16[256,2048]{1,0:T(8,128)(2,1)} %add_convert_fusion.9), channel_id=1, source_target_pairs={{0,8},{8,16},{16,24},{24,0},{1,9},{9,17},{17,25},{25,1},{2,10},{10... | collective-permute-start | bytes 3145736 | tf_op jit(solution)/shard_map/ppermute | solution.py:503
  367.9 42.9 %collective-permute-start.25 = (bf16[256,2048]{1,0:T(8,128)(2,1)S(1)}, bf16[256,2048]{1,0:T(8,128)(2,1)S(1)}, u32[]{:S(2)}, u32[]{:S(2)}) collective-permute-start(bf16[256,2048]{1,0:T(8,128)(2,1)S(1)} %collective-permute-done.24.dout_ref), channel_id=1, source_target_pairs={{0,1},{1,0},{2,3},{3,2},{4,5},{5,4},{6,7},{7,6},{8,9},{9,8},{10,11... | collective-permute-start | bytes 3145736 | tf_op jit(solution)/shard_map/ppermute | solution.py:506
  470.5 36.4 %collective-permute-start.32 = (bf16[256,2048]{1,0:T(8,128)(2,1)}, bf16[256,2048]{1,0:T(8,128)(2,1)}, u32[]{:S(2)}, u32[]{:S(2)}) collective-permute-start(bf16[256,2048]{1,0:T(8,128)(2,1)} %get-tuple-element.151), channel_id=1, source_target_pairs={{0,1},{1,0},{2,3},{3,2},{4,5},{5,4},{6,7},{7,6},{8,9},{9,8},{10,11... | collective-permute-start | bytes 3145736 | tf_op jit(solution)/shard_map/ppermute | solution.py:506
  488.5 52.9 %all-to-all-start.3 = ((bf16[8,256,256]{2,1,0:T(8,128)(2,1)}), bf16[8,256,256]{2,1,0:T(8,128)(2,1)}, u32[]{:S(2)}, u32[]{:S(2)}) async-start(bf16[8,256,256]{2,1,0:T(8,128)(2,1)} %bitcast.145), calls=%async_computation.3 | async-start | bytes 2097152 | tf_op jit(solution)/shard_map/all_to_all | solution.py:519
  493.0 198.9 %reduce-scatter.7.cloned.1.call-start = ((), (), s32[]{:S(2)}) async-start(), calls=%async_computation.15 | async-start | bytes 3932160 | tf_op jit(solution)/shard_map/reduce_scatter | solution.py:529
  495.9 40.8 %collective-permute-start.31 = (bf16[256,2048]{1,0:T(8,128)(2,1)}, bf16[256,2048]{1,0:T(8,128)(2,1)}, u32[]{:S(2)}, u32[]{:S(2)}) collective-permute-start(bf16[256,2048]{1,0:T(8,128)(2,1)} %add_convert_fusion.6), channel_id=1, source_target_pairs={{0,8},{8,16},{16,24},{24,0},{1,9},{9,17},{17,25},{25,1},{2,10},{10... | collective-permute-start | bytes 3145736 | tf_op jit(solution)/shard_map/ppermute | solution.py:503
  499.4 72.1 %collective-permute-start.34 = (bf16[256,2048]{1,0:T(8,128)(2,1)}, bf16[256,2048]{1,0:T(8,128)(2,1)}, u32[]{:S(2)}, u32[]{:S(2)}) collective-permute-start(bf16[256,2048]{1,0:T(8,128)(2,1)} %get-tuple-element.159), channel_id=1, source_target_pairs={{0,1},{1,0},{2,3},{3,2},{4,5},{5,4},{6,7},{7,6},{8,9},{9,8},{10,11... | collective-permute-start | bytes 3145736 | tf_op jit(solution)/shard_map/ppermute | solution.py:506
  585.9 160.5 %reduce-scatter.9.cloned.1.call-start = ((), (), s32[]{:S(2)}) async-start(), calls=%async_computation.16 | async-start | bytes 5242880 | tf_op jit(solution)/shard_map/reduce_scatter | solution.py:622
  594.1 97.9 %all-to-all-start.5 = ((bf16[8,64,2048]{2,1,0:T(8,128)(2,1)}), bf16[8,64,2048]{2,1,0:T(8,128)(2,1)}, u32[]{:S(2)}, u32[]{:S(2)}) async-start(bf16[8,64,2048]{2,1,0:T(8,128)(2,1)} %bitcast.152), calls=%async_computation.7 | async-start | bytes 4194304 | tf_op jit(solution)/shard_map/all_to_all | solution.py:519
  598.7 166.2 %reduce-scatter.11.cloned.1.call-start = ((), (), s32[]{:S(2)}) async-start(), calls=%async_computation.17 | async-start | bytes 5242880 | tf_op jit(solution)/shard_map/reduce_scatter | solution.py:617
  613.1 84.2 %collective-permute-start.39 = (bf16[256,2048]{1,0:T(8,128)(2,1)}, bf16[256,2048]{1,0:T(8,128)(2,1)}, u32[]{:S(2)}, u32[]{:S(2)}) collective-permute-start(bf16[256,2048]{1,0:T(8,128)(2,1)} %get-tuple-element.169), channel_id=1, source_target_pairs={{0,1},{1,0},{2,3},{3,2},{4,5},{5,4},{6,7},{7,6},{8,9},{9,8},{10,11... | collective-permute-start | bytes 3145736 | tf_op jit(solution)/shard_map/ppermute | solution.py:506
  613.2 84.0 %collective-permute-start.38 = (bf16[256,2048]{1,0:T(8,128)(2,1)}, bf16[256,2048]{1,0:T(8,128)(2,1)}, u32[]{:S(2)}, u32[]{:S(2)}) collective-permute-start(bf16[256,2048]{1,0:T(8,128)(2,1)} %add_convert_fusion.4), channel_id=1, source_target_pairs={{0,8},{8,16},{16,24},{24,0},{1,9},{9,17},{17,25},{25,1},{2,10},{10... | collective-permute-start | bytes 3145736 | tf_op jit(solution)/shard_map/ppermute | solution.py:503
  618.7 87.7 %collective-permute-start.37 = (bf16[256,2048]{1,0:T(8,128)(2,1)}, bf16[256,2048]{1,0:T(8,128)(2,1)}, u32[]{:S(2)}, u32[]{:S(2)}) collective-permute-start(bf16[256,2048]{1,0:T(8,128)(2,1)} %convolution_convert_fusion.8), channel_id=1, source_target_pairs={{0,1},{1,0},{2,3},{3,2},{4,5},{5,4},{6,7},{7,6},{8,9},{9,8},{10,11... | collective-permute-start | bytes 3145736 | tf_op jit(solution)/shard_map/ppermute | solution.py:506
  619.1 87.4 %collective-permute-start.36 = (bf16[256,2048]{1,0:T(8,128)(2,1)}, bf16[256,2048]{1,0:T(8,128)(2,1)}, u32[]{:S(2)}, u32[]{:S(2)}) collective-permute-start(bf16[256,2048]{1,0:T(8,128)(2,1)} %add_convert_fusion.3), channel_id=1, source_target_pairs={{0,8},{8,16},{16,24},{24,0},{1,9},{9,17},{17,25},{25,1},{2,10},{10... | collective-permute-start | bytes 3145736 | tf_op jit(solution)/shard_map/ppermute | solution.py:503
  750.4 36.1 %collective-permute-start.43 = (bf16[256,2048]{1,0:T(8,128)(2,1)}, bf16[256,2048]{1,0:T(8,128)(2,1)}, u32[]{:S(2)}, u32[]{:S(2)}) collective-permute-start(bf16[256,2048]{1,0:T(8,128)(2,1)} %convolution_convert_fusion.4), channel_id=1, source_target_pairs={{0,1},{1,0},{2,3},{3,2},{4,5},{5,4},{6,7},{7,6},{8,9},{9,8},{10,11... | collective-permute-start | bytes 3145736 | tf_op jit(solution)/shard_map/ppermute | solution.py:506
  752.2 34.4 %collective-permute-start.42 = (bf16[256,2048]{1,0:T(8,128)(2,1)}, bf16[256,2048]{1,0:T(8,128)(2,1)}, u32[]{:S(2)}, u32[]{:S(2)}) collective-permute-start(bf16[256,2048]{1,0:T(8,128)(2,1)} %add_convert_fusion), channel_id=1, source_target_pairs={{0,8},{8,16},{16,24},{24,0},{1,9},{9,17},{17,25},{25,1},{2,10},{10... | collective-permute-start | bytes 3145736 | tf_op jit(solution)/shard_map/ppermute | solution.py:503
  (64 other events, 1039.5 us)
Sparse Core Ops, SparseCore 0:
  9.9 53.9 all-gather.4
  67.4 43.1 all-gather.6
  145.8 53.5 all-gather.8
  207.5 87.6 all-gather.10
  468.2 86.6 reduce-scatter.4
  586.0 43.5 reduce-scatter.6
  632.9 52.6 reduce-scatter.8
  688.5 52.6 reduce-scatter.10

commit v4 on v3

--- a/solution.py
+++ b/solution.py
@@ -341,7 +341,7 @@
         ),
         input_output_aliases={6 + i: i for i in range(len(kept))},
         compiler_params=pltpu.CompilerParams(vmem_limit_bytes=40 << 20),
-        cost_estimate=QUICK,
+        cost_estimate=pl.CostEstimate(flops=4 * rows * model * 3 * width, bytes_accessed=12 * rows * model, transcendentals=0),
         name="project",
     )(where, one, other, w, cosine, sine, *kept)
 

time: 831 us -> 823 us (level)
  transfers between devices with their start and end apart: 60 -> 60, of which waited for: 22 -> 23; matrix products, arithmetic and copies ran while one was open for 17% -> 17% of each run, Pallas kernels for 22% -> 22%
where the time goes in v4:
time: 823 us; the launch traced here: 818 us
  waiting for transfers between devices  338 us (41%)
  Pallas kernels  183 us (22%)
  matrix products  88.9 us (11%)
  blocking collectives  56.3 us (7%)
  other arithmetic  53.3 us (6%)
  starting transfers between devices  52.4 us (6%)
  local copies, waits for them, and re-layouts  31.1 us (4%)
  between operations  15.1 us (2%)
    ppermute x21, waiting for transfers between devices, hop(): return lax.ppermute(x, 'seq', ring_pairs)  234 us
    pallas_call x4, Pallas kernels, feed(): pl.pallas_call(functools.partial(feed_kernel, steps), out_shape=[jax.Shap...  93.5 us
    dot_general x14, matrix products, dot(): lax.dot_general(left, right, (dims, ((), ())), preferred_element_type=F32)  88.9 us
    all_to_all x4, waiting for transfers between devices, exchange(): return lax.all_to_all(x, group, 0, 0, tiled=True)  76 us
    all_to_all x2, blocking collectives, exchange(): return lax.all_to_all(x, group, 0, 0, tiled=True)  56.3 us
    pallas_call x1, Pallas kernels, attend_back(): pl.pallas_call(functools.partial(attend_back_kernel, heads, ring), out_sh...  25.9 us
    pallas_call x4, Pallas kernels, project(): pl.pallas_call(project_kernel, out_shape=(jax.ShapeDtypeStruct((blocks *...  24.2 us
    all_to_all x4, starting transfers between devices, exchange(): return lax.all_to_all(x, group, 0, 0, tiled=True)  18.7 us
  transfers between devices with their start and end apart: 60, of which 23 were waited for; matrix products, arithmetic and copies ran while one was open for 17% of the time, Pallas kernels for 22%

profile of v4, /device:TPU:5, one launch (start us, length us, event | category | flops | bytes accessed | tf_op | source)
XLA Modules:
  0.0 818.3 jit_solution(17863675502649804252)
XLA Ops:
  18.3 24.4 %collective-permute-done.one_ref = bf16[320,2048]{1,0:T(8,128)(2,1)S(1)} collective-permute-done((bf16[320,2048]{1,0:T(8,128)(2,1)}, bf16[320,2048]{1,0:T(8,128)(2,1)S(1)}, u32[]{:S(2)}, u32[]{:S(2)}) %collective-permute-start) | collective-permute-done | bytes 1310752 | tf_op jit(solution)/shard_map/ppermute | solution.py:503
  42.8 25.6 %all_to_all.30 = bf16[8,64,768]{2,1,0:T(8,128)(2,1)} all-to-all(bf16[8,64,768]{2,1,0:T(8,128)(2,1)} %qkv_out.1), channel_id=1, replica_groups=mesh['seq'=4,'yx'=4,'core'=2] {'seq','core'}, dimensions={0} | all-to-all | bytes 1572864 | tf_op jit(solution)/shard_map/all_to_all | solution.py:519
  73.3 26.3 %collective-permute-done.1.one_ref = bf16[320,2048]{1,0:T(8,128)(2,1)S(1)} collective-permute-done((bf16[320,2048]{1,0:T(8,128)(2,1)S(1)}, bf16[320,2048]{1,0:T(8,128)(2,1)S(1)}, u32[]{:S(2)}, u32[]{:S(2)}) %collective-permute-start.1) | collective-permute-done | bytes 1310752 | tf_op jit(solution)/shard_map/ppermute | solution.py:503
  99.5 12.2 %all-gather.7.cloned.1.call-done = bf16[4,512,768]{2,1,0:T(8,128)(2,1)} async-done(((bf16[4,128,768]{2,1,0:T(8,128)(2,1)}), bf16[4,512,768]{2,1,0:T(8,128)(2,1)}) %all-gather.7.cloned.1.call-update) | async-done | bytes 3145744 | tf_op jit(solution)/shard_map/all_gather | solution.py:525
  113.0 30.3 %collective-permute-done.2.one_ref = bf16[320,2048]{1,0:T(8,128)(2,1)} collective-permute-done((bf16[320,2048]{1,0:T(8,128)(2,1)S(1)}, bf16[320,2048]{1,0:T(8,128)(2,1)}, u32[]{:S(2)}, u32[]{:S(2)}) %collective-permute-start.2) | collective-permute-done | bytes 1310752 | tf_op jit(solution)/shard_map/ppermute | solution.py:503
  161.9 6.1 project.4
  167.9 5.9 project.5
  173.8 6.1 project.6
  179.9 6.2 project.7
  186.1 18.4 %attend.1 = (bf16[8,256,256]{2,1,0:T(8,128)(2,1)S(1)}, f32[2,4,4,256]{3,2,1,0:T(4,128)S(1)}) custom-call(s32[2]{0:T(128)S(1)} %pad_add_fusion.where_ref, bf16[4,2,256,768]{3,2,1,0:T(8,128)(2,1)S(1)} %get-tuple-element.108.qkv_ref), custom_call_target="tpu_custom_call" | custom-call | flops 20000000000 | bytes 6291456 | tf_op jit(solution)/shard_map/attend/pallas_call | solution.py:98
  207.2 30.7 %all_to_all.31 = bf16[8,256,256]{2,1,0:T(8,128)(2,1)} all-to-all(bf16[8,256,256]{2,1,0:T(8,128)(2,1)} %copy-done.10), channel_id=1, replica_groups=mesh['seq'=4,'yx'=4,'core'=2] {'seq','core'}, dimensions={0} | all-to-all | bytes 2097152 | tf_op jit(solution)/shard_map/all_to_all | solution.py:519
  240.4 6.5 multiply_reduce_fusion.1
  249.4 16.7 %collective-permute-done.9.dout_ref = bf16[256,2048]{1,0:T(8,128)(2,1)} collective-permute-done((bf16[256,2048]{1,0:T(8,128)(2,1)}, bf16[256,2048]{1,0:T(8,128)(2,1)}, u32[]{:S(2)}, u32[]{:S(2)}) %collective-permute-start.9) | collective-permute-done | bytes 1048608 | tf_op jit(solution)/shard_map/ppermute | solution.py:503
  269.6 18.9 %collective-permute-done.7.two_ref = bf16[256,2048]{1,0:T(8,128)(2,1)} collective-permute-done((bf16[256,2048]{1,0:T(8,128)(2,1)}, bf16[256,2048]{1,0:T(8,128)(2,1)}, u32[]{:S(2)}, u32[]{:S(2)}) %collective-permute-start.7) | collective-permute-done | bytes 1048608 | tf_op jit(solution)/shard_map/ppermute | solution.py:503
  294.7 23.3 %feed.4 = (bf16[2048,2048]{1,0:T(8,128)(2,1)}, bf16[2048,2048]{1,0:T(8,128)(2,1)}, bf16[2048,1024]{1,0:T(8,128)(2,1)}, bf16[2048,2048]{1,0:T(8,128)(2,1)}, bf16[...) custom-call(bf16[256,2048]{1,0:T(8,128)(2,1)} %collective-permute-done., ...), custom_call_target="tpu_custom_call" | custom-call | flops 1610612736 | bytes 1 | tf_op jit(solution)/shard_map/feed/pallas_call | solution.py:276
  320.0 19.8 %collective-permute-done.13.two_ref = bf16[256,2048]{1,0:T(8,128)(2,1)} collective-permute-done((bf16[256,2048]{1,0:T(8,128)(2,1)}, bf16[256,2048]{1,0:T(8,128)(2,1)}, u32[]{:S(2)}, u32[]{:S(2)}) %collective-permute-start.13) | collective-permute-done | bytes 1048608 | tf_op jit(solution)/shard_map/ppermute | solution.py:503
  341.4 23.4 %feed.5 = (bf16[2048,2048]{1,0:T(8,128)(2,1)}, bf16[2048,2048]{1,0:T(8,128)(2,1)}, bf16[2048,1024]{1,0:T(8,128)(2,1)}, bf16[2048,2048]{1,0:T(8,128)(2,1)}, bf16[...) custom-call(bf16[256,2048]{1,0:T(8,128)(2,1)} %multiply_convert_fusi, ...), custom_call_target="tpu_custom_call", output_to_operand_aliasing={{0}: (8, {}), {1}: (9, {}), {2}: (10, {}), {3}: (11, {})} | custom-call | flops 1610612736 | bytes 1 | tf_op jit(solution)/shard_map/feed/pallas_call | solution.py:276
  368.5 23.3 %feed.6 = (bf16[2048,2048]{1,0:T(8,128)(2,1)}, bf16[2048,2048]{1,0:T(8,128)(2,1)}, bf16[2048,1024]{1,0:T(8,128)(2,1)}, bf16[2048,2048]{1,0:T(8,128)(2,1)}, bf16[...) custom-call(bf16[256,2048]{1,0:T(8,128)(2,1)} %collective-permute-do, ...), custom_call_target="tpu_custom_call", output_to_operand_aliasing={{0}: (8, {}), {1}: (9, {}), {2}: (10, {}), {3}: (11, {})} | custom-call | flops 1610612736 | bytes 1 | tf_op jit(solution)/shard_map/feed/pallas_call | solution.py:276
  392.5 14.8 %collective-permute-done.12 = bf16[256,2048]{1,0:T(8,128)(2,1)} collective-permute-done((bf16[256,2048]{1,0:T(8,128)(2,1)}, bf16[256,2048]{1,0:T(8,128)(2,1)}, u32[]{:S(2)}, u32[]{:S(2)}) %collective-permute-start.12) | collective-permute-done | bytes 1048608 | tf_op jit(solution)/shard_map/ppermute | solution.py:503
  412.0 23.5 %feed.7 = (bf16[2048,2048]{1,0:T(8,128)(2,1)}, bf16[2048,2048]{1,0:T(8,128)(2,1)}, bf16[2048,1024]{1,0:T(8,128)(2,1)}, bf16[2048,2048]{1,0:T(8,128)(2,1)}, bf16[...) custom-call(bf16[256,2048]{1,0:T(8,128)(2,1)} %copy-done.21, ...), custom_call_target="tpu_custom_call", output_to_operand_aliasing={{0}: (8, {}), {1}: (9, {}), {2}: (10, {}), {3}: (11, {})} | custom-call | flops 1610612736 | bytes 1 | tf_op jit(solution)/shard_map/feed/pallas_call | solution.py:276
  440.7 22.3 %convolution_convert_fusion = bf16[2048,2048]{1,0:T(8,128)(2,1)} fusion(bf16[2048,2048]{1,0:T(8,128)(2,1)S(1)} %copy-done.11, bf16[2048,2048]{1,0:T(8,128)(2,1)} %get-tuple-element.142), kind=kOutput, calls=%fused_computation | convolution fusion | flops 17184063488 | bytes 25165824 | tf_op jit(solution)/shard_map/dot_general | solution.py:23
  476.5 7.1 convolution_convert_fusion.12
  500.7 5.9 convolution_convert_fusion.2
  506.6 29.8 %collective-permute-done.31 = bf16[256,2048]{1,0:T(8,128)(2,1)} collective-permute-done((bf16[256,2048]{1,0:T(8,128)(2,1)}, bf16[256,2048]{1,0:T(8,128)(2,1)}, u32[]{:S(2)}, u32[]{:S(2)}) %collective-permute-start.31) | collective-permute-done | bytes 1048608 | tf_op jit(solution)/shard_map/ppermute | solution.py:503
  545.4 25.9 %attend_back.1 = bf16[4,2,256,768]{3,2,1,0:T(8,128)(2,1)} custom-call(s32[2]{0:T(128)S(1)} %pad_add_fusion.where_ref, bf16[4,2,256,768]{3,2,1,0:T(8,128)(2,1)} %copy-done.1, bf16[8,256,256]{2,1,0:T(8,128)(2,1)} %all-to-all-done.3.datt_ref, f32[2,4,4,256]{3,2,1,0:T(4,128)S(1)} %get-tuple-element.153.lse_ref, f32[1024,128]{1,0:T(8,128)S(1)} %copy-done.3, ...), custom_call_target="tpu_custom_call" | custom-call | flops 28000000000 | bytes 12582912 | tf_op jit(solution)/shard_map/attend_back/pallas_call | solution.py:204
  574.1 11.6 %convolution_convert_fusion.3 = bf16[2048,768]{1,0:T(8,128)(2,1)} fusion(bf16[2048,2048]{1,0:T(8,128)(2,1)} %get-tuple-element.161, bf16[2048,768]{1,0:T(8,128)(2,1)} %bitcast.158), kind=kOutput, calls=%fused_computation.3 | convolution fusion | flops 6444023808 | bytes 14680064 | tf_op jit(solution)/shard_map/dot_general | solution.py:23
  598.5 14.4 %convolution_convert_fusion.1 = bf16[1024,2048]{1,0:T(8,128)(2,1)} fusion(bf16[2048,1024]{1,0:T(8,128)(2,1)} %get-tuple-element.182, bf16[2048,2048]{1,0:T(8,128)(2,1)} %get-tuple-element.184), kind=kOutput, calls=%fused_computation.1 | convolution fusion | flops 8592031744 | bytes 16777216 | tf_op jit(solution)/shard_map/dot_general | solution.py:23
  619.4 72.4 %all-to-all-done.5.hat_ref = bf16[8,64,2048]{2,1,0:T(8,128)(2,1)} async-done(((bf16[8,64,2048]{2,1,0:T(8,128)(2,1)}), bf16[8,64,2048]{2,1,0:T(8,128)(2,1)}, u32[]{:S(2)}, u32[]{:S(2)}) %all-to-all-start.5) | async-done | bytes 2097184 | tf_op jit(solution)/shard_map/all_to_all | solution.py:519
  719.2 23.9 %collective-permute-done.40 = bf16[256,2048]{1,0:T(8,128)(2,1)} collective-permute-done((bf16[256,2048]{1,0:T(8,128)(2,1)}, bf16[256,2048]{1,0:T(8,128)(2,1)}, u32[]{:S(2)}, u32[]{:S(2)}) %collective-permute-start.40) | collective-permute-done | bytes 1048608 | tf_op jit(solution)/shard_map/ppermute | solution.py:503
  756.1 6.5 qkv_back.1
  767.6 17.6 %collective-permute-done.45 = bf16[64,2048]{1,0:T(8,128)(2,1)} collective-permute-done((bf16[64,2048]{1,0:T(8,128)(2,1)S(1)}, bf16[64,2048]{1,0:T(8,128)(2,1)}, u32[]{:S(2)}, u32[]{:S(2)}) %collective-permute-start.45) | collective-permute-done | bytes 262176 | tf_op jit(solution)/shard_map/ppermute | solution.py:503
  802.4 8.0 collective-permute-done.47
  (250 shorter events, 195.5 us)
Async XLA Ops:
  7.2 61.2 %all-gather.5.cloned.1.call-start = ((), (), s32[]{:S(2)}) async-start(), calls=%async_computation.10 | async-start | bytes 5242880 | tf_op jit(solution)/shard_map/all_gather | solution.py:541
  7.9 103.8 %all-gather.7.cloned.1.call-start = ((), (), s32[]{:S(2)}) async-start(), calls=%async_computation.11 | async-start | bytes 3932160 | tf_op jit(solution)/shard_map/all_gather | solution.py:525
  11.0 31.8 %collective-permute-start = (bf16[320,2048]{1,0:T(8,128)(2,1)}, bf16[320,2048]{1,0:T(8,128)(2,1)S(1)}, u32[]{:S(2)}, u32[]{:S(2)}) collective-permute-start(bf16[320,2048]{1,0:T(8,128)(2,1)} %pad_maximum_fusion.one_ref), channel_id=1, source_target_pairs={{0,8},{8,16},{16,24},{24,0},{1,9},{9,17},{17,25},{25,1},{2,10},{10... | collective-permute-start | bytes 3932168 | tf_op jit(solution)/shard_map/ppermute | solution.py:503
  68.4 171.9 %all-gather.9.cloned.1.call-start = ((), (), s32[]{:S(2)}) async-start(), calls=%async_computation.12 | async-start | bytes 9437184 | tf_op jit(solution)/shard_map/all_gather | solution.py:550
  68.5 31.1 %collective-permute-start.1 = (bf16[320,2048]{1,0:T(8,128)(2,1)S(1)}, bf16[320,2048]{1,0:T(8,128)(2,1)S(1)}, u32[]{:S(2)}, u32[]{:S(2)}) collective-permute-start(bf16[320,2048]{1,0:T(8,128)(2,1)S(1)} %collective-permute-done.one_ref), channel_id=1, source_target_pairs={{0,8},{8,16},{16,24},{24,0},{1,9},{9,17},{17,25},{25,1},{2,10},{10... | collective-permute-start | bytes 3932168 | tf_op jit(solution)/shard_map/ppermute | solution.py:503
  111.8 31.5 %collective-permute-start.2 = (bf16[320,2048]{1,0:T(8,128)(2,1)S(1)}, bf16[320,2048]{1,0:T(8,128)(2,1)}, u32[]{:S(2)}, u32[]{:S(2)}) collective-permute-start(bf16[320,2048]{1,0:T(8,128)(2,1)S(1)} %collective-permute-done.1.one_ref), channel_id=1, source_target_pairs={{0,8},{8,16},{16,24},{24,0},{1,9},{9,17},{17,25},{25,1},{2,10},{10... | collective-permute-start | bytes 3932168 | tf_op jit(solution)/shard_map/ppermute | solution.py:503
  148.2 58.9 %all-to-all-start.1 = ((bf16[8,64,2048]{2,1,0:T(8,128)(2,1)}), bf16[8,64,2048]{2,1,0:T(8,128)(2,1)}, u32[]{:S(2)}, u32[]{:S(2)}) async-start(bf16[8,64,2048]{2,1,0:T(8,128)(2,1)} %ff_out.1), calls=%async_computation.1 | async-start | bytes 4194304 | tf_op jit(solution)/shard_map/all_to_all | solution.py:519
  152.5 142.2 %all-gather.11.cloned.1.call-start = ((), (), s32[]{:S(2)}) async-start(), calls=%async_computation.13 | async-start | bytes 10485760 | tf_op jit(solution)/shard_map/all_gather | solution.py:525
  207.1 367.0 %reduce-scatter.5.cloned.1.call-start = ((), (), s32[]{:S(2)}) async-start(), calls=%async_computation.14 | async-start | bytes 10485760 | tf_op jit(solution)/shard_map/reduce_scatter | solution.py:529
  249.4 39.2 %collective-permute-start.7 = (bf16[256,2048]{1,0:T(8,128)(2,1)}, bf16[256,2048]{1,0:T(8,128)(2,1)}, u32[]{:S(2)}, u32[]{:S(2)}) collective-permute-start(bf16[256,2048]{1,0:T(8,128)(2,1)} %multiply_convert_fusion.two_ref), channel_id=1, source_target_pairs={{0,8},{8,16},{16,24},{24,0},{1,9},{9,17},{17,25},{25,1},{2,10},{10... | collective-permute-start | bytes 3145736 | tf_op jit(solution)/shard_map/ppermute | solution.py:503
  290.5 49.4 %collective-permute-start.13 = (bf16[256,2048]{1,0:T(8,128)(2,1)}, bf16[256,2048]{1,0:T(8,128)(2,1)}, u32[]{:S(2)}, u32[]{:S(2)}) collective-permute-start(bf16[256,2048]{1,0:T(8,128)(2,1)} %collective-permute-done.7.two_ref), channel_id=1, source_target_pairs={{0,8},{8,16},{16,24},{24,0},{1,9},{9,17},{17,25},{25,1},{2,10},{10... | collective-permute-start | bytes 3145736 | tf_op jit(solution)/shard_map/ppermute | solution.py:503
  290.5 50.5 %collective-permute-start.17 = (bf16[256,2048]{1,0:T(8,128)(2,1)}, bf16[256,2048]{1,0:T(8,128)(2,1)}, u32[]{:S(2)}, u32[]{:S(2)}) collective-permute-start(bf16[256,2048]{1,0:T(8,128)(2,1)} %multiply_convert_fusion.two_ref), channel_id=1, source_target_pairs={{0,1},{1,0},{2,3},{3,2},{4,5},{5,4},{6,7},{7,6},{8,9},{9,8},{10,11... | collective-permute-start | bytes 3145736 | tf_op jit(solution)/shard_map/ppermute | solution.py:506
  318.0 46.9 %collective-permute-start.11 = (bf16[256,2048]{1,0:T(8,128)(2,1)}, bf16[256,2048]{1,0:T(8,128)(2,1)}, u32[]{:S(2)}, u32[]{:S(2)}) collective-permute-start(bf16[256,2048]{1,0:T(8,128)(2,1)} %get-tuple-element.115), channel_id=1, source_target_pairs={{0,1},{1,0},{2,3},{3,2},{4,5},{5,4},{6,7},{7,6},{8,9},{9,8},{10,11... | collective-permute-start | bytes 3145736 | tf_op jit(solution)/shard_map/ppermute | solution.py:506
  318.7 48.8 %collective-permute-start.16 = (bf16[256,2048]{1,0:T(8,128)(2,1)}, bf16[256,2048]{1,0:T(8,128)(2,1)S(1)}, u32[]{:S(2)}, u32[]{:S(2)}) collective-permute-start(bf16[256,2048]{1,0:T(8,128)(2,1)} %collective-permute-done.15.dout_ref), channel_id=1, source_target_pairs={{0,1},{1,0},{2,3},{3,2},{4,5},{5,4},{6,7},{7,6},{8,9},{9,8},{10,11... | collective-permute-start | bytes 3145736 | tf_op jit(solution)/shard_map/ppermute | solution.py:506
  318.8 48.9 %collective-permute-start.24 = (bf16[256,2048]{1,0:T(8,128)(2,1)}, bf16[256,2048]{1,0:T(8,128)(2,1)S(1)}, u32[]{:S(2)}, u32[]{:S(2)}) collective-permute-start(bf16[256,2048]{1,0:T(8,128)(2,1)} %collective-permute-done.15.dout_ref), channel_id=1, source_target_pairs={{0,8},{8,16},{16,24},{24,0},{1,9},{9,17},{17,25},{25,1},{2,10},{10... | collective-permute-start | bytes 3145736 | tf_op jit(solution)/shard_map/ppermute | solution.py:503
  341.0 51.4 %collective-permute-start.22 = (bf16[256,2048]{1,0:T(8,128)(2,1)}, bf16[256,2048]{1,0:T(8,128)(2,1)S(1)}, u32[]{:S(2)}, u32[]{:S(2)}) collective-permute-start(bf16[256,2048]{1,0:T(8,128)(2,1)} %collective-permute-done.13.two_ref), channel_id=1, source_target_pairs={{0,8},{8,16},{16,24},{24,0},{1,9},{9,17},{17,25},{25,1},{2,10},{10... | collective-permute-start | bytes 3145736 | tf_op jit(solution)/shard_map/ppermute | solution.py:503
  367.6 39.7 %collective-permute-start.12 = (bf16[256,2048]{1,0:T(8,128)(2,1)}, bf16[256,2048]{1,0:T(8,128)(2,1)}, u32[]{:S(2)}, u32[]{:S(2)}) collective-permute-start(bf16[256,2048]{1,0:T(8,128)(2,1)} %add_convert_fusion.9), channel_id=1, source_target_pairs={{0,8},{8,16},{16,24},{24,0},{1,9},{9,17},{17,25},{25,1},{2,10},{10... | collective-permute-start | bytes 3145736 | tf_op jit(solution)/shard_map/ppermute | solution.py:503
  367.8 42.9 %collective-permute-start.25 = (bf16[256,2048]{1,0:T(8,128)(2,1)S(1)}, bf16[256,2048]{1,0:T(8,128)(2,1)S(1)}, u32[]{:S(2)}, u32[]{:S(2)}) collective-permute-start(bf16[256,2048]{1,0:T(8,128)(2,1)S(1)} %collective-permute-done.24.dout_ref), channel_id=1, source_target_pairs={{0,1},{1,0},{2,3},{3,2},{4,5},{5,4},{6,7},{7,6},{8,9},{9,8},{10,11... | collective-permute-start | bytes 3145736 | tf_op jit(solution)/shard_map/ppermute | solution.py:506
  470.2 36.4 %collective-permute-start.32 = (bf16[256,2048]{1,0:T(8,128)(2,1)}, bf16[256,2048]{1,0:T(8,128)(2,1)}, u32[]{:S(2)}, u32[]{:S(2)}) collective-permute-start(bf16[256,2048]{1,0:T(8,128)(2,1)} %get-tuple-element.151), channel_id=1, source_target_pairs={{0,1},{1,0},{2,3},{3,2},{4,5},{5,4},{6,7},{7,6},{8,9},{9,8},{10,11... | collective-permute-start | bytes 3145736 | tf_op jit(solution)/shard_map/ppermute | solution.py:506
  488.2 52.9 %all-to-all-start.3 = ((bf16[8,256,256]{2,1,0:T(8,128)(2,1)}), bf16[8,256,256]{2,1,0:T(8,128)(2,1)}, u32[]{:S(2)}, u32[]{:S(2)}) async-start(bf16[8,256,256]{2,1,0:T(8,128)(2,1)} %bitcast.145), calls=%async_computation.3 | async-start | bytes 2097152 | tf_op jit(solution)/shard_map/all_to_all | solution.py:519
  492.8 199.0 %reduce-scatter.7.cloned.1.call-start = ((), (), s32[]{:S(2)}) async-start(), calls=%async_computation.15 | async-start | bytes 3932160 | tf_op jit(solution)/shard_map/reduce_scatter | solution.py:529
  495.7 40.8 %collective-permute-start.31 = (bf16[256,2048]{1,0:T(8,128)(2,1)}, bf16[256,2048]{1,0:T(8,128)(2,1)}, u32[]{:S(2)}, u32[]{:S(2)}) collective-permute-start(bf16[256,2048]{1,0:T(8,128)(2,1)} %add_convert_fusion.6), channel_id=1, source_target_pairs={{0,8},{8,16},{16,24},{24,0},{1,9},{9,17},{17,25},{25,1},{2,10},{10... | collective-permute-start | bytes 3145736 | tf_op jit(solution)/shard_map/ppermute | solution.py:503
  499.2 72.1 %collective-permute-start.34 = (bf16[256,2048]{1,0:T(8,128)(2,1)}, bf16[256,2048]{1,0:T(8,128)(2,1)}, u32[]{:S(2)}, u32[]{:S(2)}) collective-permute-start(bf16[256,2048]{1,0:T(8,128)(2,1)} %get-tuple-element.159), channel_id=1, source_target_pairs={{0,1},{1,0},{2,3},{3,2},{4,5},{5,4},{6,7},{7,6},{8,9},{9,8},{10,11... | collective-permute-start | bytes 3145736 | tf_op jit(solution)/shard_map/ppermute | solution.py:506
  585.7 160.4 %reduce-scatter.9.cloned.1.call-start = ((), (), s32[]{:S(2)}) async-start(), calls=%async_computation.16 | async-start | bytes 5242880 | tf_op jit(solution)/shard_map/reduce_scatter | solution.py:622
  593.9 97.9 %all-to-all-start.5 = ((bf16[8,64,2048]{2,1,0:T(8,128)(2,1)}), bf16[8,64,2048]{2,1,0:T(8,128)(2,1)}, u32[]{:S(2)}, u32[]{:S(2)}) async-start(bf16[8,64,2048]{2,1,0:T(8,128)(2,1)} %bitcast.152), calls=%async_computation.7 | async-start | bytes 4194304 | tf_op jit(solution)/shard_map/all_to_all | solution.py:519
  598.5 166.2 %reduce-scatter.11.cloned.1.call-start = ((), (), s32[]{:S(2)}) async-start(), calls=%async_computation.17 | async-start | bytes 5242880 | tf_op jit(solution)/shard_map/reduce_scatter | solution.py:617
  612.9 84.1 %collective-permute-start.39 = (bf16[256,2048]{1,0:T(8,128)(2,1)}, bf16[256,2048]{1,0:T(8,128)(2,1)}, u32[]{:S(2)}, u32[]{:S(2)}) collective-permute-start(bf16[256,2048]{1,0:T(8,128)(2,1)} %get-tuple-element.169), channel_id=1, source_target_pairs={{0,1},{1,0},{2,3},{3,2},{4,5},{5,4},{6,7},{7,6},{8,9},{9,8},{10,11... | collective-permute-start | bytes 3145736 | tf_op jit(solution)/shard_map/ppermute | solution.py:506
  613.0 84.0 %collective-permute-start.38 = (bf16[256,2048]{1,0:T(8,128)(2,1)}, bf16[256,2048]{1,0:T(8,128)(2,1)}, u32[]{:S(2)}, u32[]{:S(2)}) collective-permute-start(bf16[256,2048]{1,0:T(8,128)(2,1)} %add_convert_fusion.4), channel_id=1, source_target_pairs={{0,8},{8,16},{16,24},{24,0},{1,9},{9,17},{17,25},{25,1},{2,10},{10... | collective-permute-start | bytes 3145736 | tf_op jit(solution)/shard_map/ppermute | solution.py:503
  618.6 87.6 %collective-permute-start.37 = (bf16[256,2048]{1,0:T(8,128)(2,1)}, bf16[256,2048]{1,0:T(8,128)(2,1)}, u32[]{:S(2)}, u32[]{:S(2)}) collective-permute-start(bf16[256,2048]{1,0:T(8,128)(2,1)} %convolution_convert_fusion.8), channel_id=1, source_target_pairs={{0,1},{1,0},{2,3},{3,2},{4,5},{5,4},{6,7},{7,6},{8,9},{9,8},{10,11... | collective-permute-start | bytes 3145736 | tf_op jit(solution)/shard_map/ppermute | solution.py:506
  619.0 87.3 %collective-permute-start.36 = (bf16[256,2048]{1,0:T(8,128)(2,1)}, bf16[256,2048]{1,0:T(8,128)(2,1)}, u32[]{:S(2)}, u32[]{:S(2)}) collective-permute-start(bf16[256,2048]{1,0:T(8,128)(2,1)} %add_convert_fusion.3), channel_id=1, source_target_pairs={{0,8},{8,16},{16,24},{24,0},{1,9},{9,17},{17,25},{25,1},{2,10},{10... | collective-permute-start | bytes 3145736 | tf_op jit(solution)/shard_map/ppermute | solution.py:503
  750.2 36.1 %collective-permute-start.43 = (bf16[256,2048]{1,0:T(8,128)(2,1)}, bf16[256,2048]{1,0:T(8,128)(2,1)}, u32[]{:S(2)}, u32[]{:S(2)}) collective-permute-start(bf16[256,2048]{1,0:T(8,128)(2,1)} %convolution_convert_fusion.4), channel_id=1, source_target_pairs={{0,1},{1,0},{2,3},{3,2},{4,5},{5,4},{6,7},{7,6},{8,9},{9,8},{10,11... | collective-permute-start | bytes 3145736 | tf_op jit(solution)/shard_map/ppermute | solution.py:506
  752.0 34.3 %collective-permute-start.42 = (bf16[256,2048]{1,0:T(8,128)(2,1)}, bf16[256,2048]{1,0:T(8,128)(2,1)}, u32[]{:S(2)}, u32[]{:S(2)}) collective-permute-start(bf16[256,2048]{1,0:T(8,128)(2,1)} %add_convert_fusion), channel_id=1, source_target_pairs={{0,8},{8,16},{16,24},{24,0},{1,9},{9,17},{17,25},{25,1},{2,10},{10... | collective-permute-start | bytes 3145736 | tf_op jit(solution)/shard_map/ppermute | solution.py:503
  (62 other events, 1022.2 us)
Sparse Core Ops, SparseCore 0:
  9.9 53.8 all-gather.4
  68.5 43.1 all-gather.6
  146.7 53.5 all-gather.8
  207.2 87.3 all-gather.10
  468.0 86.3 reduce-scatter.4
  585.8 43.3 reduce-scatter.6
  632.5 52.6 reduce-scatter.8
  688.2 52.6 reduce-scatter.10
